TPU v7x, 256 devices: a whole 4x4x8 slice. The times are simulated.
256 devices in a mesh: section: 16 (over x_lo, y, core), batch: 16 (over x_hi, z).
Axes of the slice: x: 4 (x_hi: 2, x_lo: 2; x = x_hi * 2 + x_lo), y: 4, z: 8, core: 2. Of those that a mesh axis runs over, the one named last changes fastest.
Arguments:
- states: bfloat16 [32, 32, 64, 1024], P('section', 'batch'), may hold values from -6 to 6
- weights: bfloat16 [32, 64, 576], P('section'), may hold values from -0.25 to 0.25
- guess: float32 [16, 32, 64, 1024], P('section', 'batch'), may hold values from -6 to 6
- loss_cotangent: float32 [32, 64, 1024], P('batch'), may hold values from -6 to 6
Outputs:
- start_cotangents: float32 [16, 32, 64, 1024], P('section', 'batch')
- weight_grads: float32 [32, 36864], P('section', 'batch')
All inputs are finite; a program needn't handle non-finite values.
Results may differ from a plain program's by a relative error of at most 0.0039.
Values may be sent and summed in bfloat16 or wider, within the bound.
No kernel may reach another device: no remote copies, remote signals or barrier semaphores. Data moves between devices by JAX's collectives and lax.ppermute only.
A program may use at most 128 MiB of HBM per device.

v0:
```python
import math

import jax
import jax.numpy as jnp
from jax import lax
from jax.sharding import PartitionSpec as P

STEP = 0.0625


def passed_along(block, axis, distance):
    devices = range(lax.axis_size(axis))
    route = [(i - distance, i) for i in devices if i - distance in devices]
    return lax.ppermute(block, axis, route)


def unfold_taps(values, pixel_side, direction):
    length = values.shape[-1]
    margin = pixel_side + 1
    widths = [(0, 0)] * (values.ndim - 1) + [(margin, margin)]
    padded = jnp.pad(values, widths)
    column_base = jnp.arange(length) % pixel_side
    copies = []
    for row_step in (-1, 0, 1):
        for col_step in (-1, 0, 1):
            delta = direction * (row_step * pixel_side + col_step)
            window = lax.slice_in_dim(
                padded, margin + delta, margin + delta + length, axis=values.ndim - 1
            )
            column = column_base + direction * col_step
            inside = (column >= 0) & (column < pixel_side)
            copies.append(jnp.where(inside, window, jnp.zeros_like(window)))
    return jnp.stack(copies, axis=1)


def back_conv(weight, rounded, pixel_side):
    channels = weight.shape[0]
    kernel = weight.reshape(channels, 9, channels)
    stacked = unfold_taps(rounded, pixel_side, -1)
    return jnp.einsum("okc,bkop->bcp", kernel, stacked, preferred_element_type=jnp.float32)


def advance(cotangent, rounded, layer_state, weight, step_size, pixel_side):
    activ = jnp.tanh(layer_state.astype(jnp.float32))
    return cotangent + step_size * (1.0 - activ * activ) * back_conv(weight, rounded, pixel_side)


def layer_grad(rounded, layer_state, pixel_side):
    activ = jnp.tanh(layer_state.astype(jnp.float32)).astype(jnp.bfloat16)
    stacked = unfold_taps(activ, pixel_side, 1)
    product = jnp.einsum("bop,bkcp->okc", rounded, stacked, preferred_element_type=jnp.float32)
    return (product * STEP).reshape(-1)


def shards(states, weights, guess, loss_cotangent):
    pixel_side = math.isqrt(states.shape[-1])
    sections = lax.axis_size("section")
    position = lax.axis_index("section")
    per_section = states.shape[0]
    initial = guess[0]
    relaxed = initial
    for layer_index in range(per_section - 1, -1, -1):
        relaxed = advance(
            relaxed,
            relaxed.astype(jnp.bfloat16),
            states[layer_index],
            weights[layer_index],
            STEP,
            pixel_side,
        )
    incoming = passed_along(relaxed, "section", -1)
    residual = jnp.where(position == sections - 1, loss_cotangent - initial, incoming - initial)
    coarse_size = per_section * STEP

    def coarse_round(round_index, running):
        carried = advance(
            running, running.astype(jnp.bfloat16), states[0], weights[0], coarse_size, pixel_side
        )
        return passed_along(carried, "section", -1) + residual

    correction = lax.fori_loop(0, sections - 1, coarse_round, residual)
    cotangent = initial + correction
    gradients = []
    for layer_index in range(per_section - 1, -1, -1):
        rounded = cotangent.astype(jnp.bfloat16)
        local_grad = layer_grad(rounded, states[layer_index], pixel_side)
        gradients.append(local_grad)
        cotangent = advance(
            cotangent, rounded, states[layer_index], weights[layer_index], STEP, pixel_side
        )
    stacked = jnp.stack(gradients[::-1], axis=0)
    stacked = lax.psum_scatter(stacked, "batch", scatter_dimension=1, tiled=True)
    return (cotangent[None], stacked)


def solution(mesh):
    placed = (
        P("section", "batch", None, None),
        P("section", None, None),
        P("section", "batch", None, None),
        P("batch", None, None),
    )
    return jax.shard_map(
        shards,
        mesh=mesh,
        in_specs=placed,
        out_specs=(P("section", "batch", None, None), P("section", "batch")),
        check_vma=False,
    )
```

profile of v0, /device:TPU:32, one launch (start us, length us, event | category | flops | bytes accessed | tf_op | source)
XLA Modules:
  0.0 601.8 jit_solution(11786197021129292658)
XLA Ops:
  17.3 1.5 collective-permute-start.1
  18.9 2.1 collective-permute-done.1
  21.2 187.3 %while.12 = (s32[]{:T(128)}, f32[2,64,1024]{2,1,0:T(8,128)S(1)}, bf16[2,2,64,1024]{3,2,1,0:T(8,128)(2,1)S(1)}, bf16[2,64,576]{1,2,0:T(8,128)(2,1)S(1)}, f32[2,64,1024]{2,1,0:T(8,128)S(1)}, /*index=5*/s32[]{:T(128)}) while((s32[]{:T(128)}, f32[2,64,1024]{2,1,0:T(8,128)S(1)}, bf16[2,2,64,1024]{3,2,1,0:T(8,128)(2,1)S(1)}, ...), condition=%wide.region_1.2_spmd, body=%wide.region_0.1_spmd.sunk | while | flops 153383936 | bytes 13340781 | solution.py:81
  23.2 1.3 collective-permute-start
  24.5 8.7 %collective-permute-done = f32[2,64,1024]{2,1,0:T(8,128)S(1)} collective-permute-done((f32[2,64,1024]{2,1,0:T(8,128)S(1)}, f32[2,64,1024]{2,1,0:T(8,128)S(1)}, u32[]{:S(2)}, u32[]{:S(2)}) %collective-permute-start) | collective-permute-done | bytes 524320 | tf_op jit(solution)/shard_map/while/body/eval_jaxpr/ppermute | solution.py:14
  35.2 1.3 collective-permute-start
  36.5 9.2 %collective-permute-done = f32[2,64,1024]{2,1,0:T(8,128)S(1)} collective-permute-done((f32[2,64,1024]{2,1,0:T(8,128)S(1)}, f32[2,64,1024]{2,1,0:T(8,128)S(1)}, u32[]{:S(2)}, u32[]{:S(2)}) %collective-permute-start) | collective-permute-done | bytes 524320 | tf_op jit(solution)/shard_map/while/body/eval_jaxpr/ppermute | solution.py:14
  47.7 1.3 collective-permute-start
  49.0 9.2 %collective-permute-done = f32[2,64,1024]{2,1,0:T(8,128)S(1)} collective-permute-done((f32[2,64,1024]{2,1,0:T(8,128)S(1)}, f32[2,64,1024]{2,1,0:T(8,128)S(1)}, u32[]{:S(2)}, u32[]{:S(2)}) %collective-permute-start) | collective-permute-done | bytes 524320 | tf_op jit(solution)/shard_map/while/body/eval_jaxpr/ppermute | solution.py:14
  60.2 1.3 collective-permute-start
  61.5 9.2 %collective-permute-done = f32[2,64,1024]{2,1,0:T(8,128)S(1)} collective-permute-done((f32[2,64,1024]{2,1,0:T(8,128)S(1)}, f32[2,64,1024]{2,1,0:T(8,128)S(1)}, u32[]{:S(2)}, u32[]{:S(2)}) %collective-permute-start) | collective-permute-done | bytes 524320 | tf_op jit(solution)/shard_map/while/body/eval_jaxpr/ppermute | solution.py:14
  72.7 1.3 collective-permute-start
  74.0 9.2 %collective-permute-done = f32[2,64,1024]{2,1,0:T(8,128)S(1)} collective-permute-done((f32[2,64,1024]{2,1,0:T(8,128)S(1)}, f32[2,64,1024]{2,1,0:T(8,128)S(1)}, u32[]{:S(2)}, u32[]{:S(2)}) %collective-permute-start) | collective-permute-done | bytes 524320 | tf_op jit(solution)/shard_map/while/body/eval_jaxpr/ppermute | solution.py:14
  85.3 1.3 collective-permute-start
  86.6 9.2 %collective-permute-done = f32[2,64,1024]{2,1,0:T(8,128)S(1)} collective-permute-done((f32[2,64,1024]{2,1,0:T(8,128)S(1)}, f32[2,64,1024]{2,1,0:T(8,128)S(1)}, u32[]{:S(2)}, u32[]{:S(2)}) %collective-permute-start) | collective-permute-done | bytes 524320 | tf_op jit(solution)/shard_map/while/body/eval_jaxpr/ppermute | solution.py:14
  99.1 9.2 %collective-permute-done = f32[2,64,1024]{2,1,0:T(8,128)S(1)} collective-permute-done((f32[2,64,1024]{2,1,0:T(8,128)S(1)}, f32[2,64,1024]{2,1,0:T(8,128)S(1)}, u32[]{:S(2)}, u32[]{:S(2)}) %collective-permute-start) | collective-permute-done | bytes 524320 | tf_op jit(solution)/shard_map/while/body/eval_jaxpr/ppermute | solution.py:14
  111.6 9.2 %collective-permute-done = f32[2,64,1024]{2,1,0:T(8,128)S(1)} collective-permute-done((f32[2,64,1024]{2,1,0:T(8,128)S(1)}, f32[2,64,1024]{2,1,0:T(8,128)S(1)}, u32[]{:S(2)}, u32[]{:S(2)}) %collective-permute-start) | collective-permute-done | bytes 524320 | tf_op jit(solution)/shard_map/while/body/eval_jaxpr/ppermute | solution.py:14
  122.8 1.3 collective-permute-start
  124.1 9.2 %collective-permute-done = f32[2,64,1024]{2,1,0:T(8,128)S(1)} collective-permute-done((f32[2,64,1024]{2,1,0:T(8,128)S(1)}, f32[2,64,1024]{2,1,0:T(8,128)S(1)}, u32[]{:S(2)}, u32[]{:S(2)}) %collective-permute-start) | collective-permute-done | bytes 524320 | tf_op jit(solution)/shard_map/while/body/eval_jaxpr/ppermute | solution.py:14
  136.6 9.2 %collective-permute-done = f32[2,64,1024]{2,1,0:T(8,128)S(1)} collective-permute-done((f32[2,64,1024]{2,1,0:T(8,128)S(1)}, f32[2,64,1024]{2,1,0:T(8,128)S(1)}, u32[]{:S(2)}, u32[]{:S(2)}) %collective-permute-start) | collective-permute-done | bytes 524320 | tf_op jit(solution)/shard_map/while/body/eval_jaxpr/ppermute | solution.py:14
  149.2 9.2 %collective-permute-done = f32[2,64,1024]{2,1,0:T(8,128)S(1)} collective-permute-done((f32[2,64,1024]{2,1,0:T(8,128)S(1)}, f32[2,64,1024]{2,1,0:T(8,128)S(1)}, u32[]{:S(2)}, u32[]{:S(2)}) %collective-permute-start) | collective-permute-done | bytes 524320 | tf_op jit(solution)/shard_map/while/body/eval_jaxpr/ppermute | solution.py:14
  161.7 9.2 %collective-permute-done = f32[2,64,1024]{2,1,0:T(8,128)S(1)} collective-permute-done((f32[2,64,1024]{2,1,0:T(8,128)S(1)}, f32[2,64,1024]{2,1,0:T(8,128)S(1)}, u32[]{:S(2)}, u32[]{:S(2)}) %collective-permute-start) | collective-permute-done | bytes 524320 | tf_op jit(solution)/shard_map/while/body/eval_jaxpr/ppermute | solution.py:14
  172.9 1.3 collective-permute-start
  174.2 9.2 %collective-permute-done = f32[2,64,1024]{2,1,0:T(8,128)S(1)} collective-permute-done((f32[2,64,1024]{2,1,0:T(8,128)S(1)}, f32[2,64,1024]{2,1,0:T(8,128)S(1)}, u32[]{:S(2)}, u32[]{:S(2)}) %collective-permute-start) | collective-permute-done | bytes 524320 | tf_op jit(solution)/shard_map/while/body/eval_jaxpr/ppermute | solution.py:14
  186.7 9.2 %collective-permute-done = f32[2,64,1024]{2,1,0:T(8,128)S(1)} collective-permute-done((f32[2,64,1024]{2,1,0:T(8,128)S(1)}, f32[2,64,1024]{2,1,0:T(8,128)S(1)}, u32[]{:S(2)}, u32[]{:S(2)}) %collective-permute-start) | collective-permute-done | bytes 524320 | tf_op jit(solution)/shard_map/while/body/eval_jaxpr/ppermute | solution.py:14
  199.3 9.2 %collective-permute-done = f32[2,64,1024]{2,1,0:T(8,128)S(1)} collective-permute-done((f32[2,64,1024]{2,1,0:T(8,128)S(1)}, f32[2,64,1024]{2,1,0:T(8,128)S(1)}, u32[]{:S(2)}, u32[]{:S(2)}) %collective-permute-start) | collective-permute-done | bytes 524320 | tf_op jit(solution)/shard_map/while/body/eval_jaxpr/ppermute | solution.py:14
  209.4 2.8 fusion.25
  219.3 2.5 fusion.53
  229.5 9.6 %copy.79 = f32[2,36864]{0,1:T(8,128)} copy(f32[2,36864]{1,0:T(2,128)S(1)} %pad_maximum_fusion) | data formatting | bytes 589824
  240.8 3.1 fusion.18
  243.9 348.8 %reduce-scatter.4.cloned.1.call-done = f32[2304,2]{1,0:T(8,128)} async-done(((f32[36864,2]{1,0:T(8,128)}), f32[2304,2]{1,0:T(8,128)}) %reduce-scatter.4.cloned.1.call-update) | async-done | bytes 18448
  592.7 2.2 copy.80
  (339 shorter events, 64.8 us)
Async XLA Ops:
  7.2 585.5 %reduce-scatter.4.cloned.1.call-start = ((), (), s32[]{:S(2)}) async-start(), calls=%async_computation.1 | async-start | bytes 20054016
  8.3 8.3 %copy-start.7 = (bf16[1,64,576]{1,2,0:T(8,128)(2,1)}, bf16[1,64,576]{1,2,0:T(8,128)(2,1)S(1)}, u32[]{:S(2)}) copy-start(bf16[1,64,576]{1,2,0:T(8,128)(2,1)S(1)} %copy.69) | copy-start | bytes 221188
  8.5 5.4 copy-start.5
  9.6 2.3 copy-start.1
  12.0 1.3 copy-start
  14.9 1.4 copy-start.3
  15.7 1.6 copy-start.2
  16.3 2.4 copy-start.9
  16.4 4.6 copy-start.10
  17.3 3.8 collective-permute-start.1
  23.2 10.0 %collective-permute-start = (f32[2,64,1024]{2,1,0:T(8,128)S(1)}, f32[2,64,1024]{2,1,0:T(8,128)S(1)}, u32[]{:S(2)}, u32[]{:S(2)}) collective-permute-start(f32[2,64,1024]{2,1,0:T(8,128)S(1)} %fusion.77), channel_id=1, source_target_pairs={{16,0},{32,16},{48,32},{64,48},{80,64},{96,80},{112,96},{128,112},... | collective-permute-start | bytes 1572872 | tf_op jit(solution)/shard_map/while/body/eval_jaxpr/ppermute | solution.py:14
  35.2 10.5 %collective-permute-start = (f32[2,64,1024]{2,1,0:T(8,128)S(1)}, f32[2,64,1024]{2,1,0:T(8,128)S(1)}, u32[]{:S(2)}, u32[]{:S(2)}) collective-permute-start(f32[2,64,1024]{2,1,0:T(8,128)S(1)} %fusion.77), channel_id=1, source_target_pairs={{16,0},{32,16},{48,32},{64,48},{80,64},{96,80},{112,96},{128,112},... | collective-permute-start | bytes 1572872 | tf_op jit(solution)/shard_map/while/body/eval_jaxpr/ppermute | solution.py:14
  47.7 10.5 %collective-permute-start = (f32[2,64,1024]{2,1,0:T(8,128)S(1)}, f32[2,64,1024]{2,1,0:T(8,128)S(1)}, u32[]{:S(2)}, u32[]{:S(2)}) collective-permute-start(f32[2,64,1024]{2,1,0:T(8,128)S(1)} %fusion.77), channel_id=1, source_target_pairs={{16,0},{32,16},{48,32},{64,48},{80,64},{96,80},{112,96},{128,112},... | collective-permute-start | bytes 1572872 | tf_op jit(solution)/shard_map/while/body/eval_jaxpr/ppermute | solution.py:14
  60.2 10.5 %collective-permute-start = (f32[2,64,1024]{2,1,0:T(8,128)S(1)}, f32[2,64,1024]{2,1,0:T(8,128)S(1)}, u32[]{:S(2)}, u32[]{:S(2)}) collective-permute-start(f32[2,64,1024]{2,1,0:T(8,128)S(1)} %fusion.77), channel_id=1, source_target_pairs={{16,0},{32,16},{48,32},{64,48},{80,64},{96,80},{112,96},{128,112},... | collective-permute-start | bytes 1572872 | tf_op jit(solution)/shard_map/while/body/eval_jaxpr/ppermute | solution.py:14
  72.7 10.5 %collective-permute-start = (f32[2,64,1024]{2,1,0:T(8,128)S(1)}, f32[2,64,1024]{2,1,0:T(8,128)S(1)}, u32[]{:S(2)}, u32[]{:S(2)}) collective-permute-start(f32[2,64,1024]{2,1,0:T(8,128)S(1)} %fusion.77), channel_id=1, source_target_pairs={{16,0},{32,16},{48,32},{64,48},{80,64},{96,80},{112,96},{128,112},... | collective-permute-start | bytes 1572872 | tf_op jit(solution)/shard_map/while/body/eval_jaxpr/ppermute | solution.py:14
  85.3 10.5 %collective-permute-start = (f32[2,64,1024]{2,1,0:T(8,128)S(1)}, f32[2,64,1024]{2,1,0:T(8,128)S(1)}, u32[]{:S(2)}, u32[]{:S(2)}) collective-permute-start(f32[2,64,1024]{2,1,0:T(8,128)S(1)} %fusion.77), channel_id=1, source_target_pairs={{16,0},{32,16},{48,32},{64,48},{80,64},{96,80},{112,96},{128,112},... | collective-permute-start | bytes 1572872 | tf_op jit(solution)/shard_map/while/body/eval_jaxpr/ppermute | solution.py:14
  97.8 10.5 %collective-permute-start = (f32[2,64,1024]{2,1,0:T(8,128)S(1)}, f32[2,64,1024]{2,1,0:T(8,128)S(1)}, u32[]{:S(2)}, u32[]{:S(2)}) collective-permute-start(f32[2,64,1024]{2,1,0:T(8,128)S(1)} %fusion.77), channel_id=1, source_target_pairs={{16,0},{32,16},{48,32},{64,48},{80,64},{96,80},{112,96},{128,112},... | collective-permute-start | bytes 1572872 | tf_op jit(solution)/shard_map/while/body/eval_jaxpr/ppermute | solution.py:14
  110.3 10.5 %collective-permute-start = (f32[2,64,1024]{2,1,0:T(8,128)S(1)}, f32[2,64,1024]{2,1,0:T(8,128)S(1)}, u32[]{:S(2)}, u32[]{:S(2)}) collective-permute-start(f32[2,64,1024]{2,1,0:T(8,128)S(1)} %fusion.77), channel_id=1, source_target_pairs={{16,0},{32,16},{48,32},{64,48},{80,64},{96,80},{112,96},{128,112},... | collective-permute-start | bytes 1572872 | tf_op jit(solution)/shard_map/while/body/eval_jaxpr/ppermute | solution.py:14
  122.8 10.5 %collective-permute-start = (f32[2,64,1024]{2,1,0:T(8,128)S(1)}, f32[2,64,1024]{2,1,0:T(8,128)S(1)}, u32[]{:S(2)}, u32[]{:S(2)}) collective-permute-start(f32[2,64,1024]{2,1,0:T(8,128)S(1)} %fusion.77), channel_id=1, source_target_pairs={{16,0},{32,16},{48,32},{64,48},{80,64},{96,80},{112,96},{128,112},... | collective-permute-start | bytes 1572872 | tf_op jit(solution)/shard_map/while/body/eval_jaxpr/ppermute | solution.py:14
  135.3 10.5 %collective-permute-start = (f32[2,64,1024]{2,1,0:T(8,128)S(1)}, f32[2,64,1024]{2,1,0:T(8,128)S(1)}, u32[]{:S(2)}, u32[]{:S(2)}) collective-permute-start(f32[2,64,1024]{2,1,0:T(8,128)S(1)} %fusion.77), channel_id=1, source_target_pairs={{16,0},{32,16},{48,32},{64,48},{80,64},{96,80},{112,96},{128,112},... | collective-permute-start | bytes 1572872 | tf_op jit(solution)/shard_map/while/body/eval_jaxpr/ppermute | solution.py:14
  147.9 10.5 %collective-permute-start = (f32[2,64,1024]{2,1,0:T(8,128)S(1)}, f32[2,64,1024]{2,1,0:T(8,128)S(1)}, u32[]{:S(2)}, u32[]{:S(2)}) collective-permute-start(f32[2,64,1024]{2,1,0:T(8,128)S(1)} %fusion.77), channel_id=1, source_target_pairs={{16,0},{32,16},{48,32},{64,48},{80,64},{96,80},{112,96},{128,112},... | collective-permute-start | bytes 1572872 | tf_op jit(solution)/shard_map/while/body/eval_jaxpr/ppermute | solution.py:14
  160.4 10.5 %collective-permute-start = (f32[2,64,1024]{2,1,0:T(8,128)S(1)}, f32[2,64,1024]{2,1,0:T(8,128)S(1)}, u32[]{:S(2)}, u32[]{:S(2)}) collective-permute-start(f32[2,64,1024]{2,1,0:T(8,128)S(1)} %fusion.77), channel_id=1, source_target_pairs={{16,0},{32,16},{48,32},{64,48},{80,64},{96,80},{112,96},{128,112},... | collective-permute-start | bytes 1572872 | tf_op jit(solution)/shard_map/while/body/eval_jaxpr/ppermute | solution.py:14
  172.9 10.5 %collective-permute-start = (f32[2,64,1024]{2,1,0:T(8,128)S(1)}, f32[2,64,1024]{2,1,0:T(8,128)S(1)}, u32[]{:S(2)}, u32[]{:S(2)}) collective-permute-start(f32[2,64,1024]{2,1,0:T(8,128)S(1)} %fusion.77), channel_id=1, source_target_pairs={{16,0},{32,16},{48,32},{64,48},{80,64},{96,80},{112,96},{128,112},... | collective-permute-start | bytes 1572872 | tf_op jit(solution)/shard_map/while/body/eval_jaxpr/ppermute | solution.py:14
  185.4 10.5 %collective-permute-start = (f32[2,64,1024]{2,1,0:T(8,128)S(1)}, f32[2,64,1024]{2,1,0:T(8,128)S(1)}, u32[]{:S(2)}, u32[]{:S(2)}) collective-permute-start(f32[2,64,1024]{2,1,0:T(8,128)S(1)} %fusion.77), channel_id=1, source_target_pairs={{16,0},{32,16},{48,32},{64,48},{80,64},{96,80},{112,96},{128,112},... | collective-permute-start | bytes 1572872 | tf_op jit(solution)/shard_map/while/body/eval_jaxpr/ppermute | solution.py:14
  198.0 10.5 %collective-permute-start = (f32[2,64,1024]{2,1,0:T(8,128)S(1)}, f32[2,64,1024]{2,1,0:T(8,128)S(1)}, u32[]{:S(2)}, u32[]{:S(2)}) collective-permute-start(f32[2,64,1024]{2,1,0:T(8,128)S(1)} %fusion.77), channel_id=1, source_target_pairs={{16,0},{32,16},{48,32},{64,48},{80,64},{96,80},{112,96},{128,112},... | collective-permute-start | bytes 1572872 | tf_op jit(solution)/shard_map/while/body/eval_jaxpr/ppermute | solution.py:14
  212.5 6.9 %copy-start.6 = (bf16[1,64,576]{1,2,0:T(8,128)(2,1)S(1)}, bf16[1,64,576]{1,2,0:T(8,128)(2,1)}, u32[]{:S(2)}) copy-start(bf16[1,64,576]{1,2,0:T(8,128)(2,1)} %copy-done.5) | copy-start | bytes 221188
  219.3 3.3 copy-start.4
  239.1 1.7 copy-start.8
Sparse Core Ops, SparseCore 0:
  239.2 353.4 reduce-scatter.3
where the time goes:
time: 605 us; the launch traced here: 602 us
  waiting for transfers between devices  488 us (81%)
  other arithmetic  41.2 us (7%)
  starting transfers between devices  20.9 us (3%)
  matrix products  20.1 us (3%)
  local copies, waits for them, and re-layouts  14.5 us (2%)
  between operations  14.5 us (2%)
    unnamed x2, waiting for transfers between devices  349 us
    ppermute x16, waiting for transfers between devices, passed_along(): return lax.ppermute(block, axis, route)  140 us
    ppermute x16, starting transfers between devices, passed_along(): return lax.ppermute(block, axis, route)  20.9 us
    unnamed x42, other arithmetic  16.9 us
    dot_general x19, matrix products, back_conv(): jnp.einsum('okc,bkop->bcp', kernel, stacked, preferred_element_type=jnp.f...  16.1 us
    while x120, other arithmetic  15.1 us
    unnamed x25, local copies, waits for them, and re-layouts  12.2 us
  transfers between devices with their start and end apart: 17, of which 17 were waited for; matrix products, arithmetic and copies ran while one was open for 1% of the time, Pallas kernels for 0%

commit v1 on v0

v1 whole, which is shorter than its diff:
```python
import functools

import jax
import jax.numpy as jnp
from jax import lax
from jax.experimental import pallas as pl
from jax.experimental.pallas import tpu as pltpu
from jax.sharding import PartitionSpec as P

H = 0.0625
SIDE = 32
C = 64
N = SIDE * SIDE
F32 = jnp.float32
BF16 = jnp.bfloat16
WIDE = 640
VMEM = pltpu.VMEM


def pixel(rows=C):
    return lax.broadcasted_iota(jnp.int32, (rows, N), 1)


def cols3(v):
    column = pixel() & (SIDE - 1)
    ahead = jnp.where(column < SIDE - 1, pltpu.roll(v, N - 1, 1), 0.0)
    behind = jnp.where(column > 0, pltpu.roll(v, 1, 1), 0.0)
    return jnp.concatenate([ahead.astype(BF16), v.astype(BF16), behind.astype(BF16)], axis=0)


def rows3(t):
    p = pixel()
    up = jnp.where(p >= SIDE, pltpu.roll(t, SIDE, 1), 0.0)
    down = jnp.where(p < N - SIDE, pltpu.roll(t, N - SIDE, 1), 0.0)
    return jnp.concatenate([up.astype(BF16), t.astype(BF16), down.astype(BF16)], axis=0)


def taps(w):
    blocks = [
        jnp.concatenate([w[:, (3 * a + b) * C : (3 * a + b + 1) * C] for a in range(3)], axis=1)
        for b in range(3)
    ]
    return jnp.concatenate(blocks, axis=0).astype(F32).T.astype(BF16)


def conv(m, x3):
    y = jnp.dot(m, x3, preferred_element_type=F32)
    p = pixel()
    low = jnp.where(p < N - SIDE, pltpu.roll(y[:C], N - SIDE, 1), 0.0)
    high = jnp.where(p >= SIDE, pltpu.roll(y[2 * C :], SIDE, 1), 0.0)
    return y[C : 2 * C] + low + high


def slope(u, scale):
    t = jnp.tanh(u.astype(F32))
    return scale - scale * (t * t)


def pack_kernel(states, weights, out):
    members = out.shape[0]
    m = taps(weights[0])
    for k in range(members):
        out[k, :, :N] = states[0, k % 2]
    flat = jnp.concatenate([m[a * C : (a + 1) * C] for a in range(3)], axis=1)
    for k in range(members):
        out[k, :, N : N + 9 * C] = flat


def source_kernel(states, weights, guess, loss, out):
    members = out.shape[0]
    m0, m1 = taps(weights[0]), taps(weights[1])
    for i in range(2):
        g = guess[0, i]
        t = slope(states[1, i], H) * conv(m1, cols3(g))
        v = t - g + 2.0 * loss[i]
        p = t + slope(states[0, i], H) * conv(m0, cols3(v))
        p = p.astype(BF16)
        for k in range(i, members, 2):
            out[k] = p


def chain_kernel(where, start, sources, packed, mine, other, last):
    members = sources.shape[0]

    def step(r, e):
        s = members - 1 - r

        @pl.when(s == where[0])
        def _():
            mine[...] = e

        @pl.when(s == where[1])
        def _():
            other[...] = e

        block = packed[s]
        flat = block[:, N : N + 9 * C]
        m = jnp.concatenate([flat[:, a * 3 * C : (a + 1) * 3 * C] for a in range(3)], axis=0)
        d = slope(block[:, :N], 2.0 * H)
        return e + sources[s].astype(F32) + d * conv(m, cols3(e))

    last[...] = lax.fori_loop(0, members, step, start[...])


def finish_kernel(which, states, weights, loss, mine, other, starts, grads):
    parts = grads.shape[0]
    rows = C // parts
    m0, m1 = taps(weights[0]), taps(weights[1])
    own = which[0]
    sums = [None, None]
    for i in range(2):
        e = jnp.where(own == i, mine[...], other[...])
        v = loss[i] + e
        for layer, m in ((1, m1), (0, m0)):
            t = jnp.tanh(states[layer, i].astype(F32))
            x3 = cols3(v)
            g = lax.dot_general(
                x3, rows3(t), (((1,), (1,)), ((), ())), preferred_element_type=F32
            )
            sums[layer] = g if i == 0 else sums[layer] + g
            v = v + (H - H * (t * t)) * conv(m, x3)
        starts[0, i] = v
    for layer in range(2):
        g = sums[layer] * H
        wide = jnp.concatenate(
            [g[b * C : (b + 1) * C, a * C : (a + 1) * C] for a in range(3) for b in range(3)], axis=1
        )
        for d in range(parts):
            grads[d, layer * rows : (layer + 1) * rows, :] = wide[d * rows : (d + 1) * rows]


def total_kernel(parts, out):
    rows = parts.shape[1] // 2
    s = parts[0]
    for d in range(1, parts.shape[0]):
        s = s + parts[d]
    for layer in range(2):
        out[layer : layer + 1, :] = jnp.concatenate(
            [s[layer * rows + r : layer * rows + r + 1] for r in range(rows)], axis=1
        )


def call(kernel, outs, n_scalar, n_in, flops, moved, name):
    smem = pl.BlockSpec(memory_space=pltpu.SMEM)
    vmem = pl.BlockSpec(memory_space=VMEM)
    return pl.pallas_call(
        kernel,
        out_shape=outs,
        in_specs=[smem] * n_scalar + [vmem] * n_in,
        out_specs=jax.tree.map(lambda _: vmem, outs),
        cost_estimate=pl.CostEstimate(flops=flops, bytes_accessed=moved, transcendentals=0),
        compiler_params=pltpu.CompilerParams(vmem_limit_bytes=40 << 20),
        name=name,
    )


def shards(states, weights, guess, loss):
    sections = lax.axis_size("section")
    nb = lax.axis_size("batch")
    members = sections // 2
    at = lax.axis_index("section")
    spot = lax.rem(at, members)
    core = lax.rem(at, 2)
    groups = [list(range(members)), list(range(members, sections))]
    shape = jax.ShapeDtypeStruct

    packed = call(pack_kernel, shape((members, C, N + WIDE), BF16), 0, 2, 10**6, 3 * 10**6, "pack")(states, weights)
    packed = lax.all_to_all(packed, "section", 0, 0, axis_index_groups=groups, tiled=True)
    sources = call(source_kernel, shape((members, C, N), BF16), 0, 4, 6 * 10**8, 3 * 10**6, "source")(
        states, weights, guess, loss
    )
    sources = lax.all_to_all(sources, "section", 0, 0, axis_index_groups=groups, tiled=True)

    image = shape((C, N), F32)
    where = jnp.stack([spot, spot ^ 1]).astype(jnp.int32)
    chain = call(chain_kernel, (image, image, image), 1, 3, 12 * 10**8, 4 * 10**6, "chain")
    zero = jnp.zeros((C, N), F32)
    last = chain(where, zero, sources, packed)[2]
    carried = lax.ppermute(last, "section", [(i, i - members) for i in range(members, sections)])
    mine, other, _ = chain(where, carried, sources, packed)
    other = lax.ppermute(other, "section", [(i, i ^ 1) for i in range(sections)])

    starts, grads = call(
        finish_kernel,
        (shape((1, 2, C, N), F32), shape((nb, 2 * (C // nb), 9 * C), F32)),
        1, 5, 12 * 10**8, 3 * 10**6, "finish",
    )(core.reshape(1).astype(jnp.int32), states, weights, loss, mine, other)
    grads = lax.all_to_all(grads, "batch", 0, 0, tiled=True)
    total = call(total_kernel, shape((2, 9 * C * C // nb), F32), 0, 1, 10**6, 10**6, "total")(grads)
    return starts, total


def solution(mesh):
    placed = (
        P("section", "batch", None, None),
        P("section", None, None),
        P("section", "batch", None, None),
        P("batch", None, None),
    )
    return jax.shard_map(
        shards,
        mesh=mesh,
        in_specs=placed,
        out_specs=(P("section", "batch", None, None), P("section", "batch")),
        check_vma=False,
    )
```

time: 605 us -> 107 us (0.18)
  waiting for transfers between devices: 488 us -> 47.2 us
  other arithmetic: 41.2 us -> 0.08 us
  blocking collectives: 0 us -> 23.9 us
  matrix products: 20.1 us -> 0 us
  Pallas kernels: 0 us -> 18.4 us
  between operations: 14.5 us -> 0.69 us
  starting transfers between devices: 20.9 us -> 9.47 us
  local copies, waits for them, and re-layouts: 14.5 us -> 6.74 us
    unnamed x2 -> x0, waiting for transfers between devices: 349 us -> none
    ppermute x16 -> x2, waiting for transfers between devices: 140 us -> 10.1 us  [the longest x1 8.35 us: shards(): lax.ppermute(last, 'section', [(i, i - members) for i in range(members, s...]
    all_to_all x0 -> x2, waiting for transfers between devices: none -> 37.1 us  [the longest x1 22.8 us: shards(): lax.all_to_all(packed, 'section', 0, 0, axis_index_groups=groups, tiled=T...]
    all_to_all x0 -> x1, blocking collectives: none -> 23.9 us  [shards(): grads = lax.all_to_all(grads, 'batch', 0, 0, tiled=True)]
    dot_general x21 -> x0, matrix products: 20.1 us -> none  [the longest x19 16.1 us: back_conv(): jnp.einsum('okc,bkop->bcp', kernel, stacked, preferred_element_type=jnp.f...]
    ppermute x16 -> x2, starting transfers between devices: 20.9 us -> 1.28 us  [the longest x1 1.28 us: shards(): lax.ppermute(last, 'section', [(i, i - members) for i in range(members, s...]
    pallas_call x0 -> x6, Pallas kernels: none -> 18.4 us  [the longest x1 5.18 us: shards(): mine, other, _ = chain(where, carried, sources, packed)]
    unnamed x42 -> x0, other arithmetic: 16.9 us -> none
  transfers between devices with their start and end apart: 17 -> 4, of which waited for: 17 -> 4; matrix products, arithmetic and copies ran while one was open for 1% -> 0% of each run, Pallas kernels for 0% -> 1%
where the time goes in v1:
time: 107 us
  waiting for transfers between devices  47.2 us (44%)
  blocking collectives  23.9 us (22%)
  Pallas kernels  18.4 us (17%)
  starting transfers between devices  9.47 us (9%)
  local copies, waits for them, and re-layouts  6.74 us (6%)
    all_to_all x1, blocking collectives, shards(): grads = lax.all_to_all(grads, 'batch', 0, 0, tiled=True)  23.9 us
    all_to_all x1, waiting for transfers between devices, shards(): lax.all_to_all(packed, 'section', 0, 0, axis_index_groups=groups, tiled=T...  22.8 us
    all_to_all x1, waiting for transfers between devices, shards(): lax.all_to_all(sources, 'section', 0, 0, axis_index_groups=groups, tiled=...  14.3 us
    ppermute x1, waiting for transfers between devices, shards(): lax.ppermute(last, 'section', [(i, i - members) for i in range(members, s...  8.35 us
    unnamed x18, local copies, waits for them, and re-layouts  6.72 us
    pallas_call x1, Pallas kernels, shards(): mine, other, _ = chain(where, carried, sources, packed)  5.18 us
    pallas_call x1, Pallas kernels, shards(): last = chain(where, zero, sources, packed)[2]  5.15 us
    all_to_all x1, starting transfers between devices, shards(): lax.all_to_all(sources, 'section', 0, 0, axis_index_groups=groups, tiled=...  4.6 us
  transfers between devices with their start and end apart: 4, of which 4 were waited for; matrix products, arithmetic and copies ran while one was open for 0% of the time, Pallas kernels for 1%

profile of v1, /device:TPU:32, one launch (start us, length us, event | category | flops | bytes accessed | tf_op | source)
XLA Modules:
  0.0 106.5 jit_solution(10187246427591572821)
XLA Ops:
  0.6 0.0 copy-start
  0.6 1.0 copy-done
  1.7 0.0 copy-start.2
  1.7 0.9 copy-done.2
  2.6 0.0 copy-start.4
  2.6 1.0 copy-done.4
  3.6 0.0 copy-start.5
  3.6 1.0 copy-done.5
  4.7 2.8 %source.1 = bf16[8,64,1024]{2,1,0:T(8,128)(2,1)} custom-call(bf16[2,2,64,1024]{3,2,1,0:T(8,128)(2,1)S(1)} %copy-done, bf16[2,64,576]{2,1,0:T(8,128)(2,1)S(1)} %copy-done.2, f32[1,2,64,1024]{3,2,1,0:T(8,128)S(1)} %copy-done.4, f32[2,64,1024]{2,1,0:T(8,128)S(1)} %copy-done.5), custom_call_target="tpu_custom_call" | custom-call | flops 600000000 | bytes 3000000 | tf_op jit(solution)/shard_map/source/pallas_call | solution.py:169
  7.5 0.0 copy-start.1
  7.5 0.0 copy-start.3
  7.5 4.6 %all-to-all-start = ((bf16[8,64,1024]{2,1,0:T(8,128)(2,1)}), bf16[8,64,1024]{2,1,0:T(8,128)(2,1)S(1)}, u32[]{:S(2)}, u32[]{:S(2)}) async-start(bf16[8,64,1024]{2,1,0:T(8,128)(2,1)} %source.1), calls=%async_computation | async-start | bytes 2097152 | tf_op jit(solution)/shard_map/all_to_all | solution.py:172
  12.1 0.0 copy-done.1
  12.1 0.0 copy-done.3
  12.1 1.6 %pack.1 = bf16[8,64,1664]{2,1,0:T(8,128)(2,1)} custom-call(bf16[2,2,64,1024]{3,2,1,0:T(8,128)(2,1)S(1)} %copy-done.1, bf16[2,64,576]{2,1,0:T(8,128)(2,1)S(1)} %copy-done.3), custom_call_target="tpu_custom_call" | custom-call | flops 1000000 | bytes 3000000 | tf_op jit(solution)/shard_map/pack/pallas_call | solution.py:167
  13.7 14.3 %all-to-all-done.sources = bf16[8,64,1024]{2,1,0:T(8,128)(2,1)S(1)} async-done(((bf16[8,64,1024]{2,1,0:T(8,128)(2,1)}), bf16[8,64,1024]{2,1,0:T(8,128)(2,1)S(1)}, u32[]{:S(2)}, u32[]{:S(2)}) %all-to-all-start) | async-done | bytes 1048608 | tf_op jit(solution)/shard_map/all_to_all | solution.py:172
  28.1 3.6 %all-to-all-start.1 = ((bf16[8,64,1664]{2,1,0:T(8,128)(2,1)}), bf16[8,64,1664]{2,1,0:T(8,128)(2,1)S(1)}, u32[]{:S(2)}, u32[]{:S(2)}) async-start(bf16[8,64,1664]{2,1,0:T(8,128)(2,1)} %pack.1), calls=%async_computation.1 | async-start | bytes 3407872 | tf_op jit(solution)/shard_map/all_to_all | solution.py:168
  31.7 0.1 pad_add_fusion.where
  31.7 22.8 %all-to-all-done.1.packed = bf16[8,64,1664]{2,1,0:T(8,128)(2,1)S(1)} async-done(((bf16[8,64,1664]{2,1,0:T(8,128)(2,1)}), bf16[8,64,1664]{2,1,0:T(8,128)(2,1)S(1)}, u32[]{:S(2)}, u32[]{:S(2)}) %all-to-all-start.1) | async-done | bytes 1703968 | tf_op jit(solution)/shard_map/all_to_all | solution.py:168
  54.6 5.2 %chain.2 = (f32[64,1024]{1,0:T(8,128)}, f32[64,1024]{1,0:T(8,128)}, f32[64,1024]{1,0:T(8,128)S(1)}) custom-call(s32[2]{0:T(128)S(1)} %pad_add_fusion.where, f32[64,1024]{1,0:T(8,128)S(1)} %broadcast_in_dim.3.start, bf16[8,64,1024]{2,1,0:T(8,128)(2,1)S(1)} %all-to-all-done.sources, bf16[8,64,1664]{2,1,0:T(8,128)(2,1)S(1)} %all-to-all-done.1.packed), custom_call_target="tpu_custom_call" | custom-call | flops 1200000000 | bytes 4000000 | tf_op jit(solution)/shard_map/chain/pallas_call | solution.py:178
  59.7 1.3 %collective-permute-start = (f32[64,1024]{1,0:T(8,128)S(1)}, f32[64,1024]{1,0:T(8,128)S(1)}, u32[]{:S(2)}, u32[]{:S(2)}) collective-permute-start(f32[64,1024]{1,0:T(8,128)S(1)} %get-tuple-element.7), channel_id=1, source_target_pairs={{128,0},{144,16},{160,32},{176,48},{192,64},{208,80},{224,96},{240... | collective-permute-start | bytes 786440 | tf_op jit(solution)/shard_map/ppermute | solution.py:179
  61.0 8.4 %collective-permute-done.start = f32[64,1024]{1,0:T(8,128)S(1)} collective-permute-done((f32[64,1024]{1,0:T(8,128)S(1)}, f32[64,1024]{1,0:T(8,128)S(1)}, u32[]{:S(2)}, u32[]{:S(2)}) %collective-permute-start) | collective-permute-done | bytes 262176 | tf_op jit(solution)/shard_map/ppermute | solution.py:179
  69.3 5.2 %chain.3 = (f32[64,1024]{1,0:T(8,128)S(1)}, f32[64,1024]{1,0:T(8,128)}, f32[64,1024]{1,0:T(8,128)}) custom-call(s32[2]{0:T(128)S(1)} %pad_add_fusion.where, f32[64,1024]{1,0:T(8,128)S(1)} %collective-permute-done.start, bf16[8,64,1024]{2,1,0:T(8,128)(2,1)S(1)} %all-to-all-done.sources, bf16[8,64,1664]{2,1,0:T(8,128)(2,1)S(1)} %all-to-all-done.1.packed), custom_call_target="tpu_custom_call" | custom-call | flops 1200000000 | bytes 4000000 | tf_op jit(solution)/shard_map/chain/pallas_call | solution.py:180
  74.5 0.7 copy-done.7
  75.2 0.0 collective-permute-start.1
  75.2 1.7 %collective-permute-done.1.other = f32[64,1024]{1,0:T(8,128)S(1)} collective-permute-done((f32[64,1024]{1,0:T(8,128)}, f32[64,1024]{1,0:T(8,128)S(1)}, u32[]{:S(2)}, u32[]{:S(2)}) %collective-permute-start.1) | collective-permute-done | bytes 262176 | tf_op jit(solution)/shard_map/ppermute | solution.py:181
  77.0 0.0 copy-start.6
  77.0 1.0 copy-done.6
  78.0 0.9 copy-done.8
  79.0 2.9 %finish.1 = (f32[1,2,64,1024]{3,2,1,0:T(8,128)}, f32[16,8,576]{2,1,0:T(8,128)S(1)}) custom-call(s32[1]{0:T(128)} %bitcast.which, bf16[2,2,64,1024]{3,2,1,0:T(8,128)(2,1)S(1)} %copy-done.1, bf16[2,64,576]{2,1,0:T(8,128)(2,1)S(1)} %copy-done.3, f32[2,64,1024]{2,1,0:T(8,128)S(1)} %copy-done.6, f32[64,1024]{1,0:T(8,128)S(1)} %copy-done.8, ...), custom_call_target="tpu_custom_call" | custom-call | flops 1200000000 | bytes 3000000 | tf_op jit(solution)/shard_map/finish/pallas_call | solution.py:183
  81.9 23.9 %all_to_all.15.parts = f32[16,8,576]{2,1,0:T(8,128)S(1)} all-to-all(f32[16,8,576]{2,1,0:T(8,128)S(1)} %get-tuple-element.11), channel_id=1, replica_groups=mesh['section'=16,'batch'=16] {'batch'}, dimensions={0} | all-to-all | bytes 589824 | tf_op jit(solution)/shard_map/all_to_all | solution.py:188
  105.8 0.7 total.1
  (3 shorter events, 0.0 us)
Async XLA Ops:
  0.6 1.0 copy-start
  1.7 0.9 copy-start.2
  2.6 1.0 copy-start.4
  3.6 1.0 copy-start.5
  7.5 4.6 %copy-start.1 = (bf16[2,2,64,1024]{3,2,1,0:T(8,128)(2,1)S(1)}, bf16[2,2,64,1024]{3,2,1,0:T(8,128)(2,1)}, u32[]{:S(2)}) copy-start(bf16[2,2,64,1024]{3,2,1,0:T(8,128)(2,1)} %states.5) | copy-start | bytes 1572868
  7.5 4.6 %copy-start.3 = (bf16[2,64,576]{2,1,0:T(8,128)(2,1)S(1)}, bf16[2,64,576]{2,1,0:T(8,128)(2,1)}, u32[]{:S(2)}) copy-start(bf16[2,64,576]{2,1,0:T(8,128)(2,1)} %weights.5) | copy-start | bytes 442372
  7.5 20.5 %all-to-all-start = ((bf16[8,64,1024]{2,1,0:T(8,128)(2,1)}), bf16[8,64,1024]{2,1,0:T(8,128)(2,1)S(1)}, u32[]{:S(2)}, u32[]{:S(2)}) async-start(bf16[8,64,1024]{2,1,0:T(8,128)(2,1)} %source.1), calls=%async_computation | async-start | bytes 2097152 | tf_op jit(solution)/shard_map/all_to_all | solution.py:172
  28.1 26.5 %all-to-all-start.1 = ((bf16[8,64,1664]{2,1,0:T(8,128)(2,1)}), bf16[8,64,1664]{2,1,0:T(8,128)(2,1)S(1)}, u32[]{:S(2)}, u32[]{:S(2)}) async-start(bf16[8,64,1664]{2,1,0:T(8,128)(2,1)} %pack.1), calls=%async_computation.1 | async-start | bytes 3407872 | tf_op jit(solution)/shard_map/all_to_all | solution.py:168
  59.7 9.6 %collective-permute-start = (f32[64,1024]{1,0:T(8,128)S(1)}, f32[64,1024]{1,0:T(8,128)S(1)}, u32[]{:S(2)}, u32[]{:S(2)}) collective-permute-start(f32[64,1024]{1,0:T(8,128)S(1)} %get-tuple-element.7), channel_id=1, source_target_pairs={{128,0},{144,16},{160,32},{176,48},{192,64},{208,80},{224,96},{240... | collective-permute-start | bytes 786440 | tf_op jit(solution)/shard_map/ppermute | solution.py:179
  74.5 0.7 copy-start.7
  75.2 1.7 %collective-permute-start.1 = (f32[64,1024]{1,0:T(8,128)}, f32[64,1024]{1,0:T(8,128)S(1)}, u32[]{:S(2)}, u32[]{:S(2)}) collective-permute-start(f32[64,1024]{1,0:T(8,128)} %get-tuple-element.9), channel_id=1, source_target_pairs={{0,16},{16,0},{32,48},{48,32},{64,80},{80,64},{96,112},{112,96},{1... | collective-permute-start | bytes 786440 | tf_op jit(solution)/shard_map/ppermute | solution.py:181
  77.0 1.0 copy-start.6
  78.0 0.9 copy-start.8

commit v2 on v1

v2 whole, which is shorter than its diff:
```python
import functools

import jax
import jax.numpy as jnp
from jax import lax
from jax.experimental import pallas as pl
from jax.experimental.pallas import tpu as pltpu
from jax.sharding import PartitionSpec as P

H = 0.0625
SIDE = 32
C = 64
N = SIDE * SIDE
F32 = jnp.float32
BF16 = jnp.bfloat16
WIDE = 640
WHOLE = 62 << 20
MOST = (63 << 20) + (1 << 18)


def pixel(rows=C):
    return lax.broadcasted_iota(jnp.int32, (rows, N), 1)


def cols3(v):
    column = pixel() & (SIDE - 1)
    ahead = jnp.where(column < SIDE - 1, pltpu.roll(v, N - 1, 1), 0.0)
    behind = jnp.where(column > 0, pltpu.roll(v, 1, 1), 0.0)
    return jnp.concatenate([ahead.astype(BF16), v.astype(BF16), behind.astype(BF16)], axis=0)


def rows3(t):
    p = pixel()
    up = jnp.where(p >= SIDE, pltpu.roll(t, SIDE, 1), 0.0)
    down = jnp.where(p < N - SIDE, pltpu.roll(t, N - SIDE, 1), 0.0)
    return jnp.concatenate([up.astype(BF16), t.astype(BF16), down.astype(BF16)], axis=0)


def taps(w):
    blocks = [
        jnp.concatenate([w[:, (3 * a + b) * C : (3 * a + b + 1) * C] for a in range(3)], axis=1)
        for b in range(3)
    ]
    return jnp.concatenate(blocks, axis=0).astype(F32).T.astype(BF16)


def conv(m, x3):
    y = jnp.dot(m, x3, preferred_element_type=F32)
    p = pixel()
    low = jnp.where(p < N - SIDE, pltpu.roll(y[:C], N - SIDE, 1), 0.0)
    high = jnp.where(p >= SIDE, pltpu.roll(y[2 * C :], SIDE, 1), 0.0)
    return y[C : 2 * C] + low + high


def slope(u, scale):
    t = jnp.tanh(u.astype(F32))
    return scale - scale * (t * t)


def moves(pairs, sems, first=0):
    made = [pltpu.make_async_copy(a, b, sems.at[first + n]) for n, (a, b) in enumerate(pairs)]
    for one in made:
        one.start()
    return made


def settle(made):
    for one in made:
        one.wait()


def source_kernel(states, weights, guess, loss, out, u, w, g, lc, p, flat, sems):
    members = out.shape[0]
    in_w, in_u, in_g, in_lc = moves([(weights, w), (states, u), (guess.at[0], g), (loss, lc)], sems)
    in_w.wait()
    m0, m1 = taps(w[0]), taps(w[1])
    zero = jnp.zeros((C, WIDE - 9 * C), BF16)
    flat[...] = jnp.concatenate([m0[a * C : (a + 1) * C] for a in range(3)] + [zero], axis=1)
    sent = moves([(flat, out.at[k, :, 2 * N :]) for k in range(members)], sems, 4)
    in_u.wait()
    sent += moves([(u.at[0, k % 2], out.at[k, :, :N]) for k in range(members)], sems, 4 + members)
    settle([in_g, in_lc])
    for i in range(2):
        t = slope(u[1, i], H) * conv(m1, cols3(g[i]))
        v = t - g[i] + 2.0 * lc[i]
        p[i] = (t + slope(u[0, i], H) * conv(m0, cols3(v))).astype(BF16)
        sent += moves(
            [(p.at[i], out.at[k, :, N : 2 * N]) for k in range(i, members, 2)],
            sems, 4 + 2 * members + i * (members // 2),
        )
    settle(sent)


def chain_kernel(where, start, packed, mine, other, last):
    members = packed.shape[0]

    def step(r, e):
        s = members - 1 - r

        @pl.when(s == where[0])
        def _():
            mine[...] = e

        @pl.when(s == where[1])
        def _():
            other[...] = e

        block = packed[s]
        flat = block[:, 2 * N : 2 * N + 9 * C]
        m = jnp.concatenate([flat[:, a * 3 * C : (a + 1) * 3 * C] for a in range(3)], axis=0)
        d = slope(block[:, :N], 2.0 * H)
        return e + block[:, N : 2 * N].astype(F32) + d * conv(m, cols3(e))

    last[...] = lax.fori_loop(0, members, step, start[...].astype(F32)).astype(BF16)


def finish_kernel(which, states, weights, loss, mine, other, starts, grads, u, w, lc, e, out, sems):
    parts = grads.shape[0]
    rows = C // parts
    own = which[0]
    in_w, *ins = moves(
        [(weights, w), (loss, lc), (states, u), (mine, e.at[own]), (other, e.at[1 - own])], sems
    )
    in_w.wait()
    m0, m1 = taps(w[0]), taps(w[1])
    settle(ins)
    sums = [None, None]
    sent = []
    for i in range(2):
        v = lc[i] + e[i]
        for layer, m in ((1, m1), (0, m0)):
            t = jnp.tanh(u[layer, i].astype(F32))
            x3 = cols3(v)
            g = lax.dot_general(
                x3, rows3(t), (((1,), (1,)), ((), ())), preferred_element_type=F32
            )
            sums[layer] = g if i == 0 else sums[layer] + g
            v = v + (H - H * (t * t)) * conv(m, x3)
        out[i] = v
        sent += moves([(out.at[i], starts.at[0, i])], sems, 5 + i)
    wides = []
    for layer in range(2):
        g = sums[layer] * H
        wides.append(jnp.concatenate(
            [g[b * C : (b + 1) * C, a * C : (a + 1) * C] for a in range(3) for b in range(3)], axis=1
        ))
    for d in range(parts):
        both = [wide[d * rows : (d + 1) * rows] for wide in wides]
        grads[d] = jnp.concatenate(both, axis=0).astype(grads.dtype)
    settle(sent)


def total_kernel(parts, out):
    rows = parts.shape[1] // 2
    s = parts[0].astype(F32)
    for d in range(1, parts.shape[0]):
        s = s + parts[d].astype(F32)
    for layer in range(2):
        out[layer : layer + 1, :] = jnp.concatenate(
            [s[layer * rows + r : layer * rows + r + 1] for r in range(rows)], axis=1
        )


def call(kernel, outs, where_in, where_out, scratch, n_sems, flops, moved, name, grant=32 << 20):
    spaces = {"s": pltpu.SMEM, "v": pltpu.VMEM, "h": pltpu.HBM}
    specs = lambda text: [pl.BlockSpec(memory_space=spaces[k]) for k in text]
    out_specs = specs(where_out)
    return pl.pallas_call(
        kernel,
        out_shape=outs,
        in_specs=specs(where_in),
        out_specs=tuple(out_specs) if isinstance(outs, tuple) else out_specs[0],
        scratch_shapes=[pltpu.VMEM(*one) for one in scratch]
        + ([pltpu.SemaphoreType.DMA((n_sems,))] if n_sems else []),
        cost_estimate=pl.CostEstimate(flops=flops, bytes_accessed=moved, transcendentals=0),
        compiler_params=pltpu.CompilerParams(vmem_limit_bytes=grant),
        name=name,
    )


def shards(states, weights, guess, loss):
    sections = lax.axis_size("section")
    nb = lax.axis_size("batch")
    members = sections // 2
    at = lax.axis_index("section")
    spot = lax.rem(at, members)
    core = lax.rem(at, 2)
    groups = [list(range(members)), list(range(members, sections))]
    shape = jax.ShapeDtypeStruct

    packed = call(
        source_kernel, shape((members, C, 2 * N + WIDE), BF16), "hhhh", "h",
        [((2, 2, C, N), BF16), ((2, C, 9 * C), BF16), ((2, C, N), F32), ((2, C, N), F32),
         ((2, C, N), BF16), ((C, WIDE), BF16)],
        4 + 3 * members, 6 * 10**8, 6 * 10**6, "source", WHOLE,
    )(states, weights, guess, loss)
    packed = lax.all_to_all(packed, "section", 0, 0, axis_index_groups=groups, tiled=True)

    image = shape((C, N), F32)
    where = jnp.stack([spot, spot ^ 1]).astype(jnp.int32)
    chain = call(
        chain_kernel, (image, image, shape((C, N), BF16)), "svv", "vvv", [], 0, 12 * 10**8, 4 * 10**6, "chain"
    )
    zero = jnp.zeros((C, N), BF16)
    last = chain(where, zero, packed)[2]
    carried = lax.ppermute(last, "section", [(i, i - members) for i in range(members, sections)])
    mine, other, _ = chain(where, carried, packed)
    other = lax.ppermute(other, "section", [(i, i ^ 1) for i in range(sections)])

    starts, grads = call(
        finish_kernel,
        (shape((1, 2, C, N), F32), shape((nb, 2 * (C // nb), 9 * C), BF16)),
        "shhhvv", "hv",
        [((2, 2, C, N), BF16), ((2, C, 9 * C), BF16), ((2, C, N), F32), ((2, C, N), F32), ((2, C, N), F32)],
        7, 12 * 10**8, 3 * 10**6, "finish", MOST,
    )(core.reshape(1).astype(jnp.int32), states, weights, loss, mine, other)
    grads = lax.all_to_all(grads, "batch", 0, 0, tiled=True)
    total = call(total_kernel, shape((2, 9 * C * C // nb), F32), "v", "v", [], 0, 10**6, 10**6, "total")(grads)
    return starts, total


def solution(mesh):
    placed = (
        P("section", "batch", None, None),
        P("section", None, None),
        P("section", "batch", None, None),
        P("batch", None, None),
    )
    return jax.shard_map(
        shards,
        mesh=mesh,
        in_specs=placed,
        out_specs=(P("section", "batch", None, None), P("section", "batch")),
        check_vma=False,
    )
```

time: 107 us -> 91.1 us (0.85)
  waiting for transfers between devices: 47.2 us -> 41.2 us
  local copies, waits for them, and re-layouts: 6.74 us -> 1.42 us
  starting transfers between devices: 9.47 us -> 5.76 us
  blocking collectives: 23.9 us -> 21.4 us
  Pallas kernels: 18.4 us -> 20.2 us
    all_to_all x1 -> x0, waiting for transfers between devices: 14.3 us -> none  [shards(): lax.all_to_all(sources, 'section', 0, 0, axis_index_groups=groups, tiled=...]
    all_to_all x1, waiting for transfers between devices: 22.8 us -> 34.1 us  [shards(): lax.all_to_all(packed, 'section', 0, 0, axis_index_groups=groups, tiled=T...]
    unnamed x18 -> x4, local copies, waits for them, and re-layouts: 6.72 us -> 1.41 us
    all_to_all x1 -> x0, starting transfers between devices: 4.6 us -> none  [shards(): lax.all_to_all(sources, 'section', 0, 0, axis_index_groups=groups, tiled=...]
    ppermute x1, waiting for transfers between devices: 8.35 us -> 5.56 us  [shards(): lax.ppermute(last, 'section', [(i, i - members) for i in range(members, s...]
    pallas_call x1, Pallas kernels: 2.94 us -> 5.46 us  [shards(): call(finish_kernel, (shape((1, 2, C, N), F32), shape((nb, 2 * (C // nb),...]
    all_to_all x1, blocking collectives: 23.9 us -> 21.4 us  [shards(): grads = lax.all_to_all(grads, 'batch', 0, 0, tiled=True)]
    pallas_call x5 -> x4, Pallas kernels: 15.5 us -> 14.7 us  [the longest x1 5.13 us: shards(): mine, other, _ = chain(where, carried, packed)]
  transfers between devices with their start and end apart: 4 -> 3, of which waited for: 4 -> 3; matrix products, arithmetic and copies ran while one was open for 0% -> 0% of each run, Pallas kernels for 1% -> 0%
where the time goes in v2:
time: 91.1 us; the launch traced here: 90.8 us
  waiting for transfers between devices  41.2 us (45%)
  blocking collectives  21.4 us (23%)
  Pallas kernels  20.2 us (22%)
  starting transfers between devices  5.76 us (6%)
  local copies, waits for them, and re-layouts  1.42 us (2%)
    all_to_all x1, waiting for transfers between devices, shards(): lax.all_to_all(packed, 'section', 0, 0, axis_index_groups=groups, tiled=T...  34.1 us
    all_to_all x1, blocking collectives, shards(): grads = lax.all_to_all(grads, 'batch', 0, 0, tiled=True)  21.4 us
    ppermute x1, waiting for transfers between devices, shards(): lax.ppermute(last, 'section', [(i, i - members) for i in range(members, s...  5.56 us
    pallas_call x1, Pallas kernels, shards(): call(finish_kernel, (shape((1, 2, C, N), F32), shape((nb, 2 * (C // nb),...  5.46 us
    pallas_call x1, Pallas kernels, shards(): mine, other, _ = chain(where, carried, packed)  5.13 us
    pallas_call x1, Pallas kernels, shards(): last = chain(where, zero, packed)[2]  4.84 us
    all_to_all x1, starting transfers between devices, shards(): lax.all_to_all(packed, 'section', 0, 0, axis_index_groups=groups, tiled=T...  4.48 us
    pallas_call x1, Pallas kernels, shards(): call(source_kernel, shape((members, C, 2 * N + WIDE), BF16), 'hhhh', 'h',...  4.05 us
  transfers between devices with their start and end apart: 3, of which 3 were waited for; matrix products, arithmetic and copies ran while one was open for 0% of the time, Pallas kernels for 0%

profile of v2, /device:TPU:32, one launch (start us, length us, event | category | flops | bytes accessed | tf_op | source)
XLA Modules:
  0.0 90.8 jit_solution(7685689821264377651)
XLA Ops:
  0.6 4.0 %source.1 = bf16[8,64,2688]{2,1,0:T(8,128)(2,1)} custom-call(bf16[2,2,64,1024]{3,2,1,0:T(8,128)(2,1)} %states.3, bf16[2,64,576]{2,1,0:T(8,128)(2,1)} %weights.3, f32[1,2,64,1024]{3,2,1,0:T(8,128)} %guess.1, f32[2,64,1024]{2,1,0:T(8,128)} %loss.3), custom_call_target="tpu_custom_call" | custom-call | flops 600000000 | bytes 6000000 | tf_op jit(solution)/shard_map/source/pallas_call | solution.py:191
  4.7 4.5 %all-to-all-start = ((bf16[8,64,2688]{2,1,0:T(8,128)(2,1)}), bf16[8,64,2688]{2,1,0:T(8,128)(2,1)S(1)}, u32[]{:S(2)}, u32[]{:S(2)}) async-start(bf16[8,64,2688]{2,1,0:T(8,128)(2,1)} %source.1), calls=%async_computation | async-start | bytes 5505024 | tf_op jit(solution)/shard_map/all_to_all | solution.py:197
  9.2 0.1 pad_add_fusion.where
  9.2 34.1 %all-to-all-done.packed = bf16[8,64,2688]{2,1,0:T(8,128)(2,1)S(1)} async-done(((bf16[8,64,2688]{2,1,0:T(8,128)(2,1)}), bf16[8,64,2688]{2,1,0:T(8,128)(2,1)S(1)}, u32[]{:S(2)}, u32[]{:S(2)}) %all-to-all-start) | async-done | bytes 2752544 | tf_op jit(solution)/shard_map/all_to_all | solution.py:197
  43.4 4.8 %chain.2 = (f32[64,1024]{1,0:T(8,128)}, f32[64,1024]{1,0:T(8,128)}, bf16[64,1024]{1,0:T(8,128)(2,1)S(1)}) custom-call(s32[2]{0:T(128)S(1)} %pad_add_fusion.where, bf16[64,1024]{1,0:T(8,128)(2,1)S(1)} %broadcast_in_dim.3.start, bf16[8,64,2688]{2,1,0:T(8,128)(2,1)S(1)} %all-to-all-done.packed), custom_call_target="tpu_custom_call" | custom-call | flops 1200000000 | bytes 4000000 | tf_op jit(solution)/shard_map/chain/pallas_call | solution.py:205
  48.2 1.3 %collective-permute-start = (bf16[64,1024]{1,0:T(8,128)(2,1)S(1)}, bf16[64,1024]{1,0:T(8,128)(2,1)S(1)}, u32[]{:S(2)}, u32[]{:S(2)}) collective-permute-start(bf16[64,1024]{1,0:T(8,128)(2,1)S(1)} %get-tuple-element.7), channel_id=1, source_target_pairs={{128,0},{144,16},{160,32},{176,48},{192,64},{208,80},{224,96},{240... | collective-permute-start | bytes 393224 | tf_op jit(solution)/shard_map/ppermute | solution.py:206
  49.5 5.6 %collective-permute-done.start = bf16[64,1024]{1,0:T(8,128)(2,1)S(1)} collective-permute-done((bf16[64,1024]{1,0:T(8,128)(2,1)S(1)}, bf16[64,1024]{1,0:T(8,128)(2,1)S(1)}, u32[]{:S(2)}, u32[]{:S(2)}) %collective-permute-start) | collective-permute-done | bytes 131104 | tf_op jit(solution)/shard_map/ppermute | solution.py:206
  55.1 5.1 %chain.3 = (f32[64,1024]{1,0:T(8,128)S(1)}, f32[64,1024]{1,0:T(8,128)S(1)}, bf16[64,1024]{1,0:T(8,128)(2,1)}) custom-call(s32[2]{0:T(128)S(1)} %pad_add_fusion.where, bf16[64,1024]{1,0:T(8,128)(2,1)S(1)} %collective-permute-done.start, bf16[8,64,2688]{2,1,0:T(8,128)(2,1)S(1)} %all-to-all-done.packed), custom_call_target="tpu_custom_call" | custom-call | flops 1200000000 | bytes 4000000 | tf_op jit(solution)/shard_map/chain/pallas_call | solution.py:207
  60.2 0.0 copy-start
  60.2 0.7 copy-done
  60.9 0.0 collective-permute-start.1
  60.9 1.5 %collective-permute-done.1.other = f32[64,1024]{1,0:T(8,128)S(1)} collective-permute-done((f32[64,1024]{1,0:T(8,128)S(1)}, f32[64,1024]{1,0:T(8,128)S(1)}, u32[]{:S(2)}, u32[]{:S(2)}) %collective-permute-start.1) | collective-permute-done | bytes 262176 | tf_op jit(solution)/shard_map/ppermute | solution.py:208
  62.4 0.0 copy-start.1
  62.4 0.7 copy-done.1
  63.1 5.5 %finish.1 = (f32[1,2,64,1024]{3,2,1,0:T(8,128)}, bf16[16,8,576]{2,1,0:T(8,128)(2,1)}) custom-call(s32[1]{0:T(128)} %bitcast.which, bf16[2,2,64,1024]{3,2,1,0:T(8,128)(2,1)} %states.3, bf16[2,64,576]{2,1,0:T(8,128)(2,1)} %weights.3, f32[2,64,1024]{2,1,0:T(8,128)} %loss.3, f32[64,1024]{1,0:T(8,128)} %copy-done, f32[64,1024]{1,0:T(8,128)} %copy-done.1), custom_call_target="tpu_custom_call" | custom-call | flops 1200000000 | bytes 3000000 | tf_op jit(solution)/shard_map/finish/pallas_call | solution.py:210
  68.6 21.4 %all_to_all.10.parts = bf16[16,8,576]{2,1,0:T(8,128)(2,1)S(1)} all-to-all(bf16[16,8,576]{2,1,0:T(8,128)(2,1)} %get-tuple-element.11), channel_id=1, replica_groups=mesh['section'=16,'batch'=16] {'batch'}, dimensions={0} | all-to-all | bytes 294912 | tf_op jit(solution)/shard_map/all_to_all | solution.py:217
  90.0 0.7 total.1
  (1 shorter events, 0.0 us)
Async XLA Ops:
  4.7 38.7 %all-to-all-start = ((bf16[8,64,2688]{2,1,0:T(8,128)(2,1)}), bf16[8,64,2688]{2,1,0:T(8,128)(2,1)S(1)}, u32[]{:S(2)}, u32[]{:S(2)}) async-start(bf16[8,64,2688]{2,1,0:T(8,128)(2,1)} %source.1), calls=%async_computation | async-start | bytes 5505024 | tf_op jit(solution)/shard_map/all_to_all | solution.py:197
  48.2 6.8 %collective-permute-start = (bf16[64,1024]{1,0:T(8,128)(2,1)S(1)}, bf16[64,1024]{1,0:T(8,128)(2,1)S(1)}, u32[]{:S(2)}, u32[]{:S(2)}) collective-permute-start(bf16[64,1024]{1,0:T(8,128)(2,1)S(1)} %get-tuple-element.7), channel_id=1, source_target_pairs={{128,0},{144,16},{160,32},{176,48},{192,64},{208,80},{224,96},{240... | collective-permute-start | bytes 393224 | tf_op jit(solution)/shard_map/ppermute | solution.py:206
  60.2 0.7 copy-start
  60.9 1.5 %collective-permute-start.1 = (f32[64,1024]{1,0:T(8,128)S(1)}, f32[64,1024]{1,0:T(8,128)S(1)}, u32[]{:S(2)}, u32[]{:S(2)}) collective-permute-start(f32[64,1024]{1,0:T(8,128)S(1)} %get-tuple-element.9), channel_id=1, source_target_pairs={{0,16},{16,0},{32,48},{48,32},{64,80},{80,64},{96,112},{112,96},{1... | collective-permute-start | bytes 786440 | tf_op jit(solution)/shard_map/ppermute | solution.py:208
  62.4 0.7 copy-start.1

commit v3 on v2

v3 whole, which is shorter than its diff:
```python
import jax
import jax.numpy as jnp
from jax import lax
from jax.experimental import pallas as pl
from jax.experimental.pallas import tpu as pltpu
from jax.sharding import PartitionSpec as P


H = 0.0625
SIDE = 32
C = 64
N = SIDE * SIDE
LANES = 128
F32 = jnp.float32
BF16 = jnp.bfloat16
WIDE = 640
WHOLE = 62 << 20


def masked(values, keep):
    return jnp.where(keep, values, jnp.zeros_like(values))


def lane(shape):
    return lax.broadcasted_iota(jnp.int32, shape, len(shape) - 1)


def cols3(v):
    v = v.astype(BF16)
    column = lane(v.shape) & (SIDE - 1)
    ahead = masked(pltpu.roll(v, N - 1, 1), column < SIDE - 1)
    behind = masked(pltpu.roll(v, 1, 1), column > 0)
    return jnp.concatenate([ahead, v, behind], axis=0)


def row_up(t):
    t = pltpu.roll(t, SIDE, 1)
    edge = t[:, :LANES]
    return jnp.concatenate([masked(edge, lane(edge.shape) >= SIDE), t[:, LANES:]], axis=1)


def row_down(t):
    t = pltpu.roll(t, N - SIDE, 1)
    edge = t[:, N - LANES :]
    return jnp.concatenate([t[:, : N - LANES], masked(edge, lane(edge.shape) < LANES - SIDE)], axis=1)


def rows3(t):
    t = t.astype(BF16)
    return jnp.concatenate([row_up(t), t, row_down(t)], axis=0)


def taps(w):
    blocks = [
        jnp.concatenate([w[:, (3 * a + b) * C : (3 * a + b + 1) * C] for a in range(3)], axis=1)
        for b in range(3)
    ]
    return jnp.concatenate(blocks, axis=0).astype(F32).T.astype(BF16)


def conv(m, x3):
    y = jnp.dot(m, x3, preferred_element_type=F32)
    low = row_down(y[:C].astype(BF16))
    high = row_up(y[2 * C :].astype(BF16))
    return y[C : 2 * C] + low.astype(F32) + high.astype(F32)


def flatten_taps(m):
    pad = jnp.zeros((C, WIDE - 9 * C), BF16)
    wide = [m[a * C : (a + 1) * C, : 2 * C] for a in range(3)]
    thin = [m[a * C : (a + 1) * C, 2 * C :] for a in range(3)]
    return jnp.concatenate(wide + thin + [pad], axis=1)


def unflatten_taps(flat):
    wide = [flat[:, 2 * C * a : 2 * C * (a + 1)] for a in range(3)]
    thin = [flat[:, (6 + a) * C : (7 + a) * C] for a in range(3)]
    return jnp.concatenate([jnp.concatenate(wide, axis=0), jnp.concatenate(thin, axis=0)], axis=1)


def moves(pairs, sems, first=0):
    made = [pltpu.make_async_copy(a, b, sems.at[first + n]) for n, (a, b) in enumerate(pairs)]
    for one in made:
        one.start()
    return made


def settle(made):
    for one in made:
        one.wait()


def source_kernel(states, weights, guess, loss, out, u, w, g, lc, send, flat, sems):
    members = out.shape[0]
    in_w, in_u, in_g, in_lc = moves([(weights, w), (states, u), (guess.at[0], g), (loss, lc)], sems)
    in_w.wait()
    m1, m0 = taps(w[1]), taps(w[0])
    flat[...] = flatten_taps(m0)
    sent = moves([(flat, out.at[k, :, 2 * N :]) for k in range(members)], sems, 4)
    settle([in_u, in_g, in_lc])
    for i in range(2):
        t1 = jnp.tanh(u[1, i].astype(F32))
        t0 = jnp.tanh(u[0, i].astype(F32))
        d0 = H - H * (t0 * t0)
        send[i, :, :N] = (2.0 * d0).astype(BF16)
        t = (H - H * (t1 * t1)) * conv(m1, cols3(g[i]))
        send[i, :, N:] = (t + d0 * conv(m0, cols3(t - g[i] + 2.0 * lc[i]))).astype(BF16)
        sent += moves(
            [(send.at[i], out.at[k, :, : 2 * N]) for k in range(i, members, 2)],
            sems, 4 + members + i * (members // 2),
        )
    settle(sent)


def prep_kernel(which, states, weights, loss, ms, acts, slopes, base):
    base[...] = loss[which[0]]
    for layer in range(2):
        ms[layer] = taps(weights[layer])
        for i in range(2):
            t = jnp.tanh(states[layer, i].astype(F32))
            acts[layer, i] = rows3(t)
            slopes[layer, i] = H - H * (t * t)


def chain_kernel(where, start, packed, base, mine, other, last):
    members = packed.shape[0]

    def step(r, e):
        s = members - 1 - r

        @pl.when(s == where[0])
        def _():
            mine[...] = e + base[...]

        @pl.when(s == where[1])
        def _():
            other[...] = e + base[...]

        m = unflatten_taps(packed[s, :, 2 * N :])
        y = conv(m, cols3(e))
        return e + packed[s, :, N : 2 * N].astype(F32) + packed[s, :, :N].astype(F32) * y

    last[...] = lax.fori_loop(0, members, step, start[...].astype(F32)).astype(BF16)


def finish_kernel(which, ms, acts, slopes, mine, other, grads, x3s, lams):
    parts = grads.shape[0]
    rows = C // parts
    own = which[0]
    sums = [None, None]
    for i in range(2):
        v = jnp.where(own == i, mine[...], other[...])
        for layer in (1, 0):
            x3 = cols3(v)
            g = lax.dot_general(
                x3, acts[layer, i], (((1,), (1,)), ((), ())), preferred_element_type=F32
            )
            sums[layer] = g if i == 0 else sums[layer] + g
            if layer:
                v = v + slopes[layer, i] * conv(ms[layer], x3)
        x3s[i] = x3
        lams[i] = v
    wides = []
    for layer in range(2):
        g = sums[layer] * H
        wides.append(jnp.concatenate(
            [g[b * C : (b + 1) * C, a * C : (a + 1) * C] for a in range(3) for b in range(3)], axis=1
        ))
    for d in range(parts):
        both = [wide[d * rows : (d + 1) * rows] for wide in wides]
        grads[d] = jnp.concatenate(both, axis=0).astype(grads.dtype)


def start_kernel(ms, slopes, x3s, lams, starts):
    for i in range(2):
        starts[0, i] = lams[i] + slopes[0, i] * conv(ms[0], x3s[i])


def total_kernel(parts, out):
    rows = parts.shape[1] // 2
    s = parts[0].astype(F32)
    for d in range(1, parts.shape[0]):
        s = s + parts[d].astype(F32)
    for layer in range(2):
        out[layer : layer + 1, :] = jnp.concatenate(
            [s[layer * rows + r : layer * rows + r + 1] for r in range(rows)], axis=1
        )


def call(kernel, outs, where_in, where_out, scratch, n_sems, flops, moved, grant=16 << 20):
    spaces = {"s": pltpu.SMEM, "v": pltpu.VMEM, "h": pltpu.HBM}
    specs = lambda text: [pl.BlockSpec(memory_space=spaces[k]) for k in text]
    out_specs = specs(where_out)
    return pl.pallas_call(
        kernel,
        out_shape=outs,
        in_specs=specs(where_in),
        out_specs=tuple(out_specs) if isinstance(outs, tuple) else out_specs[0],
        scratch_shapes=[pltpu.VMEM(*one) for one in scratch]
        + ([pltpu.SemaphoreType.DMA((n_sems,))] if n_sems else []),
        cost_estimate=pl.CostEstimate(flops=flops, bytes_accessed=moved, transcendentals=0),
        compiler_params=pltpu.CompilerParams(vmem_limit_bytes=grant),
    )


def shards(states, weights, guess, loss):
    sections = lax.axis_size("section")
    nb = lax.axis_size("batch")
    members = sections // 2
    at = lax.axis_index("section")
    spot = lax.rem(at, members)
    core = lax.rem(at, 2)
    groups = [list(range(members)), list(range(members, sections))]
    shape = jax.ShapeDtypeStruct
    image = shape((C, N), F32)
    which = core.reshape(1).astype(jnp.int32)

    source = call(
        source_kernel, shape((members, C, 2 * N + WIDE), BF16), "hhhh", "h",
        [((2, 2, C, N), BF16), ((2, C, 9 * C), BF16), ((2, C, N), F32), ((2, C, N), F32),
         ((2, C, 2 * N), BF16), ((C, WIDE), BF16)],
        4 + 2 * members, 6 * 10**8, 6 * 10**6, WHOLE,
    )(states, weights, guess, loss)
    packed = lax.all_to_all(source, "section", 0, 0, axis_index_groups=groups, tiled=True)
    ms, acts, slopes, base = call(
        prep_kernel,
        (shape((2, 3 * C, 3 * C), BF16), shape((2, 2, 3 * C, N), BF16), shape((2, 2, C, N), F32), image),
        "svvv", "vvvv", [], 0, 10**8, 4 * 10**6,
    )(which, states, weights, loss)

    where = jnp.stack([spot, spot ^ 1]).astype(jnp.int32)
    chain = call(chain_kernel, (image, image, shape((C, N), BF16)), "svvv", "vvv", [], 0, 12 * 10**8, 4 * 10**6)
    zero = jnp.zeros((C, N), BF16)
    last = chain(where, zero, packed, base)[2]
    carried = lax.ppermute(last, "section", [(i, i - members) for i in range(members, sections)])
    mine, other, _ = chain(where, carried, packed, base)
    other = lax.ppermute(other, "section", [(i, i ^ 1) for i in range(sections)])

    grads, x3s, lams = call(
        finish_kernel,
        (shape((nb, 2 * (C // nb), 9 * C), BF16), shape((2, 3 * C, N), BF16), shape((2, C, N), F32)),
        "svvvvv", "vvv", [], 0, 12 * 10**8, 3 * 10**6,
    )(which, ms, acts, slopes, mine, other)
    grads = lax.all_to_all(grads, "batch", 0, 0, tiled=True)
    starts = call(start_kernel, shape((1, 2, C, N), F32), "vvvv", "v", [], 0, 3 * 10**8, 3 * 10**6)(
        ms, slopes, x3s, lams
    )
    total = call(total_kernel, shape((2, 9 * C * C // nb), F32), "v", "v", [], 0, 10**6, 10**6)(grads)
    return starts, total


def solution(mesh):
    placed = (
        P("section", "batch", None, None),
        P("section", None, None),
        P("section", "batch", None, None),
        P("batch", None, None),
    )
    return jax.shard_map(
        shards,
        mesh=mesh,
        in_specs=placed,
        out_specs=(P("section", "batch", None, None), P("section", "batch")),
        check_vma=False,
    )
```

time: 91.1 us -> 87.5 us (0.960)
  blocking collectives: 21.4 us -> 0 us
  starting transfers between devices: 5.76 us -> 17.2 us
  local copies, waits for them, and re-layouts: 1.42 us -> 5.54 us
  waiting for transfers between devices: 41.2 us -> 45.2 us
  Pallas kernels: 20.2 us -> 18.4 us
    all_to_all x1 -> x0, blocking collectives: 21.4 us -> none  [shards(): grads = lax.all_to_all(grads, 'batch', 0, 0, tiled=True)]
    all_to_all x1 -> x2, starting transfers between devices: 4.48 us -> 15.7 us  [the longest x1 11 us: shards(): grads = lax.all_to_all(grads, 'batch', 0, 0, tiled=True)]
    unnamed x4 -> x24, local copies, waits for them, and re-layouts: 1.41 us -> 5.53 us
    all_to_all x1 -> x2, waiting for transfers between devices: 34.1 us -> 38.1 us  [the longest x1 28.9 us: shards(): lax.all_to_all(source, 'section', 0, 0, axis_index_groups=groups, tiled=T...]
    pallas_call x3 -> x5, Pallas kernels: 15.4 us -> 13.5 us  [the longest x1 4.98 us: shards(): mine, other, _ = chain(where, carried, packed, base)]
  transfers between devices with their start and end apart: 3 -> 4, of which waited for: 3 -> 4; matrix products, arithmetic and copies ran while one was open for 0% -> 0% of each run, Pallas kernels for 0% -> 2%
where the time goes in v3:
time: 87.5 us; the launch traced here: 87.1 us
  waiting for transfers between devices  45.2 us (52%)
  Pallas kernels  18.4 us (21%)
  starting transfers between devices  17.2 us (20%)
  local copies, waits for them, and re-layouts  5.54 us (6%)
    all_to_all x1, waiting for transfers between devices, shards(): lax.all_to_all(source, 'section', 0, 0, axis_index_groups=groups, tiled=T...  28.9 us
    all_to_all x1, starting transfers between devices, shards(): grads = lax.all_to_all(grads, 'batch', 0, 0, tiled=True)  11 us
    all_to_all x1, waiting for transfers between devices, shards(): grads = lax.all_to_all(grads, 'batch', 0, 0, tiled=True)  9.14 us
    ppermute x1, waiting for transfers between devices, shards(): lax.ppermute(last, 'section', [(i, i - members) for i in range(members, s...  5.58 us
    unnamed x24, local copies, waits for them, and re-layouts  5.53 us
    pallas_call x1, Pallas kernels, shards(): mine, other, _ = chain(where, carried, packed, base)  4.98 us
    pallas_call x1, Pallas kernels, shards(): last = chain(where, zero, packed, base)[2]  4.71 us
    all_to_all x1, starting transfers between devices, shards(): lax.all_to_all(source, 'section', 0, 0, axis_index_groups=groups, tiled=T...  4.62 us
  transfers between devices with their start and end apart: 4, of which 4 were waited for; matrix products, arithmetic and copies ran while one was open for 0% of the time, Pallas kernels for 2%

profile of v3, /device:TPU:32, one launch (start us, length us, event | category | flops | bytes accessed | tf_op | source)
XLA Modules:
  0.0 87.1 jit_solution(1343288625605197690)
XLA Ops:
  0.6 4.1 %shard_map.60 = bf16[8,64,2688]{2,1,0:T(8,128)(2,1)} custom-call(bf16[2,2,64,1024]{3,2,1,0:T(8,128)(2,1)} %states.3, bf16[2,64,576]{2,1,0:T(8,128)(2,1)} %weights.3, f32[1,2,64,1024]{3,2,1,0:T(8,128)} %guess.1, f32[2,64,1024]{2,1,0:T(8,128)} %loss.3), custom_call_target="tpu_custom_call" | custom-call | flops 600000000 | bytes 6000000 | tf_op jit(solution)/shard_map/pallas_call | solution.py:218
  4.8 0.0 copy-start
  4.8 0.0 copy-start.5
  4.8 4.6 %all-to-all-start = ((bf16[8,64,2688]{2,1,0:T(8,128)(2,1)}), bf16[8,64,2688]{2,1,0:T(8,128)(2,1)S(1)}, u32[]{:S(2)}, u32[]{:S(2)}) async-start(bf16[8,64,2688]{2,1,0:T(8,128)(2,1)} %shard_map.60), calls=%async_computation | async-start | bytes 5505024 | tf_op jit(solution)/shard_map/all_to_all | solution.py:224
  9.4 0.0 copy-done
  9.4 0.0 copy-done.5
  9.4 0.0 copy-start.1
  9.4 1.0 %copy-done.1 = f32[2,64,1024]{2,1,0:T(8,128)S(1)} copy-done((f32[2,64,1024]{2,1,0:T(8,128)S(1)}, f32[2,64,1024]{2,1,0:T(8,128)}, u32[]{:S(2)}) %copy-start.1) | copy-done | bytes 524312
  10.5 0.6 shard_map.59
  11.1 0.0 copy-start.2
  11.1 1.0 %copy-done.2 = f32[2,2,64,1024]{3,2,1,0:T(8,128)} copy-done((f32[2,2,64,1024]{3,2,1,0:T(8,128)}, f32[2,2,64,1024]{3,2,1,0:T(8,128)S(1)}, u32[]{:S(2)}) %copy-start.2) | copy-done | bytes 1048600
  12.1 0.7 copy-done.6
  12.8 1.1 %copy-done.8 = bf16[2,2,192,1024]{3,2,1,0:T(8,128)(2,1)} copy-done((bf16[2,2,192,1024]{3,2,1,0:T(8,128)(2,1)}, bf16[2,2,192,1024]{3,2,1,0:T(8,128)(2,1)S(1)}, u32[]{:S(2)}) %copy-start.8) | copy-done | bytes 1572888
  13.9 0.7 copy-done.10
  14.6 0.1 pad_add_fusion.where
  14.7 28.9 %all-to-all-done.packed = bf16[8,64,2688]{2,1,0:T(8,128)(2,1)S(1)} async-done(((bf16[8,64,2688]{2,1,0:T(8,128)(2,1)}), bf16[8,64,2688]{2,1,0:T(8,128)(2,1)S(1)}, u32[]{:S(2)}, u32[]{:S(2)}) %all-to-all-start) | async-done | bytes 2752544 | tf_op jit(solution)/shard_map/all_to_all | solution.py:224
  43.6 0.0 copy-start.11
  43.6 0.9 %copy-done.11 = f32[64,1024]{1,0:T(8,128)S(1)} copy-done((f32[64,1024]{1,0:T(8,128)S(1)}, f32[64,1024]{1,0:T(8,128)}, u32[]{:S(2)}) %copy-start.11) | copy-done | bytes 262168
  44.6 4.7 %shard_map.61 = (f32[64,1024]{1,0:T(8,128)}, f32[64,1024]{1,0:T(8,128)}, bf16[64,1024]{1,0:T(8,128)(2,1)S(1)}) custom-call(s32[2]{0:T(128)S(1)} %pad_add_fusion.where, bf16[64,1024]{1,0:T(8,128)(2,1)S(1)} %broadcast_in_dim.3.start, bf16[8,64,2688]{2,1,0:T(8,128)(2,1)S(1)} %all-to-all-done.packed, f32[64,1024]{1,0:T(8,128)S(1)} %copy-done.11), custom_call_target="tpu_custom_call" | custom-call | flops 1200000000 | bytes 4000000 | tf_op jit(solution)/shard_map/pallas_call | solution.py:234
  49.3 1.5 %collective-permute-start = (bf16[64,1024]{1,0:T(8,128)(2,1)S(1)}, bf16[64,1024]{1,0:T(8,128)(2,1)S(1)}, u32[]{:S(2)}, u32[]{:S(2)}) collective-permute-start(bf16[64,1024]{1,0:T(8,128)(2,1)S(1)} %get-tuple-element.16), channel_id=1, source_target_pairs={{128,0},{144,16},{160,32},{176,48},{192,64},{208,80},{224,96},{240... | collective-permute-start | bytes 393224 | tf_op jit(solution)/shard_map/ppermute | solution.py:235
  50.8 5.6 %collective-permute-done.start = bf16[64,1024]{1,0:T(8,128)(2,1)S(1)} collective-permute-done((bf16[64,1024]{1,0:T(8,128)(2,1)S(1)}, bf16[64,1024]{1,0:T(8,128)(2,1)S(1)}, u32[]{:S(2)}, u32[]{:S(2)}) %collective-permute-start) | collective-permute-done | bytes 131104 | tf_op jit(solution)/shard_map/ppermute | solution.py:235
  56.4 5.0 %shard_map.62 = (f32[64,1024]{1,0:T(8,128)S(1)}, f32[64,1024]{1,0:T(8,128)S(1)}, bf16[64,1024]{1,0:T(8,128)(2,1)}) custom-call(s32[2]{0:T(128)S(1)} %pad_add_fusion.where, bf16[64,1024]{1,0:T(8,128)(2,1)S(1)} %collective-permute-done.start, bf16[8,64,2688]{2,1,0:T(8,128)(2,1)S(1)} %all-to-all-done.packed, f32[64,1024]{1,0:T(8,128)S(1)} %copy-done.11), custom_call_target="tpu_custom_call" | custom-call | flops 1200000000 | bytes 4000000 | tf_op jit(solution)/shard_map/pallas_call | solution.py:236
  61.4 0.0 collective-permute-start.1
  61.4 1.5 %collective-permute-done.1.other = f32[64,1024]{1,0:T(8,128)S(1)} collective-permute-done((f32[64,1024]{1,0:T(8,128)S(1)}, f32[64,1024]{1,0:T(8,128)S(1)}, u32[]{:S(2)}, u32[]{:S(2)}) %collective-permute-start.1) | collective-permute-done | bytes 262176 | tf_op jit(solution)/shard_map/ppermute | solution.py:237
  62.9 0.0 copy-done.3
  62.9 0.0 copy-done.7
  62.9 0.0 copy-done.9
  62.9 2.0 %shard_map.63 = (bf16[16,8,576]{2,1,0:T(8,128)(2,1)}, bf16[2,192,1024]{2,1,0:T(8,128)(2,1)S(1)}, f32[2,64,1024]{2,1,0:T(8,128)S(1)}) custom-call(s32[1]{0:T(128)} %bitcast.which, bf16[2,192,192]{2,1,0:T(8,128)(2,1)S(1)} %copy-done.7, bf16[2,2,192,1024]{3,2,1,0:T(8,128)(2,1)S(1)} %copy-done.9, f32[2,2,64,1024]{3,2,1,0:T(8,128)S(1)} %copy-done.3, ...), custom_call_target="tpu_custom_call" | custom-call | flops 1200000000 | bytes 3000000 | tf_op jit(solution)/shard_map/pallas_call | solution.py:239
  64.9 11.0 %all-to-all-start.1 = ((bf16[16,8,576]{2,1,0:T(8,128)(2,1)}), bf16[16,8,576]{2,1,0:T(8,128)(2,1)S(1)}, u32[]{:S(2)}, u32[]{:S(2)}) async-start(bf16[16,8,576]{2,1,0:T(8,128)(2,1)} %get-tuple-element.21), calls=%async_computation.1 | async-start | bytes 327680 | tf_op jit(solution)/shard_map/all_to_all | solution.py:244
  76.0 1.2 %shard_map.64 = f32[1,2,64,1024]{3,2,1,0:T(8,128)} custom-call(bf16[2,192,192]{2,1,0:T(8,128)(2,1)S(1)} %copy-done.7, f32[2,2,64,1024]{3,2,1,0:T(8,128)S(1)} %copy-done.4, bf16[2,192,1024]{2,1,0:T(8,128)(2,1)S(1)} %get-tuple-element.19.x3s, f32[2,64,1024]{2,1,0:T(8,128)S(1)} %get-tuple-element.20.lams), custom_call_target="tpu_custom_call" | custom-call | flops 300000000 | bytes 3000000 | tf_op jit(solution)/shard_map/pallas_call | solution.py:245
  77.2 9.1 %all-to-all-done.1.parts = bf16[16,8,576]{2,1,0:T(8,128)(2,1)S(1)} async-done(((bf16[16,8,576]{2,1,0:T(8,128)(2,1)}), bf16[16,8,576]{2,1,0:T(8,128)(2,1)S(1)}, u32[]{:S(2)}, u32[]{:S(2)}) %all-to-all-start.1) | async-done | bytes 147488 | tf_op jit(solution)/shard_map/all_to_all | solution.py:244
  86.4 0.7 shard_map.65
  (9 shorter events, 0.0 us)
Async XLA Ops:
  4.8 4.6 %copy-start = (bf16[2,2,64,1024]{3,2,1,0:T(8,128)(2,1)S(1)}, bf16[2,2,64,1024]{3,2,1,0:T(8,128)(2,1)}, u32[]{:S(2)}) copy-start(bf16[2,2,64,1024]{3,2,1,0:T(8,128)(2,1)} %states.3) | copy-start | bytes 1572868
  4.8 4.6 %copy-start.5 = (bf16[2,64,576]{2,1,0:T(8,128)(2,1)S(1)}, bf16[2,64,576]{2,1,0:T(8,128)(2,1)}, u32[]{:S(2)}) copy-start(bf16[2,64,576]{2,1,0:T(8,128)(2,1)} %weights.3) | copy-start | bytes 442372
  4.8 38.8 %all-to-all-start = ((bf16[8,64,2688]{2,1,0:T(8,128)(2,1)}), bf16[8,64,2688]{2,1,0:T(8,128)(2,1)S(1)}, u32[]{:S(2)}, u32[]{:S(2)}) async-start(bf16[8,64,2688]{2,1,0:T(8,128)(2,1)} %shard_map.60), calls=%async_computation | async-start | bytes 5505024 | tf_op jit(solution)/shard_map/all_to_all | solution.py:224
  9.4 1.0 %copy-start.1 = (f32[2,64,1024]{2,1,0:T(8,128)S(1)}, f32[2,64,1024]{2,1,0:T(8,128)}, u32[]{:S(2)}) copy-start(f32[2,64,1024]{2,1,0:T(8,128)} %loss.3) | copy-start | bytes 1572868
  11.1 1.0 %copy-start.2 = (f32[2,2,64,1024]{3,2,1,0:T(8,128)}, f32[2,2,64,1024]{3,2,1,0:T(8,128)S(1)}, u32[]{:S(2)}) copy-start(f32[2,2,64,1024]{3,2,1,0:T(8,128)S(1)} %get-tuple-element.13.slopes) | copy-start | bytes 3145732
  12.1 0.7 copy-start.6
  12.8 1.1 %copy-start.8 = (bf16[2,2,192,1024]{3,2,1,0:T(8,128)(2,1)}, bf16[2,2,192,1024]{3,2,1,0:T(8,128)(2,1)S(1)}, u32[]{:S(2)}) copy-start(bf16[2,2,192,1024]{3,2,1,0:T(8,128)(2,1)S(1)} %get-tuple-element.14.acts) | copy-start | bytes 4718596
  13.9 0.7 copy-start.10
  43.6 1.0 %copy-start.11 = (f32[64,1024]{1,0:T(8,128)S(1)}, f32[64,1024]{1,0:T(8,128)}, u32[]{:S(2)}) copy-start(f32[64,1024]{1,0:T(8,128)} %copy-done.10) | copy-start | bytes 786436
  49.3 13.7 %copy-start.3 = (f32[2,2,64,1024]{3,2,1,0:T(8,128)S(1)}, f32[2,2,64,1024]{3,2,1,0:T(8,128)}, u32[]{:S(2)}) copy-start(f32[2,2,64,1024]{3,2,1,0:T(8,128)} %copy-done.2) | copy-start | bytes 3145732
  49.3 13.7 %copy-start.7 = (bf16[2,192,192]{2,1,0:T(8,128)(2,1)S(1)}, bf16[2,192,192]{2,1,0:T(8,128)(2,1)}, u32[]{:S(2)}) copy-start(bf16[2,192,192]{2,1,0:T(8,128)(2,1)} %copy-done.6) | copy-start | bytes 442372
  49.3 13.7 %copy-start.9 = (bf16[2,2,192,1024]{3,2,1,0:T(8,128)(2,1)S(1)}, bf16[2,2,192,1024]{3,2,1,0:T(8,128)(2,1)}, u32[]{:S(2)}) copy-start(bf16[2,2,192,1024]{3,2,1,0:T(8,128)(2,1)} %copy-done.8) | copy-start | bytes 4718596
  49.3 7.1 %collective-permute-start = (bf16[64,1024]{1,0:T(8,128)(2,1)S(1)}, bf16[64,1024]{1,0:T(8,128)(2,1)S(1)}, u32[]{:S(2)}, u32[]{:S(2)}) collective-permute-start(bf16[64,1024]{1,0:T(8,128)(2,1)S(1)} %get-tuple-element.16), channel_id=1, source_target_pairs={{128,0},{144,16},{160,32},{176,48},{192,64},{208,80},{224,96},{240... | collective-permute-start | bytes 393224 | tf_op jit(solution)/shard_map/ppermute | solution.py:235
  61.4 14.6 %copy-start.4 = (f32[2,2,64,1024]{3,2,1,0:T(8,128)S(1)}, f32[2,2,64,1024]{3,2,1,0:T(8,128)}, u32[]{:S(2)}) copy-start(f32[2,2,64,1024]{3,2,1,0:T(8,128)} %copy-done.2) | copy-start | bytes 3145732
  61.4 1.5 %collective-permute-start.1 = (f32[64,1024]{1,0:T(8,128)S(1)}, f32[64,1024]{1,0:T(8,128)S(1)}, u32[]{:S(2)}, u32[]{:S(2)}) collective-permute-start(f32[64,1024]{1,0:T(8,128)S(1)} %get-tuple-element.18), channel_id=1, source_target_pairs={{0,16},{16,0},{32,48},{48,32},{64,80},{80,64},{96,112},{112,96},{1... | collective-permute-start | bytes 786440 | tf_op jit(solution)/shard_map/ppermute | solution.py:237
  64.9 21.4 %all-to-all-start.1 = ((bf16[16,8,576]{2,1,0:T(8,128)(2,1)}), bf16[16,8,576]{2,1,0:T(8,128)(2,1)S(1)}, u32[]{:S(2)}, u32[]{:S(2)}) async-start(bf16[16,8,576]{2,1,0:T(8,128)(2,1)} %get-tuple-element.21), calls=%async_computation.1 | async-start | bytes 327680 | tf_op jit(solution)/shard_map/all_to_all | solution.py:244

commit v4 on v3

v4 whole, which is shorter than its diff:
```python
import jax
import jax.numpy as jnp
from jax import lax
from jax.experimental import pallas as pl
from jax.experimental.pallas import tpu as pltpu
from jax.sharding import PartitionSpec as P


H = 0.0625
SIDE = 32
C = 64
N = SIDE * SIDE
LANES = 128
F32 = jnp.float32
BF16 = jnp.bfloat16
WIDE = 640
WHOLE = 62 << 20


def masked(values, keep):
    return jnp.where(keep, values, jnp.zeros_like(values))


def lane(shape):
    return lax.broadcasted_iota(jnp.int32, shape, len(shape) - 1)


def cols3(v):
    v = v.astype(BF16)
    column = lane(v.shape) & (SIDE - 1)
    ahead = masked(pltpu.roll(v, N - 1, 1), column < SIDE - 1)
    behind = masked(pltpu.roll(v, 1, 1), column > 0)
    return jnp.concatenate([ahead, v, behind], axis=0)


def row_up(t):
    t = pltpu.roll(t, SIDE, 1)
    edge = t[:, :LANES]
    return jnp.concatenate([masked(edge, lane(edge.shape) >= SIDE), t[:, LANES:]], axis=1)


def row_down(t):
    t = pltpu.roll(t, N - SIDE, 1)
    edge = t[:, N - LANES :]
    return jnp.concatenate([t[:, : N - LANES], masked(edge, lane(edge.shape) < LANES - SIDE)], axis=1)


def rows3(t):
    t = t.astype(BF16)
    return jnp.concatenate([row_up(t), t, row_down(t)], axis=0)


def taps(w):
    blocks = [
        jnp.concatenate([w[:, (3 * a + b) * C : (3 * a + b + 1) * C] for a in range(3)], axis=1)
        for b in range(3)
    ]
    return jnp.concatenate(blocks, axis=0).astype(F32).T.astype(BF16)


def conv(m, x3):
    y = jnp.dot(m, x3, preferred_element_type=F32)
    low = row_down(y[:C].astype(BF16))
    high = row_up(y[2 * C :].astype(BF16))
    return y[C : 2 * C] + low.astype(F32) + high.astype(F32)


def flatten_taps(m):
    pad = jnp.zeros((C, WIDE - 9 * C), BF16)
    wide = [m[a * C : (a + 1) * C, : 2 * C] for a in range(3)]
    thin = [m[a * C : (a + 1) * C, 2 * C :] for a in range(3)]
    return jnp.concatenate(wide + thin + [pad], axis=1)


def unflatten_taps(flat):
    wide = [flat[:, 2 * C * a : 2 * C * (a + 1)] for a in range(3)]
    thin = [flat[:, (6 + a) * C : (7 + a) * C] for a in range(3)]
    return jnp.concatenate([jnp.concatenate(wide, axis=0), jnp.concatenate(thin, axis=0)], axis=1)


def moves(pairs, sems, first=0):
    made = [pltpu.make_async_copy(a, b, sems.at[first + n]) for n, (a, b) in enumerate(pairs)]
    for one in made:
        one.start()
    return made


def settle(made):
    for one in made:
        one.wait()


def part_of(u, g, lc, m0, m1):
    t1 = jnp.tanh(u[1].astype(F32))
    t0 = jnp.tanh(u[0].astype(F32))
    d0 = H - H * (t0 * t0)
    t = (H - H * (t1 * t1)) * conv(m1, cols3(g))
    p = t + d0 * conv(m0, cols3(t - g + 2.0 * lc))
    return (2.0 * d0).astype(BF16), p.astype(BF16)


def give_kernel(which, states, weights, guess, loss, out, ms, u, w, g, lc, sems):
    i = 1 - which[0]
    in_w, *ins = moves(
        [(weights, w), (states.at[1, i], u.at[1]), (states.at[0, i], u.at[0]), (guess.at[0, i], g), (loss.at[i], lc)],
        sems,
    )
    in_w.wait()
    m1, m0 = taps(w[1]), taps(w[0])
    ms[0], ms[1] = m0, m1
    out[:, 2 * N :] = flatten_taps(m0)
    settle(ins)
    out[:, :N], out[:, N : 2 * N] = part_of(u, g[...], lc[...], m0, m1)


def keep_kernel(which, states, guess, loss, ms, out, u, g, lc, sems):
    i = which[0]
    settle(moves(
        [(states.at[1, i], u.at[1]), (states.at[0, i], u.at[0]), (guess.at[0, i], g), (loss.at[i], lc)], sems
    ))
    out[:, :N], out[:, N:] = part_of(u, g[...], lc[...], ms[0], ms[1])


def merge_kernel(which, keep, got, ms, out, odd, pair, sems):
    even = which[0] == 0
    mine, theirs = flatten_taps(ms[0]), got[:, 2 * N :]
    p_even = jnp.where(even, keep[:, N:], got[:, N : 2 * N])
    p_odd = jnp.where(even, got[:, N : 2 * N], keep[:, N:])
    d_even = jnp.where(even, keep[:, :N], got[:, :N])
    taps_even = jnp.where(even, mine, theirs)
    pair[:, :N] = d_even
    pair[:, N : 2 * N] = jnp.where(even, got[:, :N], keep[:, :N])
    pair[:, 3 * N : 3 * N + WIDE] = taps_even
    pair[:, 3 * N + WIDE :] = jnp.where(even, theirs, mine)
    odd[...] = p_odd
    y = conv(unflatten_taps(taps_even), cols3(p_odd))
    merged = p_even.astype(F32) + p_odd.astype(F32) + d_even.astype(F32) * y
    pair[:, 2 * N : 3 * N] = merged.astype(BF16)
    settle(moves([(pair, out.at[k]) for k in range(out.shape[0])], sems))


def prep_kernel(which, states, loss, acts, slopes, base):
    base[...] = loss[which[0]]
    for layer in range(2):
        for i in range(2):
            t = jnp.tanh(states[layer, i].astype(F32))
            acts[layer, i] = rows3(t)
            slopes[layer, i] = H - H * (t * t)


def apply(packed, k, which, e):
    m = unflatten_taps(packed[k, :, 3 * N + which * WIDE : 3 * N + (which + 1) * WIDE])
    return e + packed[k, :, which * N : (which + 1) * N].astype(F32) * conv(m, cols3(e))


def upper_kernel(packed, last):
    chips = packed.shape[0]

    def step(r, e):
        k = chips - 1 - r
        x = apply(packed, k, 1, e)
        return apply(packed, k, 0, x) + packed[k, :, 2 * N : 3 * N].astype(F32)

    e = packed[chips - 1, :, 2 * N : 3 * N].astype(F32)
    last[...] = lax.fori_loop(1, chips, step, e).astype(BF16)


def lower_kernel(where, which, start, packed, odd, base, mine, other, high, low):
    chips = packed.shape[0]

    def step(r, e):
        k = chips - 1 - r
        x = apply(packed, k, 1, e)

        @pl.when(k == where[0])
        def _():
            high[...] = e
            low[...] = x

        return apply(packed, k, 0, x) + packed[k, :, 2 * N : 3 * N].astype(F32)

    lax.fori_loop(0, chips, step, start[...].astype(F32))
    at_high = high[...] + base[...]
    at_low = low[...] + odd[...].astype(F32) + base[...]
    even = which[0] == 0
    mine[...] = jnp.where(even, at_low, at_high)
    other[...] = jnp.where(even, at_high, at_low)


def finish(i, ms, acts, slopes, v, x3_out, lam_out):
    x3 = cols3(v)
    products = [None, lax.dot_general(x3, acts[1, i], (((1,), (1,)), ((), ())), preferred_element_type=F32)]
    v = v + slopes[1, i] * conv(ms[1], x3)
    x3 = cols3(v)
    products[0] = lax.dot_general(x3, acts[0, i], (((1,), (1,)), ((), ())), preferred_element_type=F32)
    x3_out[...] = x3
    lam_out[...] = v
    return products


def own_kernel(which, ms, acts, slopes, mine, sums, x3, lam):
    sums[0], sums[1] = finish(which[0], ms, acts, slopes, mine[...], x3, lam)


def other_kernel(which, ms, acts, slopes, other, sums, grads, x3, lam):
    products = finish(1 - which[0], ms, acts, slopes, other[...], x3, lam)
    near, far = grads.shape[:2]
    rows = C // (near * far)
    wides = []
    for layer in range(2):
        g = (sums[layer] + products[layer]) * H
        wides.append(jnp.concatenate(
            [g[b * C : (b + 1) * C, a * C : (a + 1) * C] for a in range(3) for b in range(3)], axis=1
        ))
    for d in range(near * far):
        both = [wide[d * rows : (d + 1) * rows] for wide in wides]
        grads[d % near, d // near] = jnp.concatenate(both, axis=0).astype(grads.dtype)


def start_kernel(which, ms, slopes, x3_own, lam_own, x3_other, lam_other, starts):
    for i, x3, lam in ((which[0], x3_own, lam_own), (1 - which[0], x3_other, lam_other)):
        starts[0, i] = lam[...] + slopes[0, i] * conv(ms[0], x3[...])


def sum_kernel(parts, out):
    s = parts[0].astype(F32)
    for d in range(1, parts.shape[0]):
        s = s + parts[d].astype(F32)
    out[...] = s


def total_kernel(parts, out):
    rows = parts.shape[1] // 2
    s = parts[0].astype(F32)
    for d in range(1, parts.shape[0]):
        s = s + parts[d].astype(F32)
    for layer in range(2):
        out[layer : layer + 1, :] = jnp.concatenate(
            [s[layer * rows + r : layer * rows + r + 1] for r in range(rows)], axis=1
        )


def call(kernel, outs, where_in, where_out, scratch, n_sems, flops, moved, grant=16 << 20):
    spaces = {"s": pltpu.SMEM, "v": pltpu.VMEM, "h": pltpu.HBM}
    specs = lambda text: [pl.BlockSpec(memory_space=spaces[k]) for k in text]
    out_specs = specs(where_out)
    return pl.pallas_call(
        kernel,
        out_shape=outs,
        in_specs=specs(where_in),
        out_specs=tuple(out_specs) if isinstance(outs, tuple) else out_specs[0],
        scratch_shapes=[pltpu.VMEM(*one) for one in scratch]
        + ([pltpu.SemaphoreType.DMA((n_sems,))] if n_sems else []),
        cost_estimate=pl.CostEstimate(flops=flops, bytes_accessed=moved, transcendentals=0),
        compiler_params=pltpu.CompilerParams(vmem_limit_bytes=grant),
    )


def reduce_scatter(grads):
    near, far = grads.shape[:2]
    shape = jax.ShapeDtypeStruct
    quads = [[q * near + n for n in range(near)] for q in range(far)]
    parts = lax.all_to_all(grads, "batch", 0, 0, axis_index_groups=quads, tiled=True)
    summed = call(sum_kernel, shape(grads.shape[1:], F32), "v", "v", [], 0, 10**6, 10**6)(parts)
    if far > 1:
        across = [[q * near + n for q in range(far)] for n in range(near)]
        summed = lax.all_to_all(summed, "batch", 0, 0, axis_index_groups=across, tiled=True)
    rows, columns = grads.shape[2:]
    return call(total_kernel, shape((2, rows // 2 * columns), F32), "v", "v", [], 0, 10**6, 10**6)(summed)


def shards(states, weights, guess, loss):
    sections = lax.axis_size("section")
    nb = lax.axis_size("batch")
    half = sections // 2
    chips = half // 2
    at = lax.axis_index("section")
    spot = (lax.rem(at, half) // 2).reshape(1).astype(jnp.int32)
    which = lax.rem(at, 2).reshape(1).astype(jnp.int32)
    shape = jax.ShapeDtypeStruct
    image, image16 = shape((C, N), F32), shape((C, N), BF16)
    near = min(4, nb)

    swap = [(i, i ^ 1) for i in range(sections)]
    give, ms = call(
        give_kernel, (shape((C, 2 * N + WIDE), BF16), shape((2, 3 * C, 3 * C), BF16)), "shhhh", "vv",
        [((2, C, N), BF16), ((2, C, 9 * C), BF16), ((C, N), F32), ((C, N), F32)],
        5, 3 * 10**8, 2 * 10**6, WHOLE,
    )(which, states, weights, guess, loss)
    got = lax.ppermute(give, "section", swap)
    keep = call(
        keep_kernel, shape((C, 2 * N), BF16), "shhhv", "v",
        [((2, C, N), BF16), ((C, N), F32), ((C, N), F32)], 4, 3 * 10**8, 2 * 10**6, WHOLE,
    )(which, states, guess, loss, ms)
    pairs, odd = call(
        merge_kernel, (shape((chips, C, 3 * N + 2 * WIDE), BF16), image16), "svvv", "hv",
        [((C, 3 * N + 2 * WIDE), BF16)], chips, 10**8, 3 * 10**6,
    )(which, keep, got, ms)
    groups = [[x * half + 2 * y + c for y in range(chips)] for x in range(2) for c in range(2)]
    packed = lax.all_to_all(pairs, "section", 0, 0, axis_index_groups=groups, tiled=True)
    acts, slopes, base = call(
        prep_kernel, (shape((2, 2, 3 * C, N), BF16), shape((2, 2, C, N), F32), image),
        "svv", "vvv", [], 0, 10**8, 4 * 10**6,
    )(which, states, loss)

    last = call(upper_kernel, image16, "v", "v", [], 0, 10**9, 2 * 10**6)(packed)
    carried = lax.ppermute(last, "section", [(i, i - half) for i in range(half, sections)])
    mine, other = call(
        lower_kernel, (image, image), "ssvvvv", "vv", [((C, N), F32), ((C, N), F32)], 0, 12 * 10**8, 2 * 10**6
    )(spot, which, carried, packed, odd, base)
    theirs = lax.ppermute(other, "section", swap)

    x3_shape = shape((3 * C, N), BF16)
    sums, x3_own, lam_own = call(
        own_kernel, (shape((2, 3 * C, 3 * C), F32), x3_shape, image), "svvvv", "vvv", [], 0, 4 * 10**8, 10**6
    )(which, ms, acts, slopes, mine)
    grads, x3_other, lam_other = call(
        other_kernel, (shape((near, nb // near, 2 * (C // nb), 9 * C), BF16), x3_shape, image),
        "svvvvv", "vvv", [], 0, 4 * 10**8, 10**6,
    )(which, ms, acts, slopes, theirs, sums)
    starts = call(start_kernel, shape((1, 2, C, N), F32), "svvvvvv", "v", [], 0, 3 * 10**8, 3 * 10**6)(
        which, ms, slopes, x3_own, lam_own, x3_other, lam_other
    )
    return starts, reduce_scatter(grads)


def solution(mesh):
    placed = (
        P("section", "batch", None, None),
        P("section", None, None),
        P("section", "batch", None, None),
        P("batch", None, None),
    )
    return jax.shard_map(
        shards,
        mesh=mesh,
        in_specs=placed,
        out_specs=(P("section", "batch", None, None), P("section", "batch")),
        check_vma=False,
    )
```

time: 87.5 us -> 93.5 us (1.069)
  blocking collectives: 0 us -> 44.1 us
  waiting for transfers between devices: 45.2 us -> 14.7 us
  starting transfers between devices: 17.2 us -> 9.67 us
    all_to_all x0 -> x2, blocking collectives: none -> 44.1 us  [the longest x1 32.6 us: shards(): lax.all_to_all(pairs, 'section', 0, 0, axis_index_groups=groups, tiled=True)]
    all_to_all x2 -> x1, waiting for transfers between devices: 38.1 us -> 9.06 us  [reduce_scatter(): lax.all_to_all(summed, 'batch', 0, 0, axis_index_groups=across, tiled=True)]
    all_to_all x2 -> x1, starting transfers between devices: 15.7 us -> 8.21 us  [reduce_scatter(): lax.all_to_all(summed, 'batch', 0, 0, axis_index_groups=across, tiled=True)]
    ppermute x2 -> x3, waiting for transfers between devices: 7.12 us -> 5.65 us  [the longest x1 5.11 us: shards(): lax.ppermute(last, 'section', [(i, i - half) for i in range(half, section...]
    unnamed x24 -> x14, local copies, waits for them, and re-layouts: 5.53 us -> 4.87 us
    pallas_call x7 -> x11, Pallas kernels: 18.4 us -> 18.7 us  [the longest x1 3.73 us: shards(): call(lower_kernel, (image, image), 'ssvvvv', 'vv', [((C, N), F32), ((C, N...]
  transfers between devices with their start and end apart: 4 -> 4, of which waited for: 4 -> 3; matrix products, arithmetic and copies ran while one was open for 0% -> 0% of each run, Pallas kernels for 2% -> 7%
where the time goes in v4:
time: 93.5 us; the launch traced here: 92.8 us
  blocking collectives  44.1 us (47%)
  Pallas kernels  18.7 us (20%)
  waiting for transfers between devices  14.7 us (16%)
  starting transfers between devices  9.67 us (10%)
  local copies, waits for them, and re-layouts  4.87 us (5%)
    all_to_all x1, blocking collectives, shards(): lax.all_to_all(pairs, 'section', 0, 0, axis_index_groups=groups, tiled=True)  32.6 us
    all_to_all x1, blocking collectives, reduce_scatter(): lax.all_to_all(grads, 'batch', 0, 0, axis_index_groups=quads, tiled=True)  11.4 us
    all_to_all x1, waiting for transfers between devices, reduce_scatter(): lax.all_to_all(summed, 'batch', 0, 0, axis_index_groups=across, tiled=True)  9.06 us
    all_to_all x1, starting transfers between devices, reduce_scatter(): lax.all_to_all(summed, 'batch', 0, 0, axis_index_groups=across, tiled=True)  8.21 us
    ppermute x1, waiting for transfers between devices, shards(): lax.ppermute(last, 'section', [(i, i - half) for i in range(half, section...  5.11 us
    unnamed x14, local copies, waits for them, and re-layouts  4.87 us
    pallas_call x1, Pallas kernels, shards(): call(lower_kernel, (image, image), 'ssvvvv', 'vv', [((C, N), F32), ((C, N...  3.73 us
    pallas_call x1, Pallas kernels, shards(): call(keep_kernel, shape((C, 2 * N), BF16), 'shhhv', 'v', [((2, C, N), BF1...  3.65 us
  transfers between devices with their start and end apart: 4, of which 3 were waited for; matrix products, arithmetic and copies ran while one was open for 0% of the time, Pallas kernels for 7%

profile of v4, /device:TPU:32, one launch (start us, length us, event | category | flops | bytes accessed | tf_op | source)
XLA Modules:
  0.0 92.8 jit_solution(10153237529597453556)
XLA Ops:
  0.6 2.9 %shard_map.59 = (bf16[64,2688]{1,0:T(8,128)(2,1)}, bf16[2,192,192]{2,1,0:T(8,128)(2,1)}) custom-call(s32[1]{0:T(128)} %bitcast.which, bf16[2,2,64,1024]{3,2,1,0:T(8,128)(2,1)} %states.5, bf16[2,64,576]{2,1,0:T(8,128)(2,1)} %weights.1, f32[1,2,64,1024]{3,2,1,0:T(8,128)} %guess.3, f32[2,64,1024]{2,1,0:T(8,128)} %loss.5), custom_call_target="tpu_custom_call" | custom-call | flops 300000000 | bytes 2000000 | tf_op jit(solution)/shard_map/pallas_call | solution.py:285
  3.5 0.1 collective-permute-start
  3.6 3.7 %shard_map.61.keep = bf16[64,2048]{1,0:T(8,128)(2,1)} custom-call(s32[1]{0:T(128)} %bitcast.which, bf16[2,2,64,1024]{3,2,1,0:T(8,128)(2,1)} %states.5, f32[1,2,64,1024]{3,2,1,0:T(8,128)} %guess.3, f32[2,64,1024]{2,1,0:T(8,128)} %loss.5, bf16[2,192,192]{2,1,0:T(8,128)(2,1)} %get-tuple-element.17.ms), custom_call_target="tpu_custom_call" | custom-call | flops 300000000 | bytes 2000000 | tf_op jit(solution)/shard_map/pallas_call | solution.py:291
  7.3 0.0 collective-permute-done.got
  7.3 0.0 copy-start
  7.3 0.9 copy-done
  8.2 0.0 copy-start.6
  8.2 0.9 %copy-done.6 = bf16[64,2048]{1,0:T(8,128)(2,1)S(1)} copy-done((bf16[64,2048]{1,0:T(8,128)(2,1)S(1)}, bf16[64,2048]{1,0:T(8,128)(2,1)}, u32[]{:S(2)}) %copy-start.6) | copy-done | bytes 262168
  9.1 0.8 shard_map.62
  10.0 32.6 %all_to_all.15.packed = bf16[4,64,4352]{2,1,0:T(8,128)(2,1)S(1)} all-to-all(bf16[4,64,4352]{2,1,0:T(8,128)(2,1)S(1)} %get-tuple-element.21), channel_id=1, replica_groups={{0,32,64,96},{16,48,80,112},{128,160,192,224},{144,176,208,240},{1,33,6..., dimensions={0} | all-to-all | bytes 4456448 | tf_op jit(solution)/shard_map/all_to_all | solution.py:300
  42.7 2.6 %shard_map.63 = bf16[64,1024]{1,0:T(8,128)(2,1)S(1)} custom-call(bf16[4,64,4352]{2,1,0:T(8,128)(2,1)S(1)} %all_to_all.15.packed), custom_call_target="tpu_custom_call" | custom-call | flops 1000000000 | bytes 2000000 | tf_op jit(solution)/shard_map/pallas_call | solution.py:306
  45.3 0.0 copy-start.4
  45.3 1.4 %copy-done.4 = bf16[4,64,4352]{2,1,0:T(8,128)(2,1)} copy-done((bf16[4,64,4352]{2,1,0:T(8,128)(2,1)}, bf16[4,64,4352]{2,1,0:T(8,128)(2,1)S(1)}, u32[]{:S(2)}) %copy-start.4) | copy-done | bytes 2228248
  46.7 1.3 %collective-permute-start.1 = (bf16[64,1024]{1,0:T(8,128)(2,1)S(1)}, bf16[64,1024]{1,0:T(8,128)(2,1)S(1)}, u32[]{:S(2)}, u32[]{:S(2)}) collective-permute-start(bf16[64,1024]{1,0:T(8,128)(2,1)S(1)} %shard_map.63), channel_id=1, source_target_pairs={{128,0},{144,16},{160,32},{176,48},{192,64},{208,80},{224,96},{240... | collective-permute-start | bytes 393224 | tf_op jit(solution)/shard_map/ppermute | solution.py:307
  48.0 0.0 copy-done.2
  48.0 0.0 copy-done.3
  48.0 0.4 shard_map.60
  48.4 0.0 copy-start.1
  48.4 5.1 %collective-permute-done.1.start = bf16[64,1024]{1,0:T(8,128)(2,1)S(1)} collective-permute-done((bf16[64,1024]{1,0:T(8,128)(2,1)S(1)}, bf16[64,1024]{1,0:T(8,128)(2,1)S(1)}, u32[]{:S(2)}, u32[]{:S(2)}) %collective-permute-start.1) | collective-permute-done | bytes 131104 | tf_op jit(solution)/shard_map/ppermute | solution.py:307
  53.5 1.6 %copy-done.5 = bf16[4,64,4352]{2,1,0:T(8,128)(2,1)S(1)} copy-done((bf16[4,64,4352]{2,1,0:T(8,128)(2,1)S(1)}, bf16[4,64,4352]{2,1,0:T(8,128)(2,1)}, u32[]{:S(2)}) %copy-start.5) | copy-done | bytes 2228248
  55.1 3.7 %shard_map.64 = (f32[64,1024]{1,0:T(8,128)S(1)}, f32[64,1024]{1,0:T(8,128)S(1)}) custom-call(s32[1]{0:T(128)} %bitcast.1.where, s32[1]{0:T(128)} %bitcast.which, bf16[64,1024]{1,0:T(8,128)(2,1)S(1)} %collective-permute-done.1.start, bf16[4,64,4352]{2,1,0:T(8,128)(2,1)S(1)} %copy-done.5, bf16[64,1024]{1,0:T(8,128)(2,1)S(1)} %get-tuple-element.22.odd, ...), custom_call_target="tpu_custom_call" | custom-call | flops 1200000000 | bytes 2000000 | tf_op jit(solution)/shard_map/pallas_call | solution.py:308
  58.9 0.1 collective-permute-start.2
  59.0 0.0 copy-done.1
  59.0 1.0 %shard_map.65 = (f32[2,192,192]{2,1,0:T(8,128)S(1)}, bf16[192,1024]{1,0:T(8,128)(2,1)S(1)}, f32[64,1024]{1,0:T(8,128)S(1)}) custom-call(s32[1]{0:T(128)} %bitcast.which, bf16[2,192,192]{2,1,0:T(8,128)(2,1)S(1)} %copy-done.1, bf16[2,2,192,1024]{3,2,1,0:T(8,128)(2,1)S(1)} %get-tuple-element.19.acts, f32[2,2,64,1024]{3,2,1,0:T(8,128)S(1)} %get-tuple-element.18.slopes, ...), custom_call_target="tpu_custom_call" | custom-call | flops 400000000 | bytes 1000000 | tf_op jit(solution)/shard_map/pallas_call | solution.py:314
  60.0 0.5 collective-permute-done.2.other
  60.5 1.0 %shard_map.66 = (bf16[4,4,8,576]{3,2,1,0:T(8,128)(2,1)S(1)}, bf16[192,1024]{1,0:T(8,128)(2,1)S(1)}, f32[64,1024]{1,0:T(8,128)S(1)}) custom-call(s32[1]{0:T(128)} %bitcast.which, bf16[2,192,192]{2,1,0:T(8,128)(2,1)S(1)} %copy-done.1, bf16[2,2,192,1024]{3,2,1,0:T(8,128)(2,1)S(1)} %get-tuple-element.19.acts, f32[2,2,64,1024]{3,2,1,0:T(8,128)S(1)} %get-tuple-element.18.slopes, ...), custom_call_target="tpu_custom_call" | custom-call | flops 400000000 | bytes 1000000 | tf_op jit(solution)/shard_map/pallas_call | solution.py:317
  61.5 11.4 %all_to_all.16.parts = bf16[4,4,8,576]{3,2,1,0:T(8,128)(2,1)S(1)} all-to-all(bf16[4,4,8,576]{3,2,1,0:T(8,128)(2,1)S(1)} %get-tuple-element.31), channel_id=1, replica_groups={{0,1,2,3},{4,5,6,7},{8,9,10,11},{12,13,14,15},{16,17,18,19},{20,21,22,2..., dimensions={0} | all-to-all | bytes 294912 | tf_op jit(solution)/shard_map/all_to_all | solution.py:263
  73.0 0.7 shard_map.68
  73.6 8.2 %all-to-all-start.2 = ((f32[4,8,576]{2,1,0:T(8,128)}), f32[4,8,576]{2,1,0:T(8,128)S(1)}, u32[]{:S(2)}, u32[]{:S(2)}) async-start(f32[4,8,576]{2,1,0:T(8,128)} %shard_map.68), calls=%async_computation.2 | async-start | bytes 163840 | tf_op jit(solution)/shard_map/all_to_all | solution.py:267
  81.8 1.2 %shard_map.67 = f32[1,2,64,1024]{3,2,1,0:T(8,128)} custom-call(s32[1]{0:T(128)} %bitcast.which, bf16[2,192,192]{2,1,0:T(8,128)(2,1)S(1)} %copy-done.1, f32[2,2,64,1024]{3,2,1,0:T(8,128)S(1)} %get-tuple-element.18.slopes, bf16[192,1024]{1,0:T(8,128)(2,1)S(1)} %get-tuple-element.25.x3_own, f32[64,1024]{1,0:T(8,128)S(1)} %get-tuple-element.26.lam_own, ...), custom_call_target="tpu_custom_call" | custom-call | flops 300000000 | bytes 3000000 | tf_op jit(solution)/shard_map/pallas_call | solution.py:321
  83.1 9.1 %all-to-all-done.2.parts = f32[4,8,576]{2,1,0:T(8,128)S(1)} async-done(((f32[4,8,576]{2,1,0:T(8,128)}), f32[4,8,576]{2,1,0:T(8,128)S(1)}, u32[]{:S(2)}, u32[]{:S(2)}) %all-to-all-start.2) | async-done | bytes 73760 | tf_op jit(solution)/shard_map/all_to_all | solution.py:267
  92.1 0.7 shard_map.69
  (3 shorter events, 0.0 us)
Async XLA Ops:
  3.5 3.8 %collective-permute-start = (bf16[64,2688]{1,0:T(8,128)(2,1)}, bf16[64,2688]{1,0:T(8,128)(2,1)S(1)}, u32[]{:S(2)}, u32[]{:S(2)}) collective-permute-start(bf16[64,2688]{1,0:T(8,128)(2,1)} %get-tuple-element.20), channel_id=1, source_target_pairs={{0,16},{16,0},{32,48},{48,32},{64,80},{80,64},{96,112},{112,96},{1... | collective-permute-start | bytes 1032200 | tf_op jit(solution)/shard_map/ppermute | solution.py:290
  7.3 0.9 copy-start
  8.2 0.9 %copy-start.6 = (bf16[64,2048]{1,0:T(8,128)(2,1)S(1)}, bf16[64,2048]{1,0:T(8,128)(2,1)}, u32[]{:S(2)}) copy-start(bf16[64,2048]{1,0:T(8,128)(2,1)} %shard_map.61.keep) | copy-start | bytes 786436
  42.7 5.3 %copy-start.2 = (bf16[2,2,64,1024]{3,2,1,0:T(8,128)(2,1)S(1)}, bf16[2,2,64,1024]{3,2,1,0:T(8,128)(2,1)}, u32[]{:S(2)}) copy-start(bf16[2,2,64,1024]{3,2,1,0:T(8,128)(2,1)} %states.5) | copy-start | bytes 1572868
  42.7 5.3 %copy-start.3 = (f32[2,64,1024]{2,1,0:T(8,128)S(1)}, f32[2,64,1024]{2,1,0:T(8,128)}, u32[]{:S(2)}) copy-start(f32[2,64,1024]{2,1,0:T(8,128)} %loss.5) | copy-start | bytes 1572868
  45.3 1.4 %copy-start.4 = (bf16[4,64,4352]{2,1,0:T(8,128)(2,1)}, bf16[4,64,4352]{2,1,0:T(8,128)(2,1)S(1)}, u32[]{:S(2)}) copy-start(bf16[4,64,4352]{2,1,0:T(8,128)(2,1)S(1)} %all_to_all.15.packed) | copy-start | bytes 6684676
  46.7 6.8 %collective-permute-start.1 = (bf16[64,1024]{1,0:T(8,128)(2,1)S(1)}, bf16[64,1024]{1,0:T(8,128)(2,1)S(1)}, u32[]{:S(2)}, u32[]{:S(2)}) collective-permute-start(bf16[64,1024]{1,0:T(8,128)(2,1)S(1)} %shard_map.63), channel_id=1, source_target_pairs={{128,0},{144,16},{160,32},{176,48},{192,64},{208,80},{224,96},{240... | collective-permute-start | bytes 393224 | tf_op jit(solution)/shard_map/ppermute | solution.py:307
  48.4 10.6 %copy-start.1 = (bf16[2,192,192]{2,1,0:T(8,128)(2,1)S(1)}, bf16[2,192,192]{2,1,0:T(8,128)(2,1)}, u32[]{:S(2)}) copy-start(bf16[2,192,192]{2,1,0:T(8,128)(2,1)} %get-tuple-element.17.ms) | copy-start | bytes 442372
  53.5 1.6 %copy-start.5 = (bf16[4,64,4352]{2,1,0:T(8,128)(2,1)S(1)}, bf16[4,64,4352]{2,1,0:T(8,128)(2,1)}, u32[]{:S(2)}) copy-start(bf16[4,64,4352]{2,1,0:T(8,128)(2,1)} %copy-done.4) | copy-start | bytes 6684676
  58.9 1.6 %collective-permute-start.2 = (f32[64,1024]{1,0:T(8,128)S(1)}, f32[64,1024]{1,0:T(8,128)S(1)}, u32[]{:S(2)}, u32[]{:S(2)}) collective-permute-start(f32[64,1024]{1,0:T(8,128)S(1)} %get-tuple-element.27), channel_id=1, source_target_pairs={{0,16},{16,0},{32,48},{48,32},{64,80},{80,64},{96,112},{112,96},{1... | collective-permute-start | bytes 786440 | tf_op jit(solution)/shard_map/ppermute | solution.py:311
  73.6 18.5 %all-to-all-start.2 = ((f32[4,8,576]{2,1,0:T(8,128)}), f32[4,8,576]{2,1,0:T(8,128)S(1)}, u32[]{:S(2)}, u32[]{:S(2)}) async-start(f32[4,8,576]{2,1,0:T(8,128)} %shard_map.68), calls=%async_computation.2 | async-start | bytes 163840 | tf_op jit(solution)/shard_map/all_to_all | solution.py:267

commit v5 on v4

v5 whole, which is shorter than its diff:
```python
import jax
import jax.numpy as jnp
from jax import lax
from jax.experimental import pallas as pl
from jax.experimental.pallas import tpu as pltpu
from jax.sharding import PartitionSpec as P


H = 0.0625
SIDE = 32
C = 64
N = SIDE * SIDE
LANES = 128
F32 = jnp.float32
BF16 = jnp.bfloat16
WIDE = 640
LEAD = 2 * N + 2 * WIDE
WHOLE = 62 << 20


def masked(values, keep):
    return jnp.where(keep, values, jnp.zeros_like(values))


def lane(shape):
    return lax.broadcasted_iota(jnp.int32, shape, len(shape) - 1)


def cols3(v):
    v = v.astype(BF16)
    column = lane(v.shape) & (SIDE - 1)
    ahead = masked(pltpu.roll(v, N - 1, 1), column < SIDE - 1)
    behind = masked(pltpu.roll(v, 1, 1), column > 0)
    return jnp.concatenate([ahead, v, behind], axis=0)


def row_up(t):
    t = pltpu.roll(t, SIDE, 1)
    edge = t[:, :LANES]
    return jnp.concatenate([masked(edge, lane(edge.shape) >= SIDE), t[:, LANES:]], axis=1)


def row_down(t):
    t = pltpu.roll(t, N - SIDE, 1)
    edge = t[:, N - LANES :]
    return jnp.concatenate([t[:, : N - LANES], masked(edge, lane(edge.shape) < LANES - SIDE)], axis=1)


def rows3(t):
    t = t.astype(BF16)
    return jnp.concatenate([row_up(t), t, row_down(t)], axis=0)


def taps(w):
    blocks = [
        jnp.concatenate([w[:, (3 * a + b) * C : (3 * a + b + 1) * C] for a in range(3)], axis=1)
        for b in range(3)
    ]
    return jnp.concatenate(blocks, axis=0).astype(F32).T.astype(BF16)


def conv(m, x3):
    y = jnp.dot(m, x3, preferred_element_type=F32)
    low = row_down(y[:C].astype(BF16))
    high = row_up(y[2 * C :].astype(BF16))
    return y[C : 2 * C] + low.astype(F32) + high.astype(F32)


def flatten_taps(m):
    pad = jnp.zeros((C, WIDE - 9 * C), BF16)
    wide = [m[a * C : (a + 1) * C, : 2 * C] for a in range(3)]
    thin = [m[a * C : (a + 1) * C, 2 * C :] for a in range(3)]
    return jnp.concatenate(wide + thin + [pad], axis=1)


def unflatten_taps(flat):
    wide = [flat[:, 2 * C * a : 2 * C * (a + 1)] for a in range(3)]
    thin = [flat[:, (6 + a) * C : (7 + a) * C] for a in range(3)]
    return jnp.concatenate([jnp.concatenate(wide, axis=0), jnp.concatenate(thin, axis=0)], axis=1)


def core():
    return lax.rem(lax.axis_index("section"), 2)


def moves(pairs, sems, first=0):
    made = [pltpu.make_async_copy(a, b, sems.at[first + n]) for n, (a, b) in enumerate(pairs)]
    for one in made:
        one.start()
    return made


def settle(made):
    for one in made:
        one.wait()


def part_of(u, g, lc, m0, m1):
    t1 = jnp.tanh(u[1].astype(F32))
    t0 = jnp.tanh(u[0].astype(F32))
    d0 = H - H * (t0 * t0)
    t = (H - H * (t1 * t1)) * conv(m1, cols3(g))
    p = t + d0 * conv(m0, cols3(t - g + 2.0 * lc))
    return (2.0 * d0).astype(BF16), p.astype(BF16)


def source_kernel(states, weights, guess, loss, give, keep, ms, u, w, g, lc, sems):
    own = core()
    in_w, *ins = moves([(weights, w), (states, u), (guess.at[0], g), (loss, lc)], sems)
    in_w.wait()
    m1, m0 = taps(w[1]), taps(w[0])
    ms[0], ms[1] = m0, m1
    give[:, 2 * N :] = flatten_taps(m0)
    settle(ins)
    for i, out in ((1 - own, give), (own, keep)):
        out[:, :N], out[:, N : 2 * N] = part_of(u.at[:, i], g[i], lc[i], m0, m1)


def merge_kernel(keep, got, ms, out, odd, pair, sems):
    even = core() == 0
    mine, theirs = flatten_taps(ms[0]), got[:, 2 * N :]
    d_even = jnp.where(even, keep[:, :N], got[:, :N])
    taps_even = jnp.where(even, mine, theirs)
    pair[:, :N] = d_even
    pair[:, N : 2 * N] = jnp.where(even, got[:, :N], keep[:, :N])
    pair[:, 2 * N : 2 * N + WIDE] = taps_even
    pair[:, 2 * N + WIDE : LEAD] = jnp.where(even, theirs, mine)
    chips = out.shape[0]
    sent = moves([(pair.at[:, :LEAD], out.at[k, :, :LEAD]) for k in range(chips)], sems)
    p_even = jnp.where(even, keep[:, N:], got[:, N : 2 * N])
    p_odd = jnp.where(even, got[:, N : 2 * N], keep[:, N:])
    odd[...] = p_odd
    y = conv(unflatten_taps(taps_even), cols3(p_odd))
    merged = p_even.astype(F32) + p_odd.astype(F32) + d_even.astype(F32) * y
    pair[:, LEAD:] = merged.astype(BF16)
    settle(sent + moves([(pair.at[:, LEAD:], out.at[k, :, LEAD:]) for k in range(chips)], sems, chips))


def prep_kernel(states, loss, acts, slopes, base):
    base[...] = loss[core()]
    for layer in range(2):
        for i in range(2):
            t = jnp.tanh(states[layer, i].astype(F32))
            acts[layer, i] = rows3(t)
            slopes[layer, i] = H - H * (t * t)


def apply(packed, k, which, e):
    m = unflatten_taps(packed[k, :, 2 * N + which * WIDE : 2 * N + (which + 1) * WIDE])
    return e + packed[k, :, which * N : (which + 1) * N].astype(F32) * conv(m, cols3(e))


def arrivals(source, packed, sems):
    made = [pltpu.make_async_copy(source.at[k], packed.at[k], sems.at[k]) for k in range(packed.shape[0])]
    for one in made[::-1]:
        one.start()
    return lambda k: pltpu.make_async_copy(source.at[k], packed.at[k], sems.at[k]).wait()


def upper_kernel(source, last, packed, sems):
    chips = packed.shape[0]
    arrived = arrivals(source, packed, sems)

    def step(r, e):
        k = chips - 1 - r
        arrived(k)
        x = apply(packed, k, 1, e)
        return apply(packed, k, 0, x) + packed[k, :, LEAD:].astype(F32)

    arrived(chips - 1)
    e = packed[chips - 1, :, LEAD:].astype(F32)
    last[...] = lax.fori_loop(1, chips, step, e).astype(BF16)


def lower_kernel(start, source, odd, base, mine, other, high, low, packed, sems):
    chips = packed.shape[0]
    arrived = arrivals(source, packed, sems)

    def step(r, e):
        k = chips - 1 - r
        arrived(k)
        x = apply(packed, k, 1, e)

        @pl.when(k == lax.rem(lax.axis_index("section") // 2, chips))
        def _():
            high[...] = e
            low[...] = x

        return apply(packed, k, 0, x) + packed[k, :, LEAD:].astype(F32)

    lax.fori_loop(0, chips, step, start[...].astype(F32))
    at_high = high[...] + base[...]
    at_low = low[...] + odd[...].astype(F32) + base[...]
    even = core() == 0
    mine[...] = jnp.where(even, at_low, at_high)
    other[...] = jnp.where(even, at_high, at_low)


def finish(i, ms, acts, slopes, v):
    x3 = cols3(v)
    first = lax.dot_general(x3, acts[1, i], (((1,), (1,)), ((), ())), preferred_element_type=F32)
    x3 = cols3(v + slopes[1, i] * conv(ms[1], x3))
    return lax.dot_general(x3, acts[0, i], (((1,), (1,)), ((), ())), preferred_element_type=F32), first


def own_kernel(ms, acts, slopes, mine, sums):
    sums[0], sums[1] = finish(core(), ms, acts, slopes, mine[...])


def other_kernel(ms, acts, slopes, other, sums, grads):
    products = finish(1 - core(), ms, acts, slopes, other[...])
    parts = grads.shape[0]
    rows = C // parts
    wides = []
    for layer in range(2):
        g = (sums[layer] + products[layer]) * H
        wides.append(jnp.concatenate(
            [g[b * C : (b + 1) * C, a * C : (a + 1) * C] for a in range(3) for b in range(3)], axis=1
        ))
    for d in range(parts):
        both = [wide[d * rows : (d + 1) * rows] for wide in wides]
        grads[d] = jnp.concatenate(both, axis=0).astype(grads.dtype)


def start_kernel(ms, slopes, mine, theirs, starts):
    for i, lam in ((core(), mine), (1 - core(), theirs)):
        v = lam[...]
        for layer in (1, 0):
            v = v + slopes[layer, i] * conv(ms[layer], cols3(v))
        starts[0, i] = v


def total_kernel(parts, out):
    rows = parts.shape[1] // 2
    s = parts[0].astype(F32)
    for d in range(1, parts.shape[0]):
        s = s + parts[d].astype(F32)
    for layer in range(2):
        out[layer : layer + 1, :] = jnp.concatenate(
            [s[layer * rows + r : layer * rows + r + 1] for r in range(rows)], axis=1
        )


def call(kernel, outs, where_in, where_out, scratch, n_sems, flops, moved, grant=16 << 20):
    spaces = {"s": pltpu.SMEM, "v": pltpu.VMEM, "h": pltpu.HBM}
    specs = lambda text: [pl.BlockSpec(memory_space=spaces[k]) for k in text]
    out_specs = specs(where_out)
    return pl.pallas_call(
        kernel,
        out_shape=outs,
        in_specs=specs(where_in),
        out_specs=tuple(out_specs) if isinstance(outs, tuple) else out_specs[0],
        scratch_shapes=[pltpu.VMEM(*one) for one in scratch]
        + ([pltpu.SemaphoreType.DMA((n_sems,))] if n_sems else []),
        cost_estimate=pl.CostEstimate(flops=flops, bytes_accessed=moved, transcendentals=0),
        compiler_params=pltpu.CompilerParams(vmem_limit_bytes=grant),
    )


def shards(states, weights, guess, loss):
    sections = lax.axis_size("section")
    nb = lax.axis_size("batch")
    half = sections // 2
    chips = half // 2
    shape = jax.ShapeDtypeStruct
    image, image16 = shape((C, N), F32), shape((C, N), BF16)

    swap = [(i, i ^ 1) for i in range(sections)]
    give, keep, ms = call(
        source_kernel,
        (shape((C, 2 * N + WIDE), BF16), shape((C, 2 * N), BF16), shape((2, 3 * C, 3 * C), BF16)), "hhhh", "vvv",
        [((2, 2, C, N), BF16), ((2, C, 9 * C), BF16), ((2, C, N), F32), ((2, C, N), F32)],
        4, 6 * 10**8, 2 * 10**6, WHOLE,
    )(states, weights, guess, loss)
    got = lax.ppermute(give, "section", swap)
    pairs, odd = call(
        merge_kernel, (shape((chips, C, LEAD + N), BF16), image16), "vvv", "hv",
        [((C, LEAD + N), BF16)], 2 * chips, 10**8, 3 * 10**6,
    )(keep, got, ms)
    groups = [[x * half + 2 * y + c for y in range(chips)] for x in range(2) for c in range(2)]
    packed = lax.all_to_all(pairs, "section", 0, 0, axis_index_groups=groups, tiled=True)
    acts, slopes, base = call(
        prep_kernel, (shape((2, 2, 3 * C, N), BF16), shape((2, 2, C, N), F32), image),
        "vv", "vvv", [], 0, 10**8, 4 * 10**6,
    )(states, loss)

    last = call(upper_kernel, image16, "h", "v", [((chips, C, LEAD + N), BF16)], chips, 10**9, 2 * 10**6)(packed)
    carried = lax.ppermute(last, "section", [(i, i - half) for i in range(half, sections)])
    mine, other = call(
        lower_kernel, (image, image), "vhvv", "vv",
        [((C, N), F32), ((C, N), F32), ((chips, C, LEAD + N), BF16)], chips, 12 * 10**8, 2 * 10**6
    )(carried, packed, odd, base)
    theirs = lax.ppermute(other, "section", swap)

    sums = call(own_kernel, shape((2, 3 * C, 3 * C), F32), "vvvv", "v", [], 0, 4 * 10**8, 10**6)(ms, acts, slopes, mine)
    grads = call(
        other_kernel, shape((nb, 2 * (C // nb), 9 * C), BF16), "vvvvv", "v", [], 0, 4 * 10**8, 10**6
    )(ms, acts, slopes, theirs, sums)
    starts = call(start_kernel, shape((1, 2, C, N), F32), "vvvv", "v", [], 0, 6 * 10**8, 3 * 10**6)(
        ms, slopes, mine, theirs
    )
    grads = lax.all_to_all(grads, "batch", 0, 0, tiled=True)
    total = call(total_kernel, shape((2, 9 * C * C // nb), F32), "v", "v", [], 0, 10**6, 10**6)(grads)
    return starts, total


def solution(mesh):
    placed = (
        P("section", "batch", None, None),
        P("section", None, None),
        P("section", "batch", None, None),
        P("batch", None, None),
    )
    return jax.shard_map(
        shards,
        mesh=mesh,
        in_specs=placed,
        out_specs=(P("section", "batch", None, None), P("section", "batch")),
        check_vma=False,
    )
```

time: 93.5 us -> 80.9 us (0.87)
  blocking collectives: 44.1 us -> 32.3 us
  local copies, waits for them, and re-layouts: 4.87 us -> 1.89 us
  starting transfers between devices: 9.67 us -> 12.5 us
  Pallas kernels: 18.7 us -> 17.4 us
  waiting for transfers between devices: 14.7 us -> 15.8 us
    all_to_all x1 -> x0, blocking collectives: 11.4 us -> none  [reduce_scatter(): lax.all_to_all(grads, 'batch', 0, 0, axis_index_groups=quads, tiled=True)]
    unnamed x14 -> x10, local copies, waits for them, and re-layouts: 4.87 us -> 1.89 us
    all_to_all x1, starting transfers between devices: 8.21 us -> 11.1 us  [shards(): grads = lax.all_to_all(grads, 'batch', 0, 0, tiled=True)]
    ppermute x1, waiting for transfers between devices: 0.01 us -> 1.85 us  [shards(): got = lax.ppermute(give, 'section', swap)]
    pallas_call x10 -> x8, Pallas kernels: 18.3 us -> 17 us  [the longest x1 4.02 us: shards(): call(lower_kernel, (image, image), 'vhvv', 'vv', [((C, N), F32), ((C, N),...]
  transfers between devices with their start and end apart: 4 -> 4, of which waited for: 3 -> 4; matrix products, arithmetic and copies ran while one was open for 0% -> 0% of each run, Pallas kernels for 7% -> 4%
where the time goes in v5:
time: 80.9 us; the launch traced here: 80.6 us
  blocking collectives  32.3 us (40%)
  Pallas kernels  17.4 us (22%)
  waiting for transfers between devices  15.8 us (20%)
  starting transfers between devices  12.5 us (15%)
  local copies, waits for them, and re-layouts  1.89 us (2%)
    all_to_all x1, blocking collectives, shards(): lax.all_to_all(pairs, 'section', 0, 0, axis_index_groups=groups, tiled=True)  32.3 us
    all_to_all x1, starting transfers between devices, shards(): grads = lax.all_to_all(grads, 'batch', 0, 0, tiled=True)  11.1 us
    all_to_all x1, waiting for transfers between devices, shards(): grads = lax.all_to_all(grads, 'batch', 0, 0, tiled=True)  8.24 us
    ppermute x1, waiting for transfers between devices, shards(): lax.ppermute(last, 'section', [(i, i - half) for i in range(half, section...  5.12 us
    pallas_call x1, Pallas kernels, shards(): call(lower_kernel, (image, image), 'vhvv', 'vv', [((C, N), F32), ((C, N),...  4.02 us
    pallas_call x1, Pallas kernels, shards(): call(source_kernel, (shape((C, 2 * N + WIDE), BF16), shape((C, 2 * N), BF...  3.63 us
    pallas_call x1, Pallas kernels, shards(): call(upper_kernel, image16, 'h', 'v', [((chips, C, LEAD + N), BF16)], chi...  2.97 us
    pallas_call x1, Pallas kernels, shards(): call(start_kernel, shape((1, 2, C, N), F32), 'vvvv', 'v', [], 0, 6 * 10 *...  2.14 us
  transfers between devices with their start and end apart: 4, of which 4 were waited for; matrix products, arithmetic and copies ran while one was open for 0% of the time, Pallas kernels for 4%

profile of v5, /device:TPU:32, one launch (start us, length us, event | category | flops | bytes accessed | tf_op | source)
XLA Modules:
  0.0 80.6 jit_solution(13326924902702401001)
XLA Ops:
  0.6 3.6 %shard_map.59 = (bf16[64,2688]{1,0:T(8,128)(2,1)}, bf16[64,2048]{1,0:T(8,128)(2,1)}, bf16[2,192,192]{2,1,0:T(8,128)(2,1)}) custom-call(bf16[2,2,64,1024]{3,2,1,0:T(8,128)(2,1)} %states.3, bf16[2,64,576]{2,1,0:T(8,128)(2,1)} %weights.1, f32[1,2,64,1024]{3,2,1,0:T(8,128)} %guess.1, f32[2,64,1024]{2,1,0:T(8,128)} %loss.3), custom_call_target="tpu_custom_call" | custom-call | flops 600000000 | bytes 2000000 | tf_op jit(solution)/shard_map/pallas_call | solution.py:269
  4.3 0.1 collective-permute-start
  4.4 1.9 %collective-permute-done.got = bf16[64,2688]{1,0:T(8,128)(2,1)S(1)} collective-permute-done((bf16[64,2688]{1,0:T(8,128)(2,1)}, bf16[64,2688]{1,0:T(8,128)(2,1)S(1)}, u32[]{:S(2)}, u32[]{:S(2)}) %collective-permute-start) | collective-permute-done | bytes 344096 | tf_op jit(solution)/shard_map/ppermute | solution.py:275
  6.2 0.0 copy-start
  6.2 0.9 %copy-done = bf16[2,192,192]{2,1,0:T(8,128)(2,1)S(1)} copy-done((bf16[2,192,192]{2,1,0:T(8,128)(2,1)S(1)}, bf16[2,192,192]{2,1,0:T(8,128)(2,1)}, u32[]{:S(2)}) %copy-start) | copy-done | bytes 147480
  7.1 0.0 copy-start.4
  7.1 0.9 %copy-done.4 = bf16[64,2048]{1,0:T(8,128)(2,1)S(1)} copy-done((bf16[64,2048]{1,0:T(8,128)(2,1)S(1)}, bf16[64,2048]{1,0:T(8,128)(2,1)}, u32[]{:S(2)}) %copy-start.4) | copy-done | bytes 262168
  8.1 0.9 %shard_map.61 = (bf16[4,64,4352]{2,1,0:T(8,128)(2,1)S(1)}, bf16[64,1024]{1,0:T(8,128)(2,1)S(1)}) custom-call(bf16[64,2048]{1,0:T(8,128)(2,1)S(1)} %copy-done.4, bf16[64,2688]{1,0:T(8,128)(2,1)S(1)} %collective-permute-done.got, bf16[2,192,192]{2,1,0:T(8,128)(2,1)S(1)} %copy-done), custom_call_target="tpu_custom_call" | custom-call | flops 100000000 | bytes 3000000 | tf_op jit(solution)/shard_map/pallas_call | solution.py:276
  9.0 32.3 %all_to_all.10.source = bf16[4,64,4352]{2,1,0:T(8,128)(2,1)S(1)} all-to-all(bf16[4,64,4352]{2,1,0:T(8,128)(2,1)S(1)} %get-tuple-element.16), channel_id=1, replica_groups={{0,32,64,96},{16,48,80,112},{128,160,192,224},{144,176,208,240},{1,33,6..., dimensions={0} | all-to-all | bytes 4456448 | tf_op jit(solution)/shard_map/all_to_all | solution.py:281
  41.3 0.0 copy-start.2
  41.3 0.0 copy-start.3
  41.3 3.0 %shard_map.62 = bf16[64,1024]{1,0:T(8,128)(2,1)S(1)} custom-call(bf16[4,64,4352]{2,1,0:T(8,128)(2,1)S(1)} %all_to_all.10.source), custom_call_target="tpu_custom_call" | custom-call | flops 1000000000 | bytes 2000000 | tf_op jit(solution)/shard_map/pallas_call | solution.py:287
  44.2 1.3 %collective-permute-start.1 = (bf16[64,1024]{1,0:T(8,128)(2,1)S(1)}, bf16[64,1024]{1,0:T(8,128)(2,1)S(1)}, u32[]{:S(2)}, u32[]{:S(2)}) collective-permute-start(bf16[64,1024]{1,0:T(8,128)(2,1)S(1)} %shard_map.62), channel_id=1, source_target_pairs={{128,0},{144,16},{160,32},{176,48},{192,64},{208,80},{224,96},{240... | collective-permute-start | bytes 393224 | tf_op jit(solution)/shard_map/ppermute | solution.py:288
  45.5 0.0 copy-done.2
  45.6 0.0 copy-done.3
  45.6 0.4 shard_map.60
  46.0 0.0 copy-start.1
  46.0 5.1 %collective-permute-done.1.start = bf16[64,1024]{1,0:T(8,128)(2,1)S(1)} collective-permute-done((bf16[64,1024]{1,0:T(8,128)(2,1)S(1)}, bf16[64,1024]{1,0:T(8,128)(2,1)S(1)}, u32[]{:S(2)}, u32[]{:S(2)}) %collective-permute-start.1) | collective-permute-done | bytes 131104 | tf_op jit(solution)/shard_map/ppermute | solution.py:288
  51.1 4.0 %shard_map.63 = (f32[64,1024]{1,0:T(8,128)S(1)}, f32[64,1024]{1,0:T(8,128)S(1)}) custom-call(bf16[64,1024]{1,0:T(8,128)(2,1)S(1)} %collective-permute-done.1.start, bf16[4,64,4352]{2,1,0:T(8,128)(2,1)S(1)} %all_to_all.10.source, bf16[64,1024]{1,0:T(8,128)(2,1)S(1)} %get-tuple-element.17.odd, f32[64,1024]{1,0:T(8,128)S(1)} %get-tuple-element.18.base), custom_call_target="tpu_custom_call" | custom-call | flops 1200000000 | bytes 2000000 | tf_op jit(solution)/shard_map/pallas_call | solution.py:289
  55.1 0.1 collective-permute-start.2
  55.2 0.0 copy-done.1
  55.2 0.9 %shard_map.65.sums = f32[2,192,192]{2,1,0:T(8,128)S(1)} custom-call(bf16[2,192,192]{2,1,0:T(8,128)(2,1)S(1)} %copy-done.1, bf16[2,2,192,1024]{3,2,1,0:T(8,128)(2,1)S(1)} %get-tuple-element.21.acts, f32[2,2,64,1024]{3,2,1,0:T(8,128)S(1)} %get-tuple-element.13.slopes, f32[64,1024]{1,0:T(8,128)S(1)} %get-tuple-element.19.mine), custom_call_target="tpu_custom_call" | custom-call | flops 400000000 | bytes 1000000 | tf_op jit(solution)/shard_map/pallas_call | solution.py:295
  56.2 0.6 collective-permute-done.2.theirs.other
  56.8 1.7 %shard_map.66 = bf16[16,8,576]{2,1,0:T(8,128)(2,1)} custom-call(bf16[2,192,192]{2,1,0:T(8,128)(2,1)S(1)} %copy-done.1, bf16[2,2,192,1024]{3,2,1,0:T(8,128)(2,1)S(1)} %get-tuple-element.21.acts, f32[2,2,64,1024]{3,2,1,0:T(8,128)S(1)} %get-tuple-element.13.slopes, f32[64,1024]{1,0:T(8,128)S(1)} %collective-permute-done.2.theirs.other, ...), custom_call_target="tpu_custom_call" | custom-call | flops 400000000 | bytes 1000000 | tf_op jit(solution)/shard_map/pallas_call | solution.py:296
  58.4 11.1 %all-to-all-start.1 = ((bf16[16,8,576]{2,1,0:T(8,128)(2,1)}), bf16[16,8,576]{2,1,0:T(8,128)(2,1)S(1)}, u32[]{:S(2)}, u32[]{:S(2)}) async-start(bf16[16,8,576]{2,1,0:T(8,128)(2,1)} %shard_map.66), calls=%async_computation.1 | async-start | bytes 327680 | tf_op jit(solution)/shard_map/all_to_all | solution.py:302
  69.5 2.1 %shard_map.64 = f32[1,2,64,1024]{3,2,1,0:T(8,128)} custom-call(bf16[2,192,192]{2,1,0:T(8,128)(2,1)S(1)} %copy-done.1, f32[2,2,64,1024]{3,2,1,0:T(8,128)S(1)} %get-tuple-element.13.slopes, f32[64,1024]{1,0:T(8,128)S(1)} %get-tuple-element.19.mine, f32[64,1024]{1,0:T(8,128)S(1)} %collective-permute-done.2.theirs.other), custom_call_target="tpu_custom_call" | custom-call | flops 600000000 | bytes 3000000 | tf_op jit(solution)/shard_map/pallas_call | solution.py:299
  71.6 8.2 %all-to-all-done.1.parts = bf16[16,8,576]{2,1,0:T(8,128)(2,1)S(1)} async-done(((bf16[16,8,576]{2,1,0:T(8,128)(2,1)}), bf16[16,8,576]{2,1,0:T(8,128)(2,1)S(1)}, u32[]{:S(2)}, u32[]{:S(2)}) %all-to-all-start.1) | async-done | bytes 147488 | tf_op jit(solution)/shard_map/all_to_all | solution.py:302
  79.9 0.7 shard_map.67
Async XLA Ops:
  4.3 1.9 %collective-permute-start = (bf16[64,2688]{1,0:T(8,128)(2,1)}, bf16[64,2688]{1,0:T(8,128)(2,1)S(1)}, u32[]{:S(2)}, u32[]{:S(2)}) collective-permute-start(bf16[64,2688]{1,0:T(8,128)(2,1)} %get-tuple-element.15), channel_id=1, source_target_pairs={{0,16},{16,0},{32,48},{48,32},{64,80},{80,64},{96,112},{112,96},{1... | collective-permute-start | bytes 1032200 | tf_op jit(solution)/shard_map/ppermute | solution.py:275
  6.2 0.9 %copy-start = (bf16[2,192,192]{2,1,0:T(8,128)(2,1)S(1)}, bf16[2,192,192]{2,1,0:T(8,128)(2,1)}, u32[]{:S(2)}) copy-start(bf16[2,192,192]{2,1,0:T(8,128)(2,1)} %get-tuple-element.12.ms) | copy-start | bytes 442372
  7.1 0.9 %copy-start.4 = (bf16[64,2048]{1,0:T(8,128)(2,1)S(1)}, bf16[64,2048]{1,0:T(8,128)(2,1)}, u32[]{:S(2)}) copy-start(bf16[64,2048]{1,0:T(8,128)(2,1)} %get-tuple-element.14.keep) | copy-start | bytes 786436
  41.3 4.3 %copy-start.2 = (bf16[2,2,64,1024]{3,2,1,0:T(8,128)(2,1)S(1)}, bf16[2,2,64,1024]{3,2,1,0:T(8,128)(2,1)}, u32[]{:S(2)}) copy-start(bf16[2,2,64,1024]{3,2,1,0:T(8,128)(2,1)} %states.3) | copy-start | bytes 1572868
  41.3 4.3 %copy-start.3 = (f32[2,64,1024]{2,1,0:T(8,128)S(1)}, f32[2,64,1024]{2,1,0:T(8,128)}, u32[]{:S(2)}) copy-start(f32[2,64,1024]{2,1,0:T(8,128)} %loss.3) | copy-start | bytes 1572868
  44.2 6.9 %collective-permute-start.1 = (bf16[64,1024]{1,0:T(8,128)(2,1)S(1)}, bf16[64,1024]{1,0:T(8,128)(2,1)S(1)}, u32[]{:S(2)}, u32[]{:S(2)}) collective-permute-start(bf16[64,1024]{1,0:T(8,128)(2,1)S(1)} %shard_map.62), channel_id=1, source_target_pairs={{128,0},{144,16},{160,32},{176,48},{192,64},{208,80},{224,96},{240... | collective-permute-start | bytes 393224 | tf_op jit(solution)/shard_map/ppermute | solution.py:288
  46.0 9.3 %copy-start.1 = (bf16[2,192,192]{2,1,0:T(8,128)(2,1)S(1)}, bf16[2,192,192]{2,1,0:T(8,128)(2,1)}, u32[]{:S(2)}) copy-start(bf16[2,192,192]{2,1,0:T(8,128)(2,1)} %get-tuple-element.12.ms) | copy-start | bytes 442372
  55.1 1.6 %collective-permute-start.2 = (f32[64,1024]{1,0:T(8,128)S(1)}, f32[64,1024]{1,0:T(8,128)S(1)}, u32[]{:S(2)}, u32[]{:S(2)}) collective-permute-start(f32[64,1024]{1,0:T(8,128)S(1)} %get-tuple-element.20), channel_id=1, source_target_pairs={{0,16},{16,0},{32,48},{48,32},{64,80},{80,64},{96,112},{112,96},{1... | collective-permute-start | bytes 786440 | tf_op jit(solution)/shard_map/ppermute | solution.py:293
  58.4 21.4 %all-to-all-start.1 = ((bf16[16,8,576]{2,1,0:T(8,128)(2,1)}), bf16[16,8,576]{2,1,0:T(8,128)(2,1)S(1)}, u32[]{:S(2)}, u32[]{:S(2)}) async-start(bf16[16,8,576]{2,1,0:T(8,128)(2,1)} %shard_map.66), calls=%async_computation.1 | async-start | bytes 327680 | tf_op jit(solution)/shard_map/all_to_all | solution.py:302

commit v6 on v5

--- a/solution.py
+++ b/solution.py
@@ -14,8 +14,8 @@
 F32 = jnp.float32
 BF16 = jnp.bfloat16
 WIDE = 640
-LEAD = 2 * N + 2 * WIDE
-WHOLE = 62 << 20
+LEAD = 2 * N + 18 * C
+WHOLE = 53 << 20
 
 
 def masked(values, keep):
@@ -67,15 +67,19 @@
 
 
 def flatten_taps(m):
-    pad = jnp.zeros((C, WIDE - 9 * C), BF16)
     wide = [m[a * C : (a + 1) * C, : 2 * C] for a in range(3)]
     thin = [m[a * C : (a + 1) * C, 2 * C :] for a in range(3)]
-    return jnp.concatenate(wide + thin + [pad], axis=1)
-
-
-def unflatten_taps(flat):
-    wide = [flat[:, 2 * C * a : 2 * C * (a + 1)] for a in range(3)]
-    thin = [flat[:, (6 + a) * C : (7 + a) * C] for a in range(3)]
+    return jnp.concatenate(wide + thin, axis=1)
+
+
+def pair_taps(even, odd):
+    thin = [flat[:, (6 + a) * C : (7 + a) * C] for a in range(3) for flat in (even, odd)]
+    return jnp.concatenate([even[:, : 6 * C], odd[:, : 6 * C]] + thin, axis=1)
+
+
+def one_of_pair(pair, which):
+    wide = [pair[:, (6 * which + 2 * a) * C : (6 * which + 2 * a + 2) * C] for a in range(3)]
+    thin = [pair[:, (12 + 2 * a + which) * C : (13 + 2 * a + which) * C] for a in range(3)]
     return jnp.concatenate([jnp.concatenate(wide, axis=0), jnp.concatenate(thin, axis=0)], axis=1)
 
 
@@ -110,7 +114,8 @@
     in_w.wait()
     m1, m0 = taps(w[1]), taps(w[0])
     ms[0], ms[1] = m0, m1
-    give[:, 2 * N :] = flatten_taps(m0)
+    give[:, 2 * N : 2 * N + 9 * C] = flatten_taps(m0)
+    give[:, 2 * N + 9 * C :] = jnp.zeros((C, WIDE - 9 * C), BF16)
     settle(ins)
     for i, out in ((1 - own, give), (own, keep)):
         out[:, :N], out[:, N : 2 * N] = part_of(u.at[:, i], g[i], lc[i], m0, m1)
@@ -118,19 +123,18 @@
 
 def merge_kernel(keep, got, ms, out, odd, pair, sems):
     even = core() == 0
-    mine, theirs = flatten_taps(ms[0]), got[:, 2 * N :]
+    mine, theirs = flatten_taps(ms[0]), got[:, 2 * N : 2 * N + 9 * C]
     d_even = jnp.where(even, keep[:, :N], got[:, :N])
-    taps_even = jnp.where(even, mine, theirs)
+    both = pair_taps(jnp.where(even, mine, theirs), jnp.where(even, theirs, mine))
     pair[:, :N] = d_even
     pair[:, N : 2 * N] = jnp.where(even, got[:, :N], keep[:, :N])
-    pair[:, 2 * N : 2 * N + WIDE] = taps_even
-    pair[:, 2 * N + WIDE : LEAD] = jnp.where(even, theirs, mine)
+    pair[:, 2 * N : LEAD] = both
     chips = out.shape[0]
     sent = moves([(pair.at[:, :LEAD], out.at[k, :, :LEAD]) for k in range(chips)], sems)
     p_even = jnp.where(even, keep[:, N:], got[:, N : 2 * N])
     p_odd = jnp.where(even, got[:, N : 2 * N], keep[:, N:])
     odd[...] = p_odd
-    y = conv(unflatten_taps(taps_even), cols3(p_odd))
+    y = conv(one_of_pair(both, 0), cols3(p_odd))
     merged = p_even.astype(F32) + p_odd.astype(F32) + d_even.astype(F32) * y
     pair[:, LEAD:] = merged.astype(BF16)
     settle(sent + moves([(pair.at[:, LEAD:], out.at[k, :, LEAD:]) for k in range(chips)], sems, chips))
@@ -146,7 +150,7 @@
 
 
 def apply(packed, k, which, e):
-    m = unflatten_taps(packed[k, :, 2 * N + which * WIDE : 2 * N + (which + 1) * WIDE])
+    m = one_of_pair(packed[k, :, 2 * N : LEAD], which)
     return e + packed[k, :, which * N : (which + 1) * N].astype(F32) * conv(m, cols3(e))
 
 
@@ -175,20 +179,29 @@
 def lower_kernel(start, source, odd, base, mine, other, high, low, packed, sems):
     chips = packed.shape[0]
     arrived = arrivals(source, packed, sems)
+    spot = lax.rem(lax.axis_index("section") // 2, chips)
 
     def step(r, e):
         k = chips - 1 - r
         arrived(k)
         x = apply(packed, k, 1, e)
 
-        @pl.when(k == lax.rem(lax.axis_index("section") // 2, chips))
+        @pl.when(k == spot)
         def _():
             high[...] = e
             low[...] = x
 
         return apply(packed, k, 0, x) + packed[k, :, LEAD:].astype(F32)
 
-    lax.fori_loop(0, chips, step, start[...].astype(F32))
+    e = lax.fori_loop(0, chips - 1, step, start[...].astype(F32))
+    arrived(0)
+    x = apply(packed, 0, 1, e)
+
+    @pl.when(spot == 0)
+    def _():
+        high[...] = e
+        low[...] = x
+
     at_high = high[...] + base[...]
     at_low = low[...] + odd[...].astype(F32) + base[...]
     even = core() == 0

time: 80.9 us -> 77.7 us (0.960)
  Pallas kernels: 17.4 us -> 16.1 us
  local copies, waits for them, and re-layouts: 1.89 us -> 0.92 us
    unnamed x10 -> x6, local copies, waits for them, and re-layouts: 1.89 us -> 0.92 us
  transfers between devices with their start and end apart: 4 -> 4, of which waited for: 4 -> 4; matrix products, arithmetic and copies ran while one was open for 0% -> 0% of each run, Pallas kernels for 4% -> 5%
where the time goes in v6:
time: 77.7 us; the launch traced here: 77.4 us
  blocking collectives  31.6 us (41%)
  Pallas kernels  16.1 us (21%)
  waiting for transfers between devices  15.6 us (20%)
  starting transfers between devices  12.5 us (16%)
  local copies, waits for them, and re-layouts  0.92 us (1%)
    all_to_all x1, blocking collectives, shards(): lax.all_to_all(pairs, 'section', 0, 0, axis_index_groups=groups, tiled=True)  31.6 us
    all_to_all x1, starting transfers between devices, shards(): grads = lax.all_to_all(grads, 'batch', 0, 0, tiled=True)  11 us
    all_to_all x1, waiting for transfers between devices, shards(): grads = lax.all_to_all(grads, 'batch', 0, 0, tiled=True)  8.23 us
    ppermute x1, waiting for transfers between devices, shards(): lax.ppermute(last, 'section', [(i, i - half) for i in range(half, section...  5.13 us
    pallas_call x1, Pallas kernels, shards(): call(lower_kernel, (image, image), 'vhvv', 'vv', [((C, N), F32), ((C, N),...  3.47 us
    pallas_call x1, Pallas kernels, shards(): call(source_kernel, (shape((C, 2 * N + WIDE), BF16), shape((C, 2 * N), BF...  2.95 us
    pallas_call x1, Pallas kernels, shards(): call(upper_kernel, image16, 'h', 'v', [((chips, C, LEAD + N), BF16)], chi...  2.86 us
    pallas_call x1, Pallas kernels, shards(): call(start_kernel, shape((1, 2, C, N), F32), 'vvvv', 'v', [], 0, 6 * 10 *...  2.14 us
  transfers between devices with their start and end apart: 4, of which 4 were waited for; matrix products, arithmetic and copies ran while one was open for 0% of the time, Pallas kernels for 5%

profile of v6, /device:TPU:32, one launch (start us, length us, event | category | flops | bytes accessed | tf_op | source)
XLA Modules:
  0.0 77.4 jit_solution(2240414704527494218)
XLA Ops:
  0.6 0.0 copy-start.2
  0.6 0.9 %copy-done.2 = bf16[2,64,576]{2,1,0:T(8,128)(2,1)S(1)} copy-done((bf16[2,64,576]{2,1,0:T(8,128)(2,1)S(1)}, bf16[2,64,576]{2,1,0:T(8,128)(2,1)}, u32[]{:S(2)}) %copy-start.2) | copy-done | bytes 147480
  1.5 2.9 %shard_map.59 = (bf16[64,2688]{1,0:T(8,128)(2,1)S(1)}, bf16[64,2048]{1,0:T(8,128)(2,1)S(1)}, bf16[2,192,192]{2,1,0:T(8,128)(2,1)S(1)}) custom-call(bf16[2,2,64,1024]{3,2,1,0:T(8,128)(2,1)} %states.3, bf16[2,64,576]{2,1,0:T(8,128)(2,1)S(1)} %copy-done.2, f32[1,2,64,1024]{3,2,1,0:T(8,128)} %guess.1, f32[2,64,1024]{2,1,0:T(8,128)} %loss.3), custom_call_target="tpu_custom_call" | custom-call | flops 600000000 | bytes 2000000 | tf_op jit(solution)/shard_map/pallas_call | solution.py:282
  4.5 0.1 collective-permute-start
  4.6 1.6 %collective-permute-done.got = bf16[64,2688]{1,0:T(8,128)(2,1)S(1)} collective-permute-done((bf16[64,2688]{1,0:T(8,128)(2,1)S(1)}, bf16[64,2688]{1,0:T(8,128)(2,1)S(1)}, u32[]{:S(2)}, u32[]{:S(2)}) %collective-permute-start) | collective-permute-done | bytes 344096 | tf_op jit(solution)/shard_map/ppermute | solution.py:288
  6.2 0.9 %shard_map.61 = (bf16[4,64,4224]{2,1,0:T(8,128)(2,1)S(1)}, bf16[64,1024]{1,0:T(8,128)(2,1)S(1)}) custom-call(bf16[64,2048]{1,0:T(8,128)(2,1)S(1)} %get-tuple-element.14.keep, bf16[64,2688]{1,0:T(8,128)(2,1)S(1)} %collective-permute-done.got, bf16[2,192,192]{2,1,0:T(8,128)(2,1)S(1)} %get-tuple-element.12.ms), custom_call_target="tpu_custom_call" | custom-call | flops 100000000 | bytes 3000000 | tf_op jit(solution)/shard_map/pallas_call | solution.py:289
  7.2 31.6 %all_to_all.10.source = bf16[4,64,4224]{2,1,0:T(8,128)(2,1)S(1)} all-to-all(bf16[4,64,4224]{2,1,0:T(8,128)(2,1)S(1)} %get-tuple-element.16), channel_id=1, replica_groups={{0,32,64,96},{16,48,80,112},{128,160,192,224},{144,176,208,240},{1,33,6..., dimensions={0} | all-to-all | bytes 4325376 | tf_op jit(solution)/shard_map/all_to_all | solution.py:294
  38.8 0.0 copy-start
  38.8 0.0 copy-start.1
  38.8 2.9 %shard_map.62 = bf16[64,1024]{1,0:T(8,128)(2,1)S(1)} custom-call(bf16[4,64,4224]{2,1,0:T(8,128)(2,1)S(1)} %all_to_all.10.source), custom_call_target="tpu_custom_call" | custom-call | flops 1000000000 | bytes 2000000 | tf_op jit(solution)/shard_map/pallas_call | solution.py:300
  41.6 1.3 %collective-permute-start.1 = (bf16[64,1024]{1,0:T(8,128)(2,1)S(1)}, bf16[64,1024]{1,0:T(8,128)(2,1)S(1)}, u32[]{:S(2)}, u32[]{:S(2)}) collective-permute-start(bf16[64,1024]{1,0:T(8,128)(2,1)S(1)} %shard_map.62), channel_id=1, source_target_pairs={{128,0},{144,16},{160,32},{176,48},{192,64},{208,80},{224,96},{240... | collective-permute-start | bytes 393224 | tf_op jit(solution)/shard_map/ppermute | solution.py:301
  42.9 0.0 copy-done
  43.0 0.0 copy-done.1
  43.0 0.4 shard_map.60
  43.4 5.1 %collective-permute-done.1.start = bf16[64,1024]{1,0:T(8,128)(2,1)S(1)} collective-permute-done((bf16[64,1024]{1,0:T(8,128)(2,1)S(1)}, bf16[64,1024]{1,0:T(8,128)(2,1)S(1)}, u32[]{:S(2)}, u32[]{:S(2)}) %collective-permute-start.1) | collective-permute-done | bytes 131104 | tf_op jit(solution)/shard_map/ppermute | solution.py:301
  48.5 3.5 %shard_map.63 = (f32[64,1024]{1,0:T(8,128)S(1)}, f32[64,1024]{1,0:T(8,128)S(1)}) custom-call(bf16[64,1024]{1,0:T(8,128)(2,1)S(1)} %collective-permute-done.1.start, bf16[4,64,4224]{2,1,0:T(8,128)(2,1)S(1)} %all_to_all.10.source, bf16[64,1024]{1,0:T(8,128)(2,1)S(1)} %get-tuple-element.17.odd, f32[64,1024]{1,0:T(8,128)S(1)} %get-tuple-element.18.base), custom_call_target="tpu_custom_call" | custom-call | flops 1200000000 | bytes 2000000 | tf_op jit(solution)/shard_map/pallas_call | solution.py:302
  52.0 0.1 collective-permute-start.2
  52.1 0.9 %shard_map.65.sums = f32[2,192,192]{2,1,0:T(8,128)S(1)} custom-call(bf16[2,192,192]{2,1,0:T(8,128)(2,1)S(1)} %get-tuple-element.12.ms, bf16[2,2,192,1024]{3,2,1,0:T(8,128)(2,1)S(1)} %get-tuple-element.21.acts, f32[2,2,64,1024]{3,2,1,0:T(8,128)S(1)} %get-tuple-element.13.slopes, f32[64,1024]{1,0:T(8,128)S(1)} %get-tuple-element.19.mine), custom_call_target="tpu_custom_call" | custom-call | flops 400000000 | bytes 1000000 | tf_op jit(solution)/shard_map/pallas_call | solution.py:308
  53.0 0.6 collective-permute-done.2.theirs.other
  53.6 1.7 %shard_map.66 = bf16[16,8,576]{2,1,0:T(8,128)(2,1)} custom-call(bf16[2,192,192]{2,1,0:T(8,128)(2,1)S(1)} %get-tuple-element.12.ms, bf16[2,2,192,1024]{3,2,1,0:T(8,128)(2,1)S(1)} %get-tuple-element.21.acts, f32[2,2,64,1024]{3,2,1,0:T(8,128)S(1)} %get-tuple-element.13.slopes, f32[64,1024]{1,0:T(8,128)S(1)} %collective-permute-done.2.theirs.other, ...), custom_call_target="tpu_custom_call" | custom-call | flops 400000000 | bytes 1000000 | tf_op jit(solution)/shard_map/pallas_call | solution.py:309
  55.3 11.0 %all-to-all-start.1 = ((bf16[16,8,576]{2,1,0:T(8,128)(2,1)}), bf16[16,8,576]{2,1,0:T(8,128)(2,1)S(1)}, u32[]{:S(2)}, u32[]{:S(2)}) async-start(bf16[16,8,576]{2,1,0:T(8,128)(2,1)} %shard_map.66), calls=%async_computation.1 | async-start | bytes 327680 | tf_op jit(solution)/shard_map/all_to_all | solution.py:315
  66.3 2.1 %shard_map.64 = f32[1,2,64,1024]{3,2,1,0:T(8,128)} custom-call(bf16[2,192,192]{2,1,0:T(8,128)(2,1)S(1)} %get-tuple-element.12.ms, f32[2,2,64,1024]{3,2,1,0:T(8,128)S(1)} %get-tuple-element.13.slopes, f32[64,1024]{1,0:T(8,128)S(1)} %get-tuple-element.19.mine, f32[64,1024]{1,0:T(8,128)S(1)} %collective-permute-done.2.theirs.other), custom_call_target="tpu_custom_call" | custom-call | flops 600000000 | bytes 3000000 | tf_op jit(solution)/shard_map/pallas_call | solution.py:312
  68.5 8.2 %all-to-all-done.1.parts = bf16[16,8,576]{2,1,0:T(8,128)(2,1)S(1)} async-done(((bf16[16,8,576]{2,1,0:T(8,128)(2,1)}), bf16[16,8,576]{2,1,0:T(8,128)(2,1)S(1)}, u32[]{:S(2)}, u32[]{:S(2)}) %all-to-all-start.1) | async-done | bytes 147488 | tf_op jit(solution)/shard_map/all_to_all | solution.py:315
  76.7 0.7 shard_map.67
Async XLA Ops:
  0.6 0.9 %copy-start.2 = (bf16[2,64,576]{2,1,0:T(8,128)(2,1)S(1)}, bf16[2,64,576]{2,1,0:T(8,128)(2,1)}, u32[]{:S(2)}) copy-start(bf16[2,64,576]{2,1,0:T(8,128)(2,1)} %weights.1) | copy-start | bytes 442372
  4.5 1.7 %collective-permute-start = (bf16[64,2688]{1,0:T(8,128)(2,1)S(1)}, bf16[64,2688]{1,0:T(8,128)(2,1)S(1)}, u32[]{:S(2)}, u32[]{:S(2)}) collective-permute-start(bf16[64,2688]{1,0:T(8,128)(2,1)S(1)} %get-tuple-element.15), channel_id=1, source_target_pairs={{0,16},{16,0},{32,48},{48,32},{64,80},{80,64},{96,112},{112,96},{1... | collective-permute-start | bytes 1032200 | tf_op jit(solution)/shard_map/ppermute | solution.py:288
  38.8 4.2 %copy-start = (bf16[2,2,64,1024]{3,2,1,0:T(8,128)(2,1)S(1)}, bf16[2,2,64,1024]{3,2,1,0:T(8,128)(2,1)}, u32[]{:S(2)}) copy-start(bf16[2,2,64,1024]{3,2,1,0:T(8,128)(2,1)} %states.3) | copy-start | bytes 1572868
  38.8 4.2 %copy-start.1 = (f32[2,64,1024]{2,1,0:T(8,128)S(1)}, f32[2,64,1024]{2,1,0:T(8,128)}, u32[]{:S(2)}) copy-start(f32[2,64,1024]{2,1,0:T(8,128)} %loss.3) | copy-start | bytes 1572868
  41.6 6.9 %collective-permute-start.1 = (bf16[64,1024]{1,0:T(8,128)(2,1)S(1)}, bf16[64,1024]{1,0:T(8,128)(2,1)S(1)}, u32[]{:S(2)}, u32[]{:S(2)}) collective-permute-start(bf16[64,1024]{1,0:T(8,128)(2,1)S(1)} %shard_map.62), channel_id=1, source_target_pairs={{128,0},{144,16},{160,32},{176,48},{192,64},{208,80},{224,96},{240... | collective-permute-start | bytes 393224 | tf_op jit(solution)/shard_map/ppermute | solution.py:301
  52.0 1.6 %collective-permute-start.2 = (f32[64,1024]{1,0:T(8,128)S(1)}, f32[64,1024]{1,0:T(8,128)S(1)}, u32[]{:S(2)}, u32[]{:S(2)}) collective-permute-start(f32[64,1024]{1,0:T(8,128)S(1)} %get-tuple-element.20), channel_id=1, source_target_pairs={{0,16},{16,0},{32,48},{48,32},{64,80},{80,64},{96,112},{112,96},{1... | collective-permute-start | bytes 786440 | tf_op jit(solution)/shard_map/ppermute | solution.py:306
  55.3 21.4 %all-to-all-start.1 = ((bf16[16,8,576]{2,1,0:T(8,128)(2,1)}), bf16[16,8,576]{2,1,0:T(8,128)(2,1)S(1)}, u32[]{:S(2)}, u32[]{:S(2)}) async-start(bf16[16,8,576]{2,1,0:T(8,128)(2,1)} %shard_map.66), calls=%async_computation.1 | async-start | bytes 327680 | tf_op jit(solution)/shard_map/all_to_all | solution.py:315

commit v7 on v6

--- a/solution.py
+++ b/solution.py
@@ -254,7 +254,7 @@
         )
 
 
-def call(kernel, outs, where_in, where_out, scratch, n_sems, flops, moved, grant=16 << 20):
+def call(kernel, outs, where_in, where_out, scratch, n_sems, flops, moved, grant=16 << 20, keep=False):
     spaces = {"s": pltpu.SMEM, "v": pltpu.VMEM, "h": pltpu.HBM}
     specs = lambda text: [pl.BlockSpec(memory_space=spaces[k]) for k in text]
     out_specs = specs(where_out)
@@ -266,7 +266,7 @@
         scratch_shapes=[pltpu.VMEM(*one) for one in scratch]
         + ([pltpu.SemaphoreType.DMA((n_sems,))] if n_sems else []),
         cost_estimate=pl.CostEstimate(flops=flops, bytes_accessed=moved, transcendentals=0),
-        compiler_params=pltpu.CompilerParams(vmem_limit_bytes=grant),
+        compiler_params=pltpu.CompilerParams(vmem_limit_bytes=grant, has_side_effects=keep),
     )
 
 
@@ -297,24 +297,29 @@
         "vv", "vvv", [], 0, 10**8, 4 * 10**6,
     )(states, loss)
 
-    last = call(upper_kernel, image16, "h", "v", [((chips, C, LEAD + N), BF16)], chips, 10**9, 2 * 10**6)(packed)
+    upper = call(upper_kernel, image16, "h", "v", [((chips, C, LEAD + N), BF16)], chips, 10**9, 2 * 10**6, keep=True)
+    lower = call(
+        lower_kernel, (image, image), "vhvv", "vv",
+        [((C, N), F32), ((C, N), F32), ((chips, C, LEAD + N), BF16)], chips, 12 * 10**8, 2 * 10**6, keep=True,
+    )
+    own = call(own_kernel, shape((2, 3 * C, 3 * C), F32), "vvvv", "v", [], 0, 4 * 10**8, 10**6, keep=True)
+    rest = call(other_kernel, shape((nb, 2 * (C // nb), 9 * C), BF16), "vvvvv", "v", [], 0, 4 * 10**8, 10**6, keep=True)
+    total = call(total_kernel, shape((2, 9 * C * C // nb), F32), "v", "v", [], 0, 10**6, 10**6)
+
+    near, far = lower(upper(pairs), pairs, odd, base)
+    rest(ms, acts, slopes, far, own(ms, acts, slopes, near))
+
+    last = upper(packed)
     carried = lax.ppermute(last, "section", [(i, i - half) for i in range(half, sections)])
-    mine, other = call(
-        lower_kernel, (image, image), "vhvv", "vv",
-        [((C, N), F32), ((C, N), F32), ((chips, C, LEAD + N), BF16)], chips, 12 * 10**8, 2 * 10**6
-    )(carried, packed, odd, base)
+    mine, other = lower(carried, packed, odd, base)
     theirs = lax.ppermute(other, "section", swap)
-
-    sums = call(own_kernel, shape((2, 3 * C, 3 * C), F32), "vvvv", "v", [], 0, 4 * 10**8, 10**6)(ms, acts, slopes, mine)
-    grads = call(
-        other_kernel, shape((nb, 2 * (C // nb), 9 * C), BF16), "vvvvv", "v", [], 0, 4 * 10**8, 10**6
-    )(ms, acts, slopes, theirs, sums)
+    sums = own(ms, acts, slopes, mine)
+    grads = rest(ms, acts, slopes, theirs, sums)
     starts = call(start_kernel, shape((1, 2, C, N), F32), "vvvv", "v", [], 0, 6 * 10**8, 3 * 10**6)(
         ms, slopes, mine, theirs
     )
     grads = lax.all_to_all(grads, "batch", 0, 0, tiled=True)
-    total = call(total_kernel, shape((2, 9 * C * C // nb), F32), "v", "v", [], 0, 10**6, 10**6)(grads)
-    return starts, total
+    return starts, total(grads)
 
 
 def solution(mesh):

time: 77.7 us -> 82.5 us (1.062); the launches traced: 77.4 us -> 81.4 us
  Pallas kernels: 16.1 us -> 25.2 us
  waiting for transfers between devices: 15.6 us -> 7.33 us
  local copies, waits for them, and re-layouts: 0.92 us -> 3.89 us
    pallas_call x5 -> x9, Pallas kernels: 9.67 us -> 18.8 us  [the longest x2 6.52 us: shards(): near, far = lower(upper(pairs), pairs, odd, base)]
    all_to_all x1, waiting for transfers between devices: 8.23 us -> 0.01 us  [shards(): grads = lax.all_to_all(grads, 'batch', 0, 0, tiled=True)]
    unnamed x6 -> x20, local copies, waits for them, and re-layouts: 0.92 us -> 3.89 us
  transfers between devices with their start and end apart: 4 -> 4, of which waited for: 4 -> 3; matrix products, arithmetic and copies ran while one was open for 0% -> 0% of each run, Pallas kernels for 5% -> 16%
where the time goes in v7:
time: 82.5 us; the launch traced here: 81.4 us
  blocking collectives  31.6 us (38%)
  Pallas kernels  25.2 us (31%)
  starting transfers between devices  12.5 us (15%)
  waiting for transfers between devices  7.33 us (9%)
  local copies, waits for them, and re-layouts  3.89 us (5%)
    all_to_all x1, blocking collectives, shards(): lax.all_to_all(pairs, 'section', 0, 0, axis_index_groups=groups, tiled=True)  31.6 us
    all_to_all x1, starting transfers between devices, shards(): grads = lax.all_to_all(grads, 'batch', 0, 0, tiled=True)  11 us
    pallas_call x2, Pallas kernels, shards(): near, far = lower(upper(pairs), pairs, odd, base)  6.52 us
    ppermute x1, waiting for transfers between devices, shards(): lax.ppermute(last, 'section', [(i, i - half) for i in range(half, section...  5.12 us
    unnamed x20, local copies, waits for them, and re-layouts  3.89 us
    pallas_call x1, Pallas kernels, shards(): mine, other = lower(carried, packed, odd, base)  3.48 us
    pallas_call x1, Pallas kernels, shards(): call(source_kernel, (shape((C, 2 * N + WIDE), BF16), shape((C, 2 * N), BF...  2.94 us
    pallas_call x1, Pallas kernels, shards(): last = upper(packed)  2.86 us
  transfers between devices with their start and end apart: 4, of which 3 were waited for; matrix products, arithmetic and copies ran while one was open for 0% of the time, Pallas kernels for 16%

profile of v7, /device:TPU:32, one launch (start us, length us, event | category | flops | bytes accessed | tf_op | source)
XLA Modules:
  0.0 81.4 jit_solution(13006302776272543952)
XLA Ops:
  0.6 0.0 copy-start.7
  0.6 0.9 %copy-done.7 = bf16[2,64,576]{2,1,0:T(8,128)(2,1)S(1)} copy-done((bf16[2,64,576]{2,1,0:T(8,128)(2,1)S(1)}, bf16[2,64,576]{2,1,0:T(8,128)(2,1)}, u32[]{:S(2)}) %copy-start.7) | copy-done | bytes 147480
  1.5 2.9 %shard_map.59 = (bf16[64,2688]{1,0:T(8,128)(2,1)S(1)}, bf16[64,2048]{1,0:T(8,128)(2,1)S(1)}, bf16[2,192,192]{2,1,0:T(8,128)(2,1)S(1)}) custom-call(bf16[2,2,64,1024]{3,2,1,0:T(8,128)(2,1)} %states.3, bf16[2,64,576]{2,1,0:T(8,128)(2,1)S(1)} %copy-done.7, f32[1,2,64,1024]{3,2,1,0:T(8,128)} %guess.1, f32[2,64,1024]{2,1,0:T(8,128)} %loss.3), custom_call_target="tpu_custom_call" | custom-call | flops 600000000 | bytes 2000000 | tf_op jit(solution)/shard_map/pallas_call | solution.py:282
  4.5 0.1 collective-permute-start
  4.6 1.6 %collective-permute-done.got = bf16[64,2688]{1,0:T(8,128)(2,1)S(1)} collective-permute-done((bf16[64,2688]{1,0:T(8,128)(2,1)S(1)}, bf16[64,2688]{1,0:T(8,128)(2,1)S(1)}, u32[]{:S(2)}, u32[]{:S(2)}) %collective-permute-start) | collective-permute-done | bytes 344096 | tf_op jit(solution)/shard_map/ppermute | solution.py:288
  6.2 0.9 %shard_map.61 = (bf16[4,64,4224]{2,1,0:T(8,128)(2,1)S(1)}, bf16[64,1024]{1,0:T(8,128)(2,1)S(1)}) custom-call(bf16[64,2048]{1,0:T(8,128)(2,1)S(1)} %get-tuple-element.17.keep, bf16[64,2688]{1,0:T(8,128)(2,1)S(1)} %collective-permute-done.got, bf16[2,192,192]{2,1,0:T(8,128)(2,1)S(1)} %get-tuple-element.14.ms), custom_call_target="tpu_custom_call" | custom-call | flops 100000000 | bytes 3000000 | tf_op jit(solution)/shard_map/pallas_call | solution.py:289
  7.2 0.0 copy-start.8
  7.2 31.6 %all_to_all.10.source = bf16[4,64,4224]{2,1,0:T(8,128)(2,1)S(1)} all-to-all(bf16[4,64,4224]{2,1,0:T(8,128)(2,1)S(1)} %get-tuple-element.19.source), channel_id=1, replica_groups={{0,32,64,96},{16,48,80,112},{128,160,192,224},{144,176,208,240},{1,33,6..., dimensions={0} | all-to-all | bytes 4325376 | tf_op jit(solution)/shard_map/all_to_all | solution.py:294
  38.8 1.3 %copy-done = bf16[4,64,4224]{2,1,0:T(8,128)(2,1)} copy-done((bf16[4,64,4224]{2,1,0:T(8,128)(2,1)}, bf16[4,64,4224]{2,1,0:T(8,128)(2,1)S(1)}, u32[]{:S(2)}) %copy-start) | copy-done | bytes 2162712
  40.1 2.9 %shard_map.66 = bf16[64,1024]{1,0:T(8,128)(2,1)S(1)} custom-call(bf16[4,64,4224]{2,1,0:T(8,128)(2,1)S(1)} %all_to_all.10.source), custom_call_target="tpu_custom_call" | custom-call | flops 1000000000 | bytes 2000000 | tf_op jit(solution)/shard_map/pallas_call | solution.py:312
  43.0 1.3 %collective-permute-start.1 = (bf16[64,1024]{1,0:T(8,128)(2,1)S(1)}, bf16[64,1024]{1,0:T(8,128)(2,1)S(1)}, u32[]{:S(2)}, u32[]{:S(2)}) collective-permute-start(bf16[64,1024]{1,0:T(8,128)(2,1)S(1)} %shard_map.66), channel_id=1, source_target_pairs={{128,0},{144,16},{160,32},{176,48},{192,64},{208,80},{224,96},{240... | collective-permute-start | bytes 393224 | tf_op jit(solution)/shard_map/ppermute | solution.py:313
  44.3 0.0 copy-done.3
  44.3 0.0 copy-done.4
  44.3 0.4 shard_map.60
  44.7 0.0 copy-start.5
  44.7 5.1 %collective-permute-done.1.start = bf16[64,1024]{1,0:T(8,128)(2,1)S(1)} collective-permute-done((bf16[64,1024]{1,0:T(8,128)(2,1)S(1)}, bf16[64,1024]{1,0:T(8,128)(2,1)S(1)}, u32[]{:S(2)}, u32[]{:S(2)}) %collective-permute-start.1) | collective-permute-done | bytes 131104 | tf_op jit(solution)/shard_map/ppermute | solution.py:313
  49.9 0.0 copy-done.8
  49.9 3.5 %shard_map.67 = (f32[64,1024]{1,0:T(8,128)S(1)}, f32[64,1024]{1,0:T(8,128)S(1)}) custom-call(bf16[64,1024]{1,0:T(8,128)(2,1)S(1)} %collective-permute-done.1.start, bf16[4,64,4224]{2,1,0:T(8,128)(2,1)S(1)} %all_to_all.10.source, bf16[64,1024]{1,0:T(8,128)(2,1)S(1)} %get-tuple-element.20.odd, f32[64,1024]{1,0:T(8,128)S(1)} %get-tuple-element.21.base), custom_call_target="tpu_custom_call" | custom-call | flops 1200000000 | bytes 2000000 | tf_op jit(solution)/shard_map/pallas_call | solution.py:314
  53.4 0.0 copy-done.5
  53.4 0.1 collective-permute-start.2
  53.5 0.9 %shard_map.69.sums = f32[2,192,192]{2,1,0:T(8,128)S(1)} custom-call(bf16[2,192,192]{2,1,0:T(8,128)(2,1)S(1)} %get-tuple-element.14.ms, bf16[2,2,192,1024]{3,2,1,0:T(8,128)(2,1)S(1)} %get-tuple-element.15.acts, f32[2,2,64,1024]{3,2,1,0:T(8,128)S(1)} %get-tuple-element.16.slopes, f32[64,1024]{1,0:T(8,128)S(1)} %get-tuple-element.24.mine), custom_call_target="tpu_custom_call" | custom-call | flops 400000000 | bytes 1000000 | tf_op jit(solution)/shard_map/pallas_call | solution.py:316
  54.4 0.6 collective-permute-done.2.theirs.other
  55.0 1.7 %shard_map.70 = bf16[16,8,576]{2,1,0:T(8,128)(2,1)} custom-call(bf16[2,192,192]{2,1,0:T(8,128)(2,1)S(1)} %get-tuple-element.14.ms, bf16[2,2,192,1024]{3,2,1,0:T(8,128)(2,1)S(1)} %get-tuple-element.15.acts, f32[2,2,64,1024]{3,2,1,0:T(8,128)S(1)} %get-tuple-element.16.slopes, f32[64,1024]{1,0:T(8,128)S(1)} %collective-permute-done.2.theirs.other, ...), custom_call_target="tpu_custom_call" | custom-call | flops 400000000 | bytes 1000000 | tf_op jit(solution)/shard_map/pallas_call | solution.py:317
  56.7 11.0 %all-to-all-start.1 = ((bf16[16,8,576]{2,1,0:T(8,128)(2,1)}), bf16[16,8,576]{2,1,0:T(8,128)(2,1)S(1)}, u32[]{:S(2)}, u32[]{:S(2)}) async-start(bf16[16,8,576]{2,1,0:T(8,128)(2,1)} %shard_map.70), calls=%async_computation.1 | async-start | bytes 327680 | tf_op jit(solution)/shard_map/all_to_all | solution.py:321
  67.7 1.6 %copy-done.1 = bf16[4,64,4224]{2,1,0:T(8,128)(2,1)S(1)} copy-done((bf16[4,64,4224]{2,1,0:T(8,128)(2,1)S(1)}, bf16[4,64,4224]{2,1,0:T(8,128)(2,1)}, u32[]{:S(2)}) %copy-start.1) | copy-done | bytes 2162712
  69.3 2.9 %shard_map.62.start = bf16[64,1024]{1,0:T(8,128)(2,1)S(1)} custom-call(bf16[4,64,4224]{2,1,0:T(8,128)(2,1)S(1)} %copy-done.1), custom_call_target="tpu_custom_call" | custom-call | flops 1000000000 | bytes 2000000 | tf_op jit(solution)/shard_map/pallas_call | solution.py:309
  72.2 3.7 %shard_map.63 = (f32[64,1024]{1,0:T(8,128)S(1)}, f32[64,1024]{1,0:T(8,128)S(1)}) custom-call(bf16[64,1024]{1,0:T(8,128)(2,1)S(1)} %shard_map.62.start, bf16[4,64,4224]{2,1,0:T(8,128)(2,1)S(1)} %copy-done.2, bf16[64,1024]{1,0:T(8,128)(2,1)S(1)} %copy-done.9, f32[64,1024]{1,0:T(8,128)S(1)} %copy-done.6), custom_call_target="tpu_custom_call" | custom-call | flops 1200000000 | bytes 2000000 | tf_op jit(solution)/shard_map/pallas_call | solution.py:309
  75.9 0.9 %shard_map.64.sums = f32[2,192,192]{2,1,0:T(8,128)S(1)} custom-call(bf16[2,192,192]{2,1,0:T(8,128)(2,1)S(1)} %get-tuple-element.14.ms, bf16[2,2,192,1024]{3,2,1,0:T(8,128)(2,1)S(1)} %get-tuple-element.15.acts, f32[2,2,64,1024]{3,2,1,0:T(8,128)S(1)} %get-tuple-element.16.slopes, f32[64,1024]{1,0:T(8,128)S(1)} %get-tuple-element.23.mine), custom_call_target="tpu_custom_call" | custom-call | flops 400000000 | bytes 1000000 | tf_op jit(solution)/shard_map/pallas_call | solution.py:310
  76.8 1.7 %shard_map.65 = bf16[16,8,576]{2,1,0:T(8,128)(2,1)} custom-call(bf16[2,192,192]{2,1,0:T(8,128)(2,1)S(1)} %get-tuple-element.14.ms, bf16[2,2,192,1024]{3,2,1,0:T(8,128)(2,1)S(1)} %get-tuple-element.15.acts, f32[2,2,64,1024]{3,2,1,0:T(8,128)S(1)} %get-tuple-element.16.slopes, f32[64,1024]{1,0:T(8,128)S(1)} %get-tuple-element.22.other, ...), custom_call_target="tpu_custom_call" | custom-call | flops 400000000 | bytes 1000000 | tf_op jit(solution)/shard_map/pallas_call | solution.py:310
  78.5 2.1 %shard_map.68 = f32[1,2,64,1024]{3,2,1,0:T(8,128)} custom-call(bf16[2,192,192]{2,1,0:T(8,128)(2,1)S(1)} %get-tuple-element.14.ms, f32[2,2,64,1024]{3,2,1,0:T(8,128)S(1)} %get-tuple-element.16.slopes, f32[64,1024]{1,0:T(8,128)S(1)} %get-tuple-element.24.mine, f32[64,1024]{1,0:T(8,128)S(1)} %collective-permute-done.2.theirs.other), custom_call_target="tpu_custom_call" | custom-call | flops 600000000 | bytes 3000000 | tf_op jit(solution)/shard_map/pallas_call | solution.py:318
  80.7 0.0 all-to-all-done.1.parts
  80.7 0.7 shard_map.71
  (10 shorter events, 0.0 us)
Async XLA Ops:
  0.6 0.9 %copy-start.7 = (bf16[2,64,576]{2,1,0:T(8,128)(2,1)S(1)}, bf16[2,64,576]{2,1,0:T(8,128)(2,1)}, u32[]{:S(2)}) copy-start(bf16[2,64,576]{2,1,0:T(8,128)(2,1)} %weights.1) | copy-start | bytes 442372
  4.5 1.7 %collective-permute-start = (bf16[64,2688]{1,0:T(8,128)(2,1)S(1)}, bf16[64,2688]{1,0:T(8,128)(2,1)S(1)}, u32[]{:S(2)}, u32[]{:S(2)}) collective-permute-start(bf16[64,2688]{1,0:T(8,128)(2,1)S(1)} %get-tuple-element.18), channel_id=1, source_target_pairs={{0,16},{16,0},{32,48},{48,32},{64,80},{80,64},{96,112},{112,96},{1... | collective-permute-start | bytes 1032200 | tf_op jit(solution)/shard_map/ppermute | solution.py:288
  7.2 42.7 %copy-start.8 = (bf16[64,1024]{1,0:T(8,128)(2,1)}, bf16[64,1024]{1,0:T(8,128)(2,1)S(1)}, u32[]{:S(2)}) copy-start(bf16[64,1024]{1,0:T(8,128)(2,1)S(1)} %get-tuple-element.20.odd) | copy-start | bytes 393220
  38.8 1.3 %copy-start = (bf16[4,64,4224]{2,1,0:T(8,128)(2,1)}, bf16[4,64,4224]{2,1,0:T(8,128)(2,1)S(1)}, u32[]{:S(2)}) copy-start(bf16[4,64,4224]{2,1,0:T(8,128)(2,1)S(1)} %get-tuple-element.19.source) | copy-start | bytes 6488068
  40.1 4.2 %copy-start.3 = (bf16[2,2,64,1024]{3,2,1,0:T(8,128)(2,1)S(1)}, bf16[2,2,64,1024]{3,2,1,0:T(8,128)(2,1)}, u32[]{:S(2)}) copy-start(bf16[2,2,64,1024]{3,2,1,0:T(8,128)(2,1)} %states.3) | copy-start | bytes 1572868
  40.1 4.2 %copy-start.4 = (f32[2,64,1024]{2,1,0:T(8,128)S(1)}, f32[2,64,1024]{2,1,0:T(8,128)}, u32[]{:S(2)}) copy-start(f32[2,64,1024]{2,1,0:T(8,128)} %loss.3) | copy-start | bytes 1572868
  43.0 6.9 %collective-permute-start.1 = (bf16[64,1024]{1,0:T(8,128)(2,1)S(1)}, bf16[64,1024]{1,0:T(8,128)(2,1)S(1)}, u32[]{:S(2)}, u32[]{:S(2)}) collective-permute-start(bf16[64,1024]{1,0:T(8,128)(2,1)S(1)} %shard_map.66), channel_id=1, source_target_pairs={{128,0},{144,16},{160,32},{176,48},{192,64},{208,80},{224,96},{240... | collective-permute-start | bytes 393224 | tf_op jit(solution)/shard_map/ppermute | solution.py:313
  44.7 8.6 %copy-start.5 = (f32[64,1024]{1,0:T(8,128)}, f32[64,1024]{1,0:T(8,128)S(1)}, u32[]{:S(2)}) copy-start(f32[64,1024]{1,0:T(8,128)S(1)} %get-tuple-element.21.base) | copy-start | bytes 786436
  53.4 1.6 %collective-permute-start.2 = (f32[64,1024]{1,0:T(8,128)S(1)}, f32[64,1024]{1,0:T(8,128)S(1)}, u32[]{:S(2)}, u32[]{:S(2)}) collective-permute-start(f32[64,1024]{1,0:T(8,128)S(1)} %get-tuple-element.25), channel_id=1, source_target_pairs={{0,16},{16,0},{32,48},{48,32},{64,80},{80,64},{96,112},{112,96},{1... | collective-permute-start | bytes 786440 | tf_op jit(solution)/shard_map/ppermute | solution.py:315
  56.7 24.0 %all-to-all-start.1 = ((bf16[16,8,576]{2,1,0:T(8,128)(2,1)}), bf16[16,8,576]{2,1,0:T(8,128)(2,1)S(1)}, u32[]{:S(2)}, u32[]{:S(2)}) async-start(bf16[16,8,576]{2,1,0:T(8,128)(2,1)} %shard_map.70), calls=%async_computation.1 | async-start | bytes 327680 | tf_op jit(solution)/shard_map/all_to_all | solution.py:321
  67.7 1.6 %copy-start.1 = (bf16[4,64,4224]{2,1,0:T(8,128)(2,1)S(1)}, bf16[4,64,4224]{2,1,0:T(8,128)(2,1)}, u32[]{:S(2)}) copy-start(bf16[4,64,4224]{2,1,0:T(8,128)(2,1)} %copy-done) | copy-start | bytes 6488068
  69.3 2.9 %copy-start.2 = (bf16[4,64,4224]{2,1,0:T(8,128)(2,1)S(1)}, bf16[4,64,4224]{2,1,0:T(8,128)(2,1)}, u32[]{:S(2)}) copy-start(bf16[4,64,4224]{2,1,0:T(8,128)(2,1)} %copy-done) | copy-start | bytes 6488068
  69.3 2.9 %copy-start.6 = (f32[64,1024]{1,0:T(8,128)S(1)}, f32[64,1024]{1,0:T(8,128)}, u32[]{:S(2)}) copy-start(f32[64,1024]{1,0:T(8,128)} %copy-done.5) | copy-start | bytes 786436
  69.3 2.9 %copy-start.9 = (bf16[64,1024]{1,0:T(8,128)(2,1)S(1)}, bf16[64,1024]{1,0:T(8,128)(2,1)}, u32[]{:S(2)}) copy-start(bf16[64,1024]{1,0:T(8,128)(2,1)} %copy-done.8) | copy-start | bytes 393220
